TPU v7x, 32 devices: a whole 2x2x4 slice. The times are simulated.
32 devices in a mesh: morton: 8 (over y, x, core), sub: 4 (over z).
Axes of the slice: x: 2, y: 2, z: 4, core: 2. Of those that a mesh axis runs over, the one named last changes fastest.
Arguments:
- leaf_dens: bfloat16 [512, 8, 294], P(('morton', 'sub')), may hold values from -6 to 6
- leaf_sources: int32 [512, 189], P(('morton', 'sub')), may hold values from 0 to 191, as said below
- leaf_classes: int32 [512, 189], P(('morton', 'sub')), may hold values from 0 to 15
- grand_sources: int32 [8, 189], P('morton'), may hold values from 0 to 7
- grand_classes: int32 [8, 189], P('morton'), may hold values from 0 to 15
- up_ops: bfloat16 [8, 294, 294], replicated, may hold values from -0.125 to 0.125
- far_ops: bfloat16 [16, 294, 294], replicated, may hold values from -0.02734375 to 0.02734375
- down_ops: bfloat16 [8, 294, 294], replicated, may hold values from -0.375 to 0.375
Outputs:
- leaf_local: bfloat16 [512, 8, 294], P(('morton', 'sub'))
Inputs may be any that keep to these rules, and one draw needn't show every extreme that they name: `leaf_sources`: positions in the pool of the finest octants of three Morton ranges of 64 octants each (range t // 64 - 1, its own, and the next); rows of the first range never name the range before it and rows of the last never name the range after it.
All inputs are finite; a program needn't handle non-finite values.
Results may differ from a plain program's by a relative error of at most 0.0085.
Values may be sent and summed in bfloat16 or wider, within the bound.
No kernel may reach another device: no remote copies, remote signals or barrier semaphores. Data moves between devices by JAX's collectives and lax.ppermute only.
A program may use at most 64 MiB of HBM per device.

v0:
```python
import jax
import jax.numpy as jnp
from jax import lax
from jax.sharding import PartitionSpec as P


def from_partner(value, axis, distance):
    mask = 2**distance
    pairs = [(source, source ^ mask) for source in range(lax.axis_size(axis))]
    return lax.ppermute(value, axis, pairs)


def padded(cells, sides, width):
    for axis, dim in sides:
        count = lax.axis_size(axis)
        ends = count - 1
        head = lax.slice_in_dim(cells, 0, width, axis=dim)
        tail = lax.slice_in_dim(cells, cells.shape[dim] - width, cells.shape[dim], axis=dim)
        cells = jnp.concatenate(
            [
                lax.ppermute(tail, axis, [(i, (i + 1) % count) for i in range(ends)]),
                cells,
                lax.ppermute(head, axis, [((i + 1) % count, i) for i in range(ends)]),
            ],
            axis=dim,
        )
    return cells


def far_block(pool_rows, sources, classes, far_matrix, rhs_count, width):
    targets = sources.shape[0]
    classes_count = far_matrix.shape[0] // width
    pool_size = pool_rows.shape[0]
    source_hot = (
        sources[:, :, None] == jnp.arange(pool_size, dtype=jnp.int32)[None, None, :]
    ).astype(jnp.bfloat16)
    class_hot = (
        classes[:, :, None] == jnp.arange(classes_count, dtype=jnp.int32)[None, None, :]
    ).astype(jnp.bfloat16)
    counts = jnp.einsum(
        "tec,teq->tcq", class_hot, source_hot, preferred_element_type=jnp.float32
    ).astype(jnp.bfloat16)
    aggregate = jnp.dot(
        counts.reshape(targets * classes_count, pool_size),
        pool_rows,
        preferred_element_type=jnp.float32,
    ).astype(jnp.bfloat16)
    rows_in = aggregate.reshape(targets, classes_count, rhs_count, width).transpose(0, 2, 1, 3)
    rows_in = rows_in.reshape(targets * rhs_count, classes_count * width)
    return jnp.dot(rows_in, far_matrix, preferred_element_type=jnp.float32).reshape(
        targets, rhs_count, width
    )


def shards(
    leaf_dens, leaf_sources, leaf_classes, grand_sources, grand_classes, up_ops, far_ops, down_ops
):
    own_leaves, rhs_count, width = leaf_dens.shape
    classes_count = far_ops.shape[0]
    parents_here = own_leaves // 8
    grand_span = 64 // own_leaves
    sub_index = lax.axis_index("sub")
    position = sub_index % grand_span
    children = leaf_dens.reshape(parents_here, 8, rhs_count, width)
    parent_dens = jnp.einsum(
        "jknw,kwv->jnv", children, up_ops, preferred_element_type=jnp.float32
    ).astype(jnp.bfloat16)
    mine = parent_dens
    for bit_number in range(grand_span.bit_length() - 1):
        partner = from_partner(mine, "sub", bit_number)
        lower_half = sub_index // (1 << bit_number) % 2 == 0
        mine = jnp.where(
            lower_half,
            jnp.concatenate([mine, partner], axis=0),
            jnp.concatenate([partner, mine], axis=0),
        )
    grand_dens = jnp.einsum("knw,kwv->nv", mine, up_ops, preferred_element_type=jnp.float32).astype(
        jnp.bfloat16
    )
    flat_dens = grand_dens.reshape(rhs_count * width)
    piece_len = rhs_count * width // grand_span
    piece = lax.dynamic_slice_in_dim(flat_dens, position * piece_len, piece_len, 0)
    range_pieces = lax.all_gather(piece[None], "sub", axis=0, tiled=True)
    range_dens = range_pieces.reshape(range_pieces.shape[0] // grand_span, rhs_count * width)
    grand_pool = lax.all_gather(range_dens, "morton", axis=0, tiled=True)
    far_matrix = far_ops.reshape(classes_count * width, width)
    row_pick = sub_index // grand_span
    my_sources = lax.dynamic_slice_in_dim(grand_sources, row_pick, 1, 0)[0]
    my_classes = lax.dynamic_slice_in_dim(grand_classes, row_pick, 1, 0)[0]
    grand_count = grand_pool.shape[0]
    source_hot = (my_sources[:, None] == jnp.arange(grand_count, dtype=jnp.int32)[None, :]).astype(
        jnp.bfloat16
    )
    class_hot = (my_classes[:, None] == jnp.arange(classes_count, dtype=jnp.int32)[None, :]).astype(
        jnp.bfloat16
    )
    grand_counts = jnp.dot(class_hot.T, source_hot, preferred_element_type=jnp.float32).astype(
        jnp.bfloat16
    )
    grand_agg = jnp.dot(grand_counts, grand_pool, preferred_element_type=jnp.float32).astype(
        jnp.bfloat16
    )
    grand_rows = grand_agg.reshape(classes_count, rhs_count, width).transpose(1, 0, 2)
    grand_rows = grand_rows.reshape(rhs_count, classes_count * width)
    grand_local = jnp.dot(grand_rows, far_matrix, preferred_element_type=jnp.float32).astype(
        jnp.bfloat16
    )
    parent_ops = lax.dynamic_slice_in_dim(down_ops, position * parents_here, parents_here, 0)
    parent_local = jnp.einsum(
        "nw,jwv->jnv", grand_local, parent_ops, preferred_element_type=jnp.float32
    ).astype(jnp.bfloat16)
    range_leaves = lax.all_gather(leaf_dens, "sub", axis=0, tiled=True)
    leaf_pool = padded(range_leaves, (("morton", 0),), range_leaves.shape[0])
    pool_rows = leaf_pool.reshape(leaf_pool.shape[0], rhs_count * width)
    leaf_far = far_block(pool_rows, leaf_sources, leaf_classes, far_matrix, rhs_count, width)
    downward = jnp.einsum(
        "jnw,kwv->jknv", parent_local, down_ops, preferred_element_type=jnp.float32
    )
    downward = downward.reshape(own_leaves, rhs_count, width)
    return (leaf_far + downward).astype(jnp.bfloat16)


def solution(mesh):
    placed = (
        P(("morton", "sub"), None, None),
        P(("morton", "sub"), None),
        P(("morton", "sub"), None),
        P("morton", None),
        P("morton", None),
        P(),
        P(),
        P(),
    )
    return jax.shard_map(
        shards,
        mesh=mesh,
        in_specs=placed,
        out_specs=P(("morton", "sub"), None, None),
        check_vma=False,
    )
```

profile of v0, /device:TPU:0, one launch (start us, length us, event | category | flops | bytes accessed | tf_op | source)
XLA Modules:
  0.0 82.7 jit_solution(12412377823219016353)
XLA Ops:
  0.0 0.0 copy-start.6
  0.0 0.0 copy-start.5
  0.0 0.0 copy-start
  0.0 0.0 copy-start.2
  0.0 0.0 copy-start.1
  0.0 2.0 %fusion.34 = bf16[2,8,294]{2,1,0:T(8,128)(2,1)S(1)} fusion(bf16[2,8,8,294]{3,2,1,0:T(8,128)(2,1)} %bitcast.77, bf16[8,294,294]{2,0,1:T(8,128)(2,1)} %param.13), kind=kOutput, calls=%fused_computation.25 | convolution fusion | flops 22132320 | bytes 1467648 | tf_op jit(solution)/shard_map/jknw,kwv->jnv/dot_general | solution.py:65
  2.0 3.2 %collective-permute-start.2 = (bf16[2,8,294]{2,1,0:T(8,128)(2,1)S(1)}, bf16[2,8,294]{2,1,0:T(8,128)(2,1)S(1)}, u32[]{:S(2)}, u32[]{:S(2)}) collective-permute-start(bf16[2,8,294]{2,1,0:T(8,128)(2,1)S(1)} %fusion.34), channel_id=1, source_target_pairs={{0,1},{1,0},{2,3},{3,2},{4,5},{5,4},{6,7},{7,6},{8,9},{9,8},{10,11... | collective-permute-start | bytes 28232 | tf_op jit(solution)/shard_map/ppermute | solution.py:10
  5.2 0.0 copy-done
  5.2 14.6 %all_gather.9 = bf16[64,8,294]{2,1,0:T(8,128)(2,1)S(1)} all-gather(bf16[16,8,294]{2,1,0:T(8,128)(2,1)S(1)} %copy-done), channel_id=1, replica_groups=mesh['morton'=8,'sub'=4] {'sub'}, dimensions={0}, use_global_device_ids=true | all-gather | bytes 376320 | tf_op jit(solution)/shard_map/all_gather | solution.py:112
  19.8 1.3 %collective-permute-start = (bf16[64,8,294]{2,1,0:T(8,128)(2,1)S(1)}, bf16[64,8,294]{2,1,0:T(8,128)(2,1)S(1)}, u32[]{:S(2)}, u32[]{:S(2)}) collective-permute-start(bf16[64,8,294]{2,1,0:T(8,128)(2,1)S(1)} %all_gather.9), channel_id=1, source_target_pairs={{0,4},{4,8},{8,12},{12,16},{16,20},{20,24},{24,28},{1,5},{5,9},{9,... | collective-permute-start | bytes 903176 | tf_op jit(solution)/shard_map/ppermute | solution.py:21
  21.1 1.3 %collective-permute-start.1 = (bf16[64,8,294]{2,1,0:T(8,128)(2,1)S(1)}, bf16[64,8,294]{2,1,0:T(8,128)(2,1)S(1)}, u32[]{:S(2)}, u32[]{:S(2)}) collective-permute-start(bf16[64,8,294]{2,1,0:T(8,128)(2,1)S(1)} %all_gather.9), channel_id=1, source_target_pairs={{4,0},{8,4},{12,8},{16,12},{20,16},{24,20},{28,24},{5,1},{9,5},{13... | collective-permute-start | bytes 903176 | tf_op jit(solution)/shard_map/ppermute | solution.py:23
  22.5 0.0 collective-permute-done.2
  22.5 0.8 collective-permute-start.3
  23.2 0.0 copy-done.2
  23.3 0.0 copy-done.1
  23.3 1.5 %fusion.20 = bf16[16,16,192]{2,1,0:T(8,128)(2,1)} fusion(s32[16,189]{1,0:T(8,128)S(1)} %copy-done.1, s32[16,189]{1,0:T(8,128)S(1)} %copy-done.2), kind=kOutput, calls=%fused_computation.20 | convolution fusion | flops 19257600 | bytes 122496 | tf_op jit(solution)/shard_map/tec,teq->tcq/dot_general | solution.py:40
  24.7 0.0 copy-done.6
  24.7 0.6 dynamic-slice
  25.3 0.0 copy-done.5
  25.3 0.6 dynamic-slice.1
  25.9 1.7 %copy.21 = bf16[8,294,294]{2,1,0:T(8,128)(2,1)S(1)} copy(bf16[8,294,294]{2,0,1:T(8,128)(2,1)} %param.15) | data formatting | bytes 2765952 | tf_op args[7]
  27.6 0.0 copy-start.3
  27.7 0.0 copy-start.4
  28.9 0.0 collective-permute-done.3
  28.9 1.9 %fusion.47 = bf16[8,294]{1,0:T(8,128)(2,1)S(1)} fusion(bf16[8,294,294]{2,0,1:T(8,128)(2,1)} %param.13, bf16[4,8,294]{2,1,0:T(8,128)(2,1)S(1)} %collective-permute-done.3, bf16[4,8,294]{2,1,0:T(8,128)(2,1)S(1)} %maximum_select_fusion.2, pred[]{:T(512)S(6)} %eq.80), kind=kOutput, calls=%fused_computation.30 | convolution fusion | flops 11122608 | bytes 1425313 | tf_op jit(solution)/shard_map/knw,kwv->nv/dot_general | solution.py:77
  30.8 0.1 reshape.38
  30.9 0.1 dynamic_slice.9
  31.0 0.2 dynamic-update-slice
  31.2 11.4 %all-reduce = bf16[2352]{0:T(1024)(128)(2,1)S(1)} all-reduce(bf16[2352]{0:T(1024)(128)(2,1)S(1)} %dynamic-update-slice), channel_id=2, replica_groups=mesh['morton'=8,'sub'=4] {'sub'}, use_global_device_ids=true, to_apply=%add | all-reduce | flops 2352 | bytes 9408
  42.6 0.3 dynamic-update-slice.1
  42.9 25.5 %all-reduce.1 = bf16[18816]{0:T(1024)(128)(2,1)S(1)} all-reduce(bf16[18816]{0:T(1024)(128)(2,1)S(1)} %dynamic-update-slice.1), channel_id=3, replica_groups=mesh['morton'=8,'sub'=4] {'morton'}, use_global_device_ids=true, to_apply=%add.1 | all-reduce | flops 18816 | bytes 75264
  68.4 0.1 reshape.44
  68.5 0.0 copy-done.3
  68.5 0.0 copy-done.4
  68.6 0.5 convolution_convert_fusion.1
  69.0 0.2 reshape.40
  69.2 3.0 %fusion.50 = bf16[8,294,1]{1,0,2:T(8,128)(2,1)S(1)} fusion(bf16[16,294,294]{2,0,1:T(8,128)(2,1)} %param.14, bf16[16,8,294]{2,1,0:T(8,128)(2,1)S(1)} %reshape.40), kind=kOutput, calls=%fused_computation.31 | convolution fusion | flops 22129968 | bytes 2845920 | tf_op jit(solution)/shard_map/dot_general | solution.py:105
  72.3 0.6 fusion.6
  72.8 0.0 collective-permute-done
  72.8 0.0 collective-permute-done.1
  72.8 0.2 pad_maximum_fusion
  73.1 0.9 %reshape.35 = bf16[192,2352]{1,0:T(8,128)(2,1)S(1)} reshape(bf16[192,8,294]{2,1,0:T(8,128)(2,1)S(1)} %pad_maximum_fusion) | data formatting | bytes 1806336 | tf_op jit(solution)/shard_map/reshape | solution.py:114
  74.0 1.5 %convolution_convert_fusion = bf16[256,2352]{0,1:T(8,128)(2,1)S(1)} fusion(bf16[256,192]{1,0:T(8,128)(2,1)} %bitcast.79, bf16[192,2352]{1,0:T(8,128)(2,1)S(1)} %reshape.35), kind=kOutput, calls=%fused_computation | convolution fusion | flops 231813120 | bytes 2205696 | tf_op jit(solution)/shard_map/dot_general | solution.py:43
  75.5 0.8 %copy.19 = bf16[256,2352]{1,0:T(8,128)(2,1)S(1)} copy(bf16[256,2352]{0,1:T(8,128)(2,1)S(1)} %convolution_convert_fusion) | data formatting | bytes 2408448 | tf_op jit(solution)/shard_map/convert_element_type | solution.py:47
  76.4 2.0 %reshape.36 = bf16[16,16,8,294]{3,2,1,0:T(8,128)(2,1)S(1)} reshape(bf16[256,2352]{1,0:T(8,128)(2,1)S(1)} %copy.19) | data formatting | bytes 2408448 | tf_op jit(solution)/shard_map/reshape | solution.py:48
  78.3 4.4 %fusion.26 = bf16[16,8,294]{2,1,0:T(8,128)(2,1)} fusion(f32[16,8,294]{2,1,0:T(8,128)S(1)} %bitcast.78, bf16[16,294,294]{2,0,1:T(8,128)(2,1)} %param.14, bf16[16,16,8,294]{3,2,1,0:T(8,128)(2,1)S(1)} %reshape.36), kind=kOutput, calls=%fused_computation.22 | convolution fusion | flops 354117120 | bytes 4195968 | tf_op jit(solution)/shard_map/dot_general | solution.py:50
  (3 shorter events, 0.0 us)
Async XLA Ops:
  0.0 24.7 %copy-start.6 = (u32[32]{0:T(128)S(1)}, u32[32]{0:T(128)}, u32[]{:S(2)}) copy-start(u32[32]{0:T(128)} %constant.71) | copy-start | bytes 388
  0.0 25.3 %copy-start.5 = (u32[32]{0:T(128)S(1)}, u32[32]{0:T(128)}, u32[]{:S(2)}) copy-start(u32[32]{0:T(128)} %constant.76) | copy-start | bytes 388
  0.0 5.2 %copy-start = (bf16[16,8,294]{2,1,0:T(8,128)(2,1)S(1)}, bf16[16,8,294]{2,1,0:T(8,128)(2,1)}, u32[]{:S(2)}) copy-start(bf16[16,8,294]{2,1,0:T(8,128)(2,1)} %param.8) | copy-start | bytes 225796
  0.0 23.2 %copy-start.2 = (s32[16,189]{1,0:T(8,128)S(1)}, s32[16,189]{1,0:T(8,128)}, u32[]{:S(2)}) copy-start(s32[16,189]{1,0:T(8,128)} %param.10) | copy-start | bytes 36292
  0.0 23.2 %copy-start.1 = (s32[16,189]{1,0:T(8,128)S(1)}, s32[16,189]{1,0:T(8,128)}, u32[]{:S(2)}) copy-start(s32[16,189]{1,0:T(8,128)} %param.9) | copy-start | bytes 36292
  2.0 20.4 %collective-permute-start.2 = (bf16[2,8,294]{2,1,0:T(8,128)(2,1)S(1)}, bf16[2,8,294]{2,1,0:T(8,128)(2,1)S(1)}, u32[]{:S(2)}, u32[]{:S(2)}) collective-permute-start(bf16[2,8,294]{2,1,0:T(8,128)(2,1)S(1)} %fusion.34), channel_id=1, source_target_pairs={{0,1},{1,0},{2,3},{3,2},{4,5},{5,4},{6,7},{7,6},{8,9},{9,8},{10,11... | collective-permute-start | bytes 28232 | tf_op jit(solution)/shard_map/ppermute | solution.py:10
  19.8 53.0 %collective-permute-start = (bf16[64,8,294]{2,1,0:T(8,128)(2,1)S(1)}, bf16[64,8,294]{2,1,0:T(8,128)(2,1)S(1)}, u32[]{:S(2)}, u32[]{:S(2)}) collective-permute-start(bf16[64,8,294]{2,1,0:T(8,128)(2,1)S(1)} %all_gather.9), channel_id=1, source_target_pairs={{0,4},{4,8},{8,12},{12,16},{16,20},{20,24},{24,28},{1,5},{5,9},{9,... | collective-permute-start | bytes 903176 | tf_op jit(solution)/shard_map/ppermute | solution.py:21
  21.1 51.7 %collective-permute-start.1 = (bf16[64,8,294]{2,1,0:T(8,128)(2,1)S(1)}, bf16[64,8,294]{2,1,0:T(8,128)(2,1)S(1)}, u32[]{:S(2)}, u32[]{:S(2)}) collective-permute-start(bf16[64,8,294]{2,1,0:T(8,128)(2,1)S(1)} %all_gather.9), channel_id=1, source_target_pairs={{4,0},{8,4},{12,8},{16,12},{20,16},{24,20},{28,24},{5,1},{9,5},{13... | collective-permute-start | bytes 903176 | tf_op jit(solution)/shard_map/ppermute | solution.py:23
  22.5 6.4 %collective-permute-start.3 = (bf16[4,8,294]{2,1,0:T(8,128)(2,1)S(1)}, bf16[4,8,294]{2,1,0:T(8,128)(2,1)S(1)}, u32[]{:S(2)}, u32[]{:S(2)}) collective-permute-start(bf16[4,8,294]{2,1,0:T(8,128)(2,1)S(1)} %maximum_select_fusion.2), channel_id=1, source_target_pairs={{0,2},{1,3},{2,0},{3,1},{4,6},{5,7},{6,4},{7,5},{8,10},{9,11},{10,... | collective-permute-start | bytes 56456 | tf_op jit(solution)/shard_map/ppermute | solution.py:10
  27.6 40.9 %copy-start.3 = (s32[1,189]{1,0:T(1,128)S(1)}, s32[1,189]{1,0:T(1,128)}, u32[]{:S(2)}) copy-start(s32[1,189]{1,0:T(1,128)} %param.11) | copy-start | bytes 2272
  27.7 40.9 %copy-start.4 = (s32[1,189]{1,0:T(1,128)S(1)}, s32[1,189]{1,0:T(1,128)}, u32[]{:S(2)}) copy-start(s32[1,189]{1,0:T(1,128)} %param.12) | copy-start | bytes 2272
where the time goes:
time: 83.1 us; the launch traced here: 82.7 us
  blocking collectives  51.5 us (62%)
  matrix products  15.4 us (19%)
  local copies, waits for them, and re-layouts  7.59 us (9%)
  starting transfers between devices  6.51 us (8%)
  between operations  1.42 us (2%)
    unnamed x2, blocking collectives  36.9 us
    all_gather x1, blocking collectives, shards(): range_leaves = lax.all_gather(leaf_dens, 'sub', axis=0, tiled=True)  14.6 us
    dot_general x1, matrix products, far_block(): jnp.dot(rows_in, far_matrix, preferred_element_type=jnp.float32)  4.39 us
    ppermute x2, starting transfers between devices, from_partner(): return lax.ppermute(value, axis, pairs)  3.91 us
    unnamed x21, local copies, waits for them, and re-layouts  3.43 us
    dot_general x1, matrix products, shards(): jnp.dot(grand_rows, far_matrix, preferred_element_type=jnp.float32)  3.05 us
    dot_general x1, matrix products, shards(): jnp.einsum('jknw,kwv->jnv', children, up_ops, preferred_element_type=jnp....  2.02 us
    reshape x1, local copies, waits for them, and re-layouts, far_block(): aggregate.reshape(targets, classes_count, rhs_count, width)  1.96 us
  transfers between devices with their start and end apart: 4, of which 0 were waited for; matrix products, arithmetic and copies ran while one was open for 14% of the time, Pallas kernels for 0%

commit v1 on v0

v1 whole, which is shorter than its diff:
```python
import jax
import jax.numpy as jnp
from jax import lax
from jax.sharding import PartitionSpec as P


def swapped(value, axis, mask):
    count = lax.axis_size(axis)
    return lax.ppermute(value, axis, [(i, i ^ mask) for i in range(count)])


def doubled(rows, axis, masks):
    own = rows.shape[0]
    pieces = {0: 0}
    for mask in masks:
        other = swapped(rows, axis, mask)
        pieces.update({p ^ mask: at + len(pieces) for p, at in list(pieces.items())})
        rows = jnp.concatenate([rows, other], axis=0)
    return jnp.concatenate(
        [rows[pieces[p] * own : (pieces[p] + 1) * own] for p in range(len(pieces))], axis=0
    )


def bits_down(count):
    return [1 << bit for bit in reversed(range(count.bit_length() - 1))]


def unxored(rows, index, count):
    for bit in range(count.bit_length() - 1):
        shape = rows.shape
        split = rows.reshape((count >> (bit + 1), 2, 1 << bit) + shape[1:])
        flipped = jnp.concatenate([split[:, 1:], split[:, :1]], axis=1)
        rows = jnp.where((index >> bit) % 2 == 1, flipped, split).reshape(shape)
    return rows


def class_counts(sources, classes, pool_size, classes_count):
    source_hot = (
        sources[:, :, None] == jnp.arange(pool_size, dtype=jnp.int32)[None, None, :]
    ).astype(jnp.bfloat16)
    class_hot = (
        classes[:, :, None] == jnp.arange(classes_count, dtype=jnp.int32)[None, None, :]
    ).astype(jnp.bfloat16)
    return jnp.einsum(
        "tec,teq->tcq", class_hot, source_hot, preferred_element_type=jnp.float32
    ).astype(jnp.bfloat16)


def shards(
    leaf_dens, leaf_sources, leaf_classes, grand_sources, grand_classes, up_ops, far_ops, down_ops
):
    own_leaves, rhs_count, width = leaf_dens.shape
    classes_count = far_ops.shape[0]
    sub_count = lax.axis_size("sub")
    morton_count = lax.axis_size("morton")
    sub_index = lax.axis_index("sub")
    morton_index = lax.axis_index("morton")
    range_size = own_leaves * sub_count
    flat_width = rhs_count * width
    grand_span = 64 // own_leaves
    grands_here = range_size // 64
    position = sub_index % grand_span
    parents_here = own_leaves // 8
    far_matrix = far_ops.reshape(classes_count * width, width)

    own = leaf_dens.reshape(own_leaves, flat_width)
    range_rows = doubled(own, "sub", bits_down(sub_count))
    outer = [(i, i + 1) for i in range(1, morton_count - 1, 2)]
    outer = outer + [(j, i) for i, j in outer]
    outer_rows = lax.ppermute(range_rows, "morton", outer)
    inner_rows = swapped(range_rows, "morton", 1)

    children = range_rows.reshape(range_size // 8, 8, rhs_count, width)
    parent_dens = jnp.einsum(
        "jknw,kwv->jnv", children, up_ops, preferred_element_type=jnp.float32
    ).astype(jnp.bfloat16)
    parent_dens = parent_dens.reshape(grands_here, grand_span, parents_here, rhs_count, width)
    parent_dens = unxored(parent_dens.transpose(1, 0, 2, 3, 4), position, grand_span)
    parent_dens = parent_dens.transpose(1, 0, 2, 3, 4).reshape(grands_here, 8, rhs_count, width)
    grand_dens = jnp.einsum(
        "gknw,kwv->gnv", parent_dens, up_ops, preferred_element_type=jnp.float32
    ).astype(jnp.bfloat16)
    grand_pool = doubled(
        grand_dens.reshape(grands_here, flat_width),
        "morton",
        list(reversed(bits_down(morton_count))),
    )
    grand_count = grand_pool.shape[0]
    row_pick = sub_index // grand_span
    my_sources = lax.dynamic_slice_in_dim(grand_sources, row_pick, 1, 0)
    my_classes = lax.dynamic_slice_in_dim(grand_classes, row_pick, 1, 0)
    my_sources = my_sources ^ (morton_index * grands_here + row_pick)
    grand_counts = class_counts(my_sources, my_classes, grand_count, classes_count)[0]
    grand_agg = jnp.dot(grand_counts, grand_pool, preferred_element_type=jnp.float32).astype(
        jnp.bfloat16
    )

    slot = leaf_sources // range_size
    slot = jnp.where(morton_index % 2 == 1, slot, 2 - slot)
    places = slot * range_size + ((leaf_sources % range_size) ^ (sub_index * own_leaves))
    counts = class_counts(places, leaf_classes, 3 * range_size, classes_count)
    pool_rows = jnp.concatenate([inner_rows, range_rows, outer_rows], axis=0)
    aggregate = jnp.dot(
        counts.reshape(own_leaves * classes_count, 3 * range_size),
        pool_rows,
        preferred_element_type=jnp.float32,
    ).astype(jnp.bfloat16)
    aggregate = jnp.concatenate([aggregate, grand_agg], axis=0)
    rows_in = aggregate.reshape(own_leaves + 1, classes_count, rhs_count, width)
    rows_in = rows_in.transpose(0, 2, 1, 3).reshape(
        (own_leaves + 1) * rhs_count, classes_count * width
    )
    far = jnp.dot(rows_in, far_matrix, preferred_element_type=jnp.float32)
    far = far.reshape(own_leaves + 1, rhs_count, width)
    leaf_far, grand_local = far[:-1], far[-1].astype(jnp.bfloat16)

    parent_ops = lax.dynamic_slice_in_dim(down_ops, position * parents_here, parents_here, 0)
    parent_local = jnp.einsum(
        "nw,jwv->jnv", grand_local, parent_ops, preferred_element_type=jnp.float32
    ).astype(jnp.bfloat16)
    downward = jnp.einsum(
        "jnw,kwv->jknv", parent_local, down_ops, preferred_element_type=jnp.float32
    )
    downward = downward.reshape(own_leaves, rhs_count, width)
    return (leaf_far + downward).astype(jnp.bfloat16)


def solution(mesh):
    placed = (
        P(("morton", "sub"), None, None),
        P(("morton", "sub"), None),
        P(("morton", "sub"), None),
        P("morton", None),
        P("morton", None),
        P(),
        P(),
        P(),
    )
    return jax.shard_map(
        shards,
        mesh=mesh,
        in_specs=placed,
        out_specs=P(("morton", "sub"), None, None),
        check_vma=False,
    )
```

time: 83.1 us -> 75.8 us (0.912)
  the two profiles are of different devices: /device:TPU:0 before, /device:TPU:1 now
where the time goes in v1:
time: 75.8 us; the launch traced here: 74.9 us
  local copies, waits for them, and re-layouts  39.2 us (52%)
  starting transfers between devices  16.4 us (22%)
  matrix products  8.73 us (12%)
  waiting for transfers between devices  7.23 us (10%)
  other arithmetic  3.08 us (4%)
    unnamed x23, local copies, waits for them, and re-layouts  13.7 us
    ppermute x6, starting transfers between devices, swapped(): return lax.ppermute(value, axis, [(i, i ^ mask) for i in range(count)])  12.5 us
    reshape x1, local copies, waits for them, and re-layouts, shards(): far_matrix = far_ops.reshape(classes_count * width, width)  5.53 us
    ppermute x6, waiting for transfers between devices, swapped(): return lax.ppermute(value, axis, [(i, i ^ mask) for i in range(count)])  5.28 us
    reshape x1, local copies, waits for them, and re-layouts, shards(): rows_in = aggregate.reshape(own_leaves + 1, classes_count, rhs_count, width)  4.47 us
    ppermute x1, starting transfers between devices, shards(): outer_rows = lax.ppermute(range_rows, 'morton', outer)  3.96 us
    reshape x1, local copies, waits for them, and re-layouts, shards(): rows_in.transpose(0, 2, 1, 3)  3.93 us
    concatenate x1, local copies, waits for them, and re-layouts, shards(): aggregate = jnp.concatenate([aggregate, grand_agg], axis=0)  3.64 us
  transfers between devices with their start and end apart: 7, of which 4 were waited for; matrix products, arithmetic and copies ran while one was open for 31% of the time, Pallas kernels for 0%

profile of v1, /device:TPU:1, one launch (start us, length us, event | category | flops | bytes accessed | tf_op | source)
XLA Modules:
  0.0 74.9 jit_solution(2488290059958860594)
XLA Ops:
  0.0 0.0 copy-start
  0.0 1.2 %reshape.210 = bf16[16,2352]{1,0:T(8,128)(2,1)S(1)} reshape(bf16[16,8,294]{2,1,0:T(8,128)(2,1)} %param.8) | data formatting | bytes 150528 | tf_op jit(solution)/shard_map/reshape | solution.py:66
  1.2 3.2 %collective-permute-start = (bf16[16,2352]{1,0:T(8,128)(2,1)S(1)}, bf16[16,2352]{1,0:T(8,128)(2,1)S(1)}, u32[]{:S(2)}, u32[]{:S(2)}) collective-permute-start(bf16[16,2352]{1,0:T(8,128)(2,1)S(1)} %reshape.210), channel_id=1, source_target_pairs={{0,2},{1,3},{2,0},{3,1},{4,6},{5,7},{6,4},{7,5},{8,10},{9,11},{10,... | collective-permute-start | bytes 225800 | tf_op jit(solution)/shard_map/ppermute | solution.py:9
  4.4 1.8 %collective-permute-done = bf16[16,2352]{1,0:T(8,128)(2,1)S(1)} collective-permute-done((bf16[16,2352]{1,0:T(8,128)(2,1)S(1)}, bf16[16,2352]{1,0:T(8,128)(2,1)S(1)}, u32[]{:S(2)}, u32[]{:S(2)}) %collective-permute-start) | collective-permute-done | bytes 75296 | tf_op jit(solution)/shard_map/ppermute | solution.py:9
  6.2 0.0 copy-start.1
  6.2 3.0 %collective-permute-start.1 = (bf16[32,2352]{1,0:T(8,128)(2,1)S(1)}, bf16[32,2352]{1,0:T(8,128)(2,1)S(1)}, u32[]{:S(2)}, u32[]{:S(2)}) collective-permute-start(bf16[32,2352]{1,0:T(8,128)(2,1)S(1)} %pad_maximum_fusion.2), channel_id=1, source_target_pairs={{0,1},{1,0},{2,3},{3,2},{4,5},{5,4},{6,7},{7,6},{8,9},{9,8},{10,11... | collective-permute-start | bytes 451592 | tf_op jit(solution)/shard_map/ppermute | solution.py:9
  9.2 2.7 %collective-permute-done.1 = bf16[32,2352]{1,0:T(8,128)(2,1)S(1)} collective-permute-done((bf16[32,2352]{1,0:T(8,128)(2,1)S(1)}, bf16[32,2352]{1,0:T(8,128)(2,1)S(1)}, u32[]{:S(2)}, u32[]{:S(2)}) %collective-permute-start.1) | collective-permute-done | bytes 150560 | tf_op jit(solution)/shard_map/ppermute | solution.py:9
  11.9 0.0 copy-start.2
  11.9 0.8 %pad_maximum_fusion.1 = bf16[64,2352]{1,0:T(8,128)(2,1)} fusion(bf16[16,2352]{1,0:T(8,128)(2,1)S(1)} %get-tuple-element.6, bf16[16,2352]{1,0:T(8,128)(2,1)S(1)} %collective-permute-done, bf16[16,2352]{1,0:T(8,128)(2,1)S(1)} %get-tuple-element.5, bf16[16,2352]{1,0:T(8,128)(2,1)S(1)} %reshape.210), kind=kLoop, calls=%fused_computation.22 | loop fusion | flops 1204224 | bytes 602112 | tf_op jit(solution)/shard_map/concatenate | solution.py:19
  12.6 1.5 %reshape.211 = bf16[8,8,8,294]{3,2,1,0:T(8,128)(2,1)S(1)} reshape(bf16[64,2352]{1,0:T(8,128)(2,1)} %pad_maximum_fusion.1) | data formatting | bytes 602112 | tf_op jit(solution)/shard_map/reshape | solution.py:73
  14.1 0.0 copy-done
  14.1 0.5 fusion.13
  14.6 0.0 copy-done.1
  14.7 0.0 copy-done.2
  14.7 0.0 copy-start.4
  14.7 0.0 copy-start.7
  14.7 0.0 copy-start.6
  14.8 0.4 fusion.20
  15.2 0.1 reshape.212
  15.3 2.9 %collective-permute-start.4 = (bf16[1,2352]{1,0:T(2,128)(2,1)S(1)}, bf16[1,2352]{1,0:T(2,128)(2,1)S(1)}, u32[]{:S(2)}, u32[]{:S(2)}) collective-permute-start(bf16[1,2352]{1,0:T(2,128)(2,1)S(1)} %reshape.212), channel_id=1, source_target_pairs={{0,4},{4,0},{8,12},{12,8},{16,20},{20,16},{24,28},{28,24},{1,5},{5... | collective-permute-start | bytes 14120 | tf_op jit(solution)/shard_map/ppermute | solution.py:9
  18.2 0.0 copy-done.4
  18.3 0.8 %collective-permute-done.4 = bf16[1,2352]{1,0:T(2,128)(2,1)S(1)} collective-permute-done((bf16[1,2352]{1,0:T(2,128)(2,1)S(1)}, bf16[1,2352]{1,0:T(2,128)(2,1)S(1)}, u32[]{:S(2)}, u32[]{:S(2)}) %collective-permute-start.4) | collective-permute-done | bytes 4736 | tf_op jit(solution)/shard_map/ppermute | solution.py:9
  19.1 1.5 %collective-permute-start.5 = (bf16[2,2352]{1,0:T(2,128)(2,1)S(1)}, bf16[2,2352]{1,0:T(2,128)(2,1)S(1)}, u32[]{:S(2)}, u32[]{:S(2)}) collective-permute-start(bf16[2,2352]{1,0:T(2,128)(2,1)S(1)} %pad_maximum_fusion.6), channel_id=1, source_target_pairs={{0,8},{4,12},{8,0},{12,4},{16,24},{20,28},{24,16},{28,20},{1,9},{5... | collective-permute-start | bytes 28232 | tf_op jit(solution)/shard_map/ppermute | solution.py:9
  20.6 0.0 copy-done.7
  20.6 1.5 %fusion.9 = bf16[16,16,192]{2,1,0:T(8,128)(2,1)} fusion(s32[16,189]{1,0:T(8,128)S(1)} %fusion.37, s32[16,189]{1,0:T(8,128)S(1)} %copy-done.7), kind=kOutput, calls=%fused_computation.13 | convolution fusion | flops 19257600 | bytes 122496 | tf_op jit(solution)/shard_map/tec,teq->tcq/dot_general | solution.py:44
  22.1 0.6 collective-permute-start.2
  22.7 0.0 collective-permute-done.5
  22.7 1.3 %collective-permute-start.6 = (bf16[4,2352]{1,0:T(4,128)(2,1)S(1)}, bf16[4,2352]{1,0:T(4,128)(2,1)S(1)}, u32[]{:S(2)}, u32[]{:S(2)}) collective-permute-start(bf16[4,2352]{1,0:T(4,128)(2,1)S(1)} %pad_maximum_fusion.5), channel_id=1, source_target_pairs={{0,16},{4,20},{8,24},{12,28},{16,0},{20,4},{24,8},{28,12},{1,17},{... | collective-permute-start | bytes 56456 | tf_op jit(solution)/shard_map/ppermute | solution.py:9
  24.0 0.0 copy-done.6
  24.0 6.9 %copy.31 = bf16[16,294,294]{1,0,2:T(8,128)(2,1)} copy(bf16[16,294,294]{2,0,1:T(8,128)(2,1)} %param.14) | data formatting | bytes 5531904 | tf_op args[6]
  31.0 5.5 %reshape.215 = bf16[4704,294]{0,1:T(8,128)(2,1)S(1)} reshape(bf16[16,294,294]{1,0,2:T(8,128)(2,1)} %copy.31) | data formatting | bytes 5531904 | tf_op jit(solution)/shard_map/reshape | solution.py:64
  36.5 0.0 copy-start.5
  36.5 3.0 %copy.32 = bf16[8,294,294]{2,1,0:T(8,128)(2,1)} copy(bf16[8,294,294]{2,0,1:T(8,128)(2,1)} %param.15) | data formatting | bytes 2765952 | tf_op args[7]
  39.5 4.0 %collective-permute-start.3 = (bf16[64,2352]{1,0:T(8,128)(2,1)}, bf16[64,2352]{1,0:T(8,128)(2,1)}, u32[]{:S(2)}, u32[]{:S(2)}) collective-permute-start(bf16[64,2352]{1,0:T(8,128)(2,1)} %pad_maximum_fusion.1), channel_id=1, source_target_pairs={{4,8},{12,16},{20,24},{8,4},{16,12},{24,20},{5,9},{13,17},{21,25},... | collective-permute-start | bytes 903176 | tf_op jit(solution)/shard_map/ppermute | solution.py:70
  43.5 0.0 collective-permute-done.6
  43.5 0.0 copy-done.5
  43.5 1.0 %convolution_convert_fusion.1 = bf16[16,2352]{1,0:T(8,128)(2,1)} fusion(bf16[4,2352]{1,0:T(4,128)(2,1)S(1)} %collective-permute-done.6, bf16[2,2352]{1,0:T(2,128)(2,1)S(1)} %collective-permute-done.5, bf16[1,2352]{1,0:T(2,128)(2,1)S(1)} %collective-permute-done.4, bf16[1,2352]{1,0:T(2,128)(2,1)S(1)} %reshape.212, s32[189]{0:T(256)S(1)} %bitcast.84, ...), kind=kOutput, calls=%fused_computation.1 | convolution fusion | flops 843320 | bytes 114408 | tf_op jit(solution)/shard_map/dot_general | solution.py:94
  44.5 1.2 %copy.28 = bf16[16,2352]{0,1:T(8,128)(2,1)S(1)} copy(bf16[16,2352]{1,0:T(8,128)(2,1)} %convolution_convert_fusion.1) | data formatting | bytes 150528 | tf_op jit(solution)/shard_map/convert_element_type | solution.py:94
  45.7 0.0 copy-start.3
  45.7 0.0 collective-permute-done.2
  45.7 1.0 %constant_dynamic-update-slice_fusion.5 = bf16[192,2352]{1,0:T(8,128)(2,1)S(1)} fusion(bf16[64,2352]{1,0:T(8,128)(2,1)} %collective-permute-done.2), kind=kLoop, calls=%fused_computation.65 | loop fusion | bytes 612352
  46.7 0.9 %constant_dynamic-update-slice_fusion.3 = bf16[192,2352]{1,0:T(8,128)(2,1)S(1)} fusion(bf16[192,2352]{1,0:T(8,128)(2,1)S(1)} %constant_dynamic-update-slice_fusion.4, bf16[32,2352]{1,0:T(8,128)(2,1)} %copy-done.2), kind=kLoop, calls=%fused_computation.63 | loop fusion | bytes 153088
  47.6 0.9 %constant_dynamic-update-slice_fusion.2 = bf16[192,2352]{1,0:T(8,128)(2,1)S(1)} fusion(bf16[192,2352]{1,0:T(8,128)(2,1)S(1)} %constant_dynamic-update-slice_fusion.3, bf16[16,2352]{1,0:T(8,128)(2,1)} %copy-done.1), kind=kLoop, calls=%fused_computation.62 | loop fusion | bytes 153088
  48.5 0.9 %constant_dynamic-update-slice_fusion.1 = bf16[192,2352]{1,0:T(8,128)(2,1)S(1)} fusion(bf16[192,2352]{1,0:T(8,128)(2,1)S(1)} %constant_dynamic-update-slice_fusion.2, bf16[32,2352]{1,0:T(8,128)(2,1)} %copy-done.2), kind=kLoop, calls=%fused_computation.61 | loop fusion | bytes 153088
  49.4 1.9 %collective-permute-done.3 = bf16[64,2352]{1,0:T(8,128)(2,1)} collective-permute-done((bf16[64,2352]{1,0:T(8,128)(2,1)}, bf16[64,2352]{1,0:T(8,128)(2,1)}, u32[]{:S(2)}, u32[]{:S(2)}) %collective-permute-start.3) | collective-permute-done | bytes 301088 | tf_op jit(solution)/shard_map/ppermute | solution.py:70
  51.4 1.0 %constant_dynamic-update-slice_fusion = bf16[192,2352]{1,0:T(8,128)(2,1)S(1)} fusion(bf16[192,2352]{1,0:T(8,128)(2,1)S(1)} %constant_dynamic-update-slice_fusion.1, bf16[64,2352]{1,0:T(8,128)(2,1)} %collective-permute-done.3), kind=kLoop, calls=%fused_computation.60 | loop fusion | bytes 612352 | tf_op jit(solution)/shard_map/concatenate | solution.py:102
  52.4 0.0 copy-done.3
  52.4 0.6 convolution_convert_fusion
  53.0 1.5 %pad_maximum_fusion = bf16[272,2352]{0,1:T(8,128)(2,1)} fusion(bf16[16,2352]{0,1:T(8,128)(2,1)S(1)} %copy.28, bf16[256,2352]{0,1:T(8,128)(2,1)S(1)} %convolution_convert_fusion), kind=kLoop, calls=%fused_computation.8 | loop fusion | flops 2558976 | bytes 2558976 | tf_op jit(solution)/shard_map/concatenate | solution.py:108
  54.5 3.6 %copy.29 = bf16[272,2352]{1,0:T(8,128)(2,1)} copy(bf16[272,2352]{0,1:T(8,128)(2,1)} %pad_maximum_fusion) | data formatting | bytes 2558976 | tf_op jit(solution)/shard_map/concatenate | solution.py:108
  58.1 4.5 %reshape.213 = bf16[17,16,8,294]{3,2,1,0:T(8,128)(2,1)} reshape(bf16[272,2352]{1,0:T(8,128)(2,1)} %copy.29) | data formatting | bytes 2558976 | tf_op jit(solution)/shard_map/reshape | solution.py:109
  62.6 3.0 %copy.30 = bf16[17,8,16,294]{3,2,1,0:T(8,128)(2,1)} copy(bf16[17,8,16,294]{3,1,2,0:T(8,128)(2,1)} %bitcast.79) | data formatting | bytes 2558976 | tf_op jit(solution)/shard_map/transpose | solution.py:110
  65.6 3.9 %reshape.214 = bf16[136,4704]{1,0:T(8,128)(2,1)} reshape(bf16[17,8,16,294]{3,2,1,0:T(8,128)(2,1)} %copy.30) | data formatting | bytes 2558976 | tf_op jit(solution)/shard_map/reshape | solution.py:110
  69.5 2.5 %fusion.61 = f32[136,294]{1,0:T(8,128)S(1)} fusion(bf16[136,4704]{1,0:T(8,128)(2,1)} %reshape.214, bf16[4704,294]{0,1:T(8,128)(2,1)S(1)} %reshape.215), kind=kOutput, calls=%fused_computation.78 | convolution fusion | flops 376169472 | bytes 4205376 | tf_op jit(solution)/shard_map/dot_general | solution.py:113
  72.0 2.2 %fusion.1 = f32[2,8,8,294]{3,1,2,0:T(8,128)S(1)} fusion(bf16[8,294,294]{2,1,0:T(8,128)(2,1)} %copy.32, s32[]{:T(128)S(6)} %select_n.99, f32[136,294]{1,0:T(8,128)S(1)} %fusion.61), kind=kOutput, calls=%fused_computation.4 | convolution fusion | flops 24898272 | bytes 2429956 | tf_op jit(solution)/shard_map/jnw,kwv->jknv/dot_general | solution.py:121
  74.2 0.7 fusion.26
  (12 shorter events, 0.2 us)
Async XLA Ops:
  0.0 14.1 %copy-start = (bf16[8,294,294]{2,0,1:T(8,128)(2,1)S(1)}, bf16[8,294,294]{2,0,1:T(8,128)(2,1)}, u32[]{:S(2)}) copy-start(bf16[8,294,294]{2,0,1:T(8,128)(2,1)} %param.13) | copy-start | bytes 4148932
  1.2 5.0 %collective-permute-start = (bf16[16,2352]{1,0:T(8,128)(2,1)S(1)}, bf16[16,2352]{1,0:T(8,128)(2,1)S(1)}, u32[]{:S(2)}, u32[]{:S(2)}) collective-permute-start(bf16[16,2352]{1,0:T(8,128)(2,1)S(1)} %reshape.210), channel_id=1, source_target_pairs={{0,2},{1,3},{2,0},{3,1},{4,6},{5,7},{6,4},{7,5},{8,10},{9,11},{10,... | collective-permute-start | bytes 225800 | tf_op jit(solution)/shard_map/ppermute | solution.py:9
  6.2 8.5 %copy-start.1 = (bf16[16,2352]{1,0:T(8,128)(2,1)}, bf16[16,2352]{1,0:T(8,128)(2,1)S(1)}, u32[]{:S(2)}) copy-start(bf16[16,2352]{1,0:T(8,128)(2,1)S(1)} %collective-permute-done) | copy-start | bytes 225796
  6.2 5.7 %collective-permute-start.1 = (bf16[32,2352]{1,0:T(8,128)(2,1)S(1)}, bf16[32,2352]{1,0:T(8,128)(2,1)S(1)}, u32[]{:S(2)}, u32[]{:S(2)}) collective-permute-start(bf16[32,2352]{1,0:T(8,128)(2,1)S(1)} %pad_maximum_fusion.2), channel_id=1, source_target_pairs={{0,1},{1,0},{2,3},{3,2},{4,5},{5,4},{6,7},{7,6},{8,9},{9,8},{10,11... | collective-permute-start | bytes 451592 | tf_op jit(solution)/shard_map/ppermute | solution.py:9
  11.9 2.8 %copy-start.2 = (bf16[32,2352]{1,0:T(8,128)(2,1)}, bf16[32,2352]{1,0:T(8,128)(2,1)S(1)}, u32[]{:S(2)}) copy-start(bf16[32,2352]{1,0:T(8,128)(2,1)S(1)} %collective-permute-done.1) | copy-start | bytes 451588
  14.7 3.6 %copy-start.4 = (s32[16,189]{1,0:T(8,128)S(1)}, s32[16,189]{1,0:T(8,128)}, u32[]{:S(2)}) copy-start(s32[16,189]{1,0:T(8,128)} %param.9) | copy-start | bytes 36292
  14.7 5.9 %copy-start.7 = (s32[16,189]{1,0:T(8,128)S(1)}, s32[16,189]{1,0:T(8,128)}, u32[]{:S(2)}) copy-start(s32[16,189]{1,0:T(8,128)} %param.10) | copy-start | bytes 36292
  14.7 9.3 %copy-start.6 = (s32[1,189]{1,0:T(1,128)S(1)}, s32[1,189]{1,0:T(1,128)}, u32[]{:S(2)}) copy-start(s32[1,189]{1,0:T(1,128)} %param.11) | copy-start | bytes 2272
  15.3 3.7 %collective-permute-start.4 = (bf16[1,2352]{1,0:T(2,128)(2,1)S(1)}, bf16[1,2352]{1,0:T(2,128)(2,1)S(1)}, u32[]{:S(2)}, u32[]{:S(2)}) collective-permute-start(bf16[1,2352]{1,0:T(2,128)(2,1)S(1)} %reshape.212), channel_id=1, source_target_pairs={{0,4},{4,0},{8,12},{12,8},{16,20},{20,16},{24,28},{28,24},{1,5},{5... | collective-permute-start | bytes 14120 | tf_op jit(solution)/shard_map/ppermute | solution.py:9
  19.1 3.6 %collective-permute-start.5 = (bf16[2,2352]{1,0:T(2,128)(2,1)S(1)}, bf16[2,2352]{1,0:T(2,128)(2,1)S(1)}, u32[]{:S(2)}, u32[]{:S(2)}) collective-permute-start(bf16[2,2352]{1,0:T(2,128)(2,1)S(1)} %pad_maximum_fusion.6), channel_id=1, source_target_pairs={{0,8},{4,12},{8,0},{12,4},{16,24},{20,28},{24,16},{28,20},{1,9},{5... | collective-permute-start | bytes 28232 | tf_op jit(solution)/shard_map/ppermute | solution.py:9
  22.1 23.6 %collective-permute-start.2 = (bf16[64,2352]{1,0:T(8,128)(2,1)}, bf16[64,2352]{1,0:T(8,128)(2,1)}, u32[]{:S(2)}, u32[]{:S(2)}) collective-permute-start(bf16[64,2352]{1,0:T(8,128)(2,1)} %pad_maximum_fusion.1), channel_id=1, source_target_pairs={{0,4},{4,0},{8,12},{12,8},{16,20},{20,16},{24,28},{28,24},{1,5},{5... | collective-permute-start | bytes 903176 | tf_op jit(solution)/shard_map/ppermute | solution.py:9
  22.7 20.7 %collective-permute-start.6 = (bf16[4,2352]{1,0:T(4,128)(2,1)S(1)}, bf16[4,2352]{1,0:T(4,128)(2,1)S(1)}, u32[]{:S(2)}, u32[]{:S(2)}) collective-permute-start(bf16[4,2352]{1,0:T(4,128)(2,1)S(1)} %pad_maximum_fusion.5), channel_id=1, source_target_pairs={{0,16},{4,20},{8,24},{12,28},{16,0},{20,4},{24,8},{28,12},{1,17},{... | collective-permute-start | bytes 56456 | tf_op jit(solution)/shard_map/ppermute | solution.py:9
  36.5 7.0 %copy-start.5 = (s32[1,189]{1,0:T(1,128)S(1)}, s32[1,189]{1,0:T(1,128)}, u32[]{:S(2)}) copy-start(s32[1,189]{1,0:T(1,128)} %param.12) | copy-start | bytes 2272
  39.5 11.9 %collective-permute-start.3 = (bf16[64,2352]{1,0:T(8,128)(2,1)}, bf16[64,2352]{1,0:T(8,128)(2,1)}, u32[]{:S(2)}, u32[]{:S(2)}) collective-permute-start(bf16[64,2352]{1,0:T(8,128)(2,1)} %pad_maximum_fusion.1), channel_id=1, source_target_pairs={{4,8},{12,16},{20,24},{8,4},{16,12},{24,20},{5,9},{13,17},{21,25},... | collective-permute-start | bytes 903176 | tf_op jit(solution)/shard_map/ppermute | solution.py:70
  45.7 6.7 %copy-start.3 = (bf16[16,16,192]{2,1,0:T(8,128)(2,1)S(1)}, bf16[16,16,192]{2,1,0:T(8,128)(2,1)}, u32[]{:S(2)}) copy-start(bf16[16,16,192]{2,1,0:T(8,128)(2,1)} %fusion.9) | copy-start | bytes 294916

commit v2 on v1

v2 whole, which is shorter than its diff:
```python
import functools

import jax
import jax.numpy as jnp
from jax import lax
from jax.experimental import pallas as pl
from jax.experimental.pallas import tpu as pltpu
from jax.sharding import PartitionSpec as P

LANES = 128
F32 = jnp.float32
BF16 = jnp.bfloat16


def swapped(value, axis, mask):
    count = lax.axis_size(axis)
    return lax.ppermute(value, axis, [(i, i ^ mask) for i in range(count)])


def masks_of(count):
    return [1 << bit for bit in range(count.bit_length() - 1)]


class Lanes:
    def __init__(self, rhs_count, width):
        self.rhs_count, self.width = rhs_count, width
        self.main = width // LANES * LANES
        self.tail = width - self.main
        self.per_tile = LANES // self.tail if self.tail else 1
        self.tail_tiles = -(-rhs_count // self.per_tile) if self.tail else 0
        self.total = rhs_count * self.main + self.tail_tiles * LANES

    def main_of(self, n):
        return slice(n * self.main, (n + 1) * self.main)

    def tail_of(self, n):
        start = self.rhs_count * self.main + n // self.per_tile * LANES
        start += n % self.per_tile * self.tail
        return slice(start, start + self.tail)

    def take(self, rows, n):
        return jnp.concatenate([rows[:, self.main_of(n)], rows[:, self.tail_of(n)]], axis=1)


def tiles_of(width):
    return -(-width // LANES)


def fill(scratch, rows):
    for tile in range(scratch.shape[0]):
        part = rows[:, tile * LANES : (tile + 1) * LANES]
        scratch[tile, :, : part.shape[1]] = part


def every(scratch, start, size, stride, width):
    parts = [scratch[tile, pl.ds(start, size, stride=stride), :] for tile in range(tiles_of(width))]
    parts[-1] = parts[-1][:, : width - (len(parts) - 1) * LANES]
    return jnp.concatenate(parts, axis=1)


def flat_kernel(lanes, dens_ref, out_ref, wide):
    own, rhs_count, width = dens_ref.shape
    fill(wide, dens_ref[...].astype(F32).reshape(own * rhs_count, width))
    tails = []
    for n in range(rhs_count):
        rows = every(wide, n, own, rhs_count, width).astype(BF16)
        out_ref[:, lanes.main_of(n)] = rows[:, : lanes.main]
        tails.append(rows[:, lanes.main :])
    for tile in range(lanes.tail_tiles):
        parts = tails[tile * lanes.per_tile : (tile + 1) * lanes.per_tile]
        spare = LANES - len(parts) * lanes.tail
        parts.append(jnp.zeros((own, spare), BF16))
        start = rhs_count * lanes.main + tile * LANES
        out_ref[:, start : start + LANES] = jnp.concatenate(parts, axis=1)


def hot_rows(values, count):
    rows = lax.broadcasted_iota(jnp.int32, (count, values.shape[1]), 0)
    return jnp.where(rows == values, 1.0, 0.0).astype(BF16)


def class_counts(classes, sources, classes_count, pool_size):
    return lax.dot_general(
        hot_rows(classes, classes_count),
        hot_rows(sources, pool_size),
        (((1,), (1,)), ((), ())),
        preferred_element_type=F32,
    )


def counts_kernel(
    rhs_count,
    index_ref,
    sources_ref,
    classes_ref,
    grand_sources_ref,
    grand_classes_ref,
    counts_ref,
    grand_counts_ref,
    wide,
):
    own = sources_ref.shape[0]
    pool_size = counts_ref.shape[1]
    classes_count = counts_ref.shape[0] // own
    range_size = pool_size // 3
    sub_index, odd, row_pick, grand_index = (index_ref[i] for i in range(4))
    for t in range(own):
        sources = sources_ref[t : t + 1, :]
        slot = sources // range_size
        inside = sources - slot * range_size
        slot = jnp.where(odd == 1, slot, 2 - slot)
        places = slot * range_size + (inside ^ (sub_index * own))
        counts = class_counts(
            classes_ref[t : t + 1, :], places, classes_count, wide.shape[0] * LANES
        )
        for tile in range(wide.shape[0]):
            part = counts[:, tile * LANES : (tile + 1) * LANES]
            wide[tile, pl.ds(t, classes_count, stride=own), :] = part
    counts_ref[...] = every(wide, 0, own * classes_count, 1, pool_size).astype(BF16)
    group = grand_counts_ref.shape[0] // classes_count
    spread = grand_counts_ref.shape[1]
    places = grand_sources_ref[pl.ds(row_pick, 1), :] ^ grand_index
    classes = grand_classes_ref[pl.ds(row_pick, 1), :]
    entries = places.shape[1]
    column_grand = lax.broadcasted_iota(jnp.int32, (spread, entries), 0) // rhs_count
    source_hot = jnp.where(column_grand == places, 1.0, 0.0).astype(BF16)
    row_class = lax.broadcasted_iota(jnp.int32, (classes_count * group, entries), 0) // group
    class_hot = jnp.where(row_class == classes, 1.0, 0.0).astype(BF16)
    all_pairs = lax.dot_general(
        class_hot, source_hot, (((1,), (1,)), ((), ())), preferred_element_type=F32
    )
    row_rhs = lax.broadcasted_iota(jnp.int32, all_pairs.shape, 0) % group
    column_rhs = lax.broadcasted_iota(jnp.int32, all_pairs.shape, 1) % rhs_count
    grand_counts_ref[...] = jnp.where(row_rhs == column_rhs, all_pairs, 0.0).astype(BF16)


def grand_kernel(lanes, span, index_ref, rows_ref, up_ref, out_ref, wide, parents):
    rhs_count, width = lanes.rhs_count, lanes.width
    range_size = rows_ref.shape[0]
    fan = up_ref.shape[0]
    parent_count = range_size // fan
    position = index_ref[0]
    fill(wide, rows_ref[...].astype(F32))
    total = jnp.zeros((rhs_count * parent_count, width), F32)
    for k in range(fan):
        rows = every(wide, k, parent_count, fan, lanes.total)
        left = jnp.concatenate([lanes.take(rows, n) for n in range(rhs_count)], axis=0)
        total += jnp.dot(left.astype(BF16), up_ref[k], preferred_element_type=F32)
    fill(parents, total.astype(BF16).astype(F32))
    per_block = fan // span
    for grand in range(parent_count // fan):
        total = jnp.zeros((rhs_count, width), F32)
        for child in range(fan):
            rows = every(parents, grand * fan + child, rhs_count, parent_count, width)
            operator = ((child // per_block) ^ position) * per_block + child % per_block
            total += jnp.dot(rows.astype(BF16), up_ref[operator], preferred_element_type=F32)
        out_ref[grand * rhs_count : (grand + 1) * rhs_count, :] = total.astype(BF16)


def far_kernel(
    lanes,
    index_ref,
    counts_ref,
    grand_counts_ref,
    inner_ref,
    range_ref,
    outer_ref,
    grand_pool_ref,
    far_ref,
    down_ref,
    out_ref,
    aggregate,
    grand_aggregate,
    far_rows,
):
    own, rhs_count, width = out_ref.shape
    classes_count = far_ref.shape[0]
    fan = down_ref.shape[0]
    group = grand_counts_ref.shape[0] // classes_count
    parents_here = own // fan
    position = index_ref[0]
    grand_aggregate[...] = jnp.dot(
        grand_counts_ref[...], grand_pool_ref[...], preferred_element_type=F32
    ).astype(BF16)
    pool = jnp.concatenate([inner_ref[...], range_ref[...], outer_ref[...]], axis=0)
    aggregate[...] = jnp.dot(counts_ref[...], pool, preferred_element_type=F32).astype(BF16)
    total = jnp.zeros((rhs_count * own + group, width), F32)
    for c in range(classes_count):
        rows = aggregate[c * own : (c + 1) * own, :]
        parts = [lanes.take(rows, n) for n in range(rhs_count)]
        parts.append(grand_aggregate[c * group : (c + 1) * group, :])
        total += jnp.dot(jnp.concatenate(parts, axis=0), far_ref[c], preferred_element_type=F32)
    pad = jnp.zeros((own, far_rows.shape[0] * LANES - width), F32)
    for n in range(rhs_count):
        rows = jnp.concatenate([total[n * own : (n + 1) * own, :], pad], axis=1)
        for tile in range(far_rows.shape[0]):
            part = rows[:, tile * LANES : (tile + 1) * LANES]
            far_rows[tile, pl.ds(n, own, stride=rhs_count), :] = part
    grand_local = total[rhs_count * own :, :].astype(BF16)
    parent_local = []
    for j in range(parents_here):
        operator = down_ref[position * parents_here + j]
        local = jnp.dot(grand_local, operator, preferred_element_type=F32)
        parent_local.append(local[:rhs_count, :])
    parent_local = jnp.concatenate(parent_local, axis=0).astype(BF16)
    for k in range(fan):
        downward = jnp.dot(parent_local, down_ref[k], preferred_element_type=F32)
        for j in range(parents_here):
            leaf = j * fan + k
            local = every(far_rows, leaf * rhs_count, rhs_count, 1, width)
            local += downward[j * rhs_count : (j + 1) * rhs_count, :]
            out_ref[leaf] = local.astype(BF16)


def tiled(rows, width):
    return pltpu.VMEM((tiles_of(width), rows, LANES), F32)


def call(kernel, outs, scratch, scalars, *operands):
    whole = pl.BlockSpec(memory_space=pltpu.VMEM)
    specs = [pl.BlockSpec(memory_space=pltpu.SMEM)] * len(scalars) + [whole] * len(operands)
    return pl.pallas_call(
        kernel,
        out_shape=outs,
        in_specs=specs,
        out_specs=jax.tree.map(lambda _: whole, outs),
        scratch_shapes=scratch,
    )(*scalars, *operands)


def shards(
    leaf_dens, leaf_sources, leaf_classes, grand_sources, grand_classes, up_ops, far_ops, down_ops
):
    own, rhs_count, width = leaf_dens.shape
    classes_count = far_ops.shape[0]
    fan = up_ops.shape[0]
    sub_count, morton_count = lax.axis_size("sub"), lax.axis_size("morton")
    sub_index, morton_index = lax.axis_index("sub"), lax.axis_index("morton")
    range_size = own * sub_count
    leaves_of_grand = fan * fan
    grand_span = leaves_of_grand // own
    grands_here = range_size // leaves_of_grand
    grand_count = morton_count * grands_here
    position = sub_index % grand_span
    row_pick = sub_index // grand_span
    lanes = Lanes(rhs_count, width)
    struct = jax.ShapeDtypeStruct

    rows = call(
        functools.partial(flat_kernel, lanes),
        struct((own, lanes.total), BF16),
        [tiled(own * rhs_count, width)],
        [],
        leaf_dens,
    )
    blocks = {0: rows}
    for mask in reversed(masks_of(sub_count)):
        held = sorted(blocks)
        joined = jnp.concatenate([blocks[p] for p in held], axis=0) if len(held) > 1 else rows
        other = swapped(joined, "sub", mask)
        for at, p in enumerate(held):
            blocks[p ^ mask] = other[at * own : (at + 1) * own]
    range_rows = jnp.concatenate([blocks[p] for p in range(sub_count)], axis=0)
    outer = [(i, i + 1) for i in range(1, morton_count - 1, 2)]
    outer = outer + [(j, i) for i, j in outer]
    outer_rows = lax.ppermute(range_rows, "morton", outer)
    inner_rows = swapped(range_rows, "morton", 1)

    index = jnp.stack(
        [sub_index, morton_index % 2, row_pick, morton_index * grands_here + row_pick]
    ).astype(jnp.int32)
    group = -(-rhs_count // 16) * 16
    counts, grand_counts = call(
        functools.partial(counts_kernel, rhs_count),
        (
            struct((classes_count * own, 3 * range_size), BF16),
            struct((classes_count * group, grand_count * rhs_count), BF16),
        ),
        [tiled(classes_count * own, 3 * range_size)],
        [index],
        leaf_sources,
        leaf_classes,
        grand_sources,
        grand_classes,
    )

    place = position.reshape(1).astype(jnp.int32)
    grand_pool = call(
        functools.partial(grand_kernel, lanes, grand_span),
        struct((grands_here * rhs_count, width), BF16),
        [
            tiled(range_size, lanes.total),
            tiled(rhs_count * range_size // fan, width),
        ],
        [place],
        range_rows,
        up_ops,
    )
    for mask in masks_of(morton_count):
        grand_pool = jnp.concatenate([grand_pool, swapped(grand_pool, "morton", mask)], axis=0)

    return call(
        functools.partial(far_kernel, lanes),
        struct(leaf_dens.shape, BF16),
        [
            pltpu.VMEM((classes_count * own, lanes.total), BF16),
            pltpu.VMEM((classes_count * group, width), BF16),
            tiled(own * rhs_count, width),
        ],
        [place],
        counts,
        grand_counts,
        inner_rows,
        range_rows,
        outer_rows,
        grand_pool,
        far_ops,
        down_ops,
    )


def solution(mesh):
    placed = (
        P(("morton", "sub"), None, None),
        P(("morton", "sub"), None),
        P(("morton", "sub"), None),
        P("morton", None),
        P("morton", None),
        P(),
        P(),
        P(),
    )
    return jax.shard_map(
        shards,
        mesh=mesh,
        in_specs=placed,
        out_specs=P(("morton", "sub"), None, None),
        check_vma=False,
    )
```

time: 75.8 us -> 43.7 us (0.58)
  the two profiles are of different devices: /device:TPU:1 before, /device:TPU:0 now
where the time goes in v2:
time: 43.7 us; the launch traced here: 43.3 us
  Pallas kernels  13.2 us (30%)
  starting transfers between devices  10.8 us (25%)
  local copies, waits for them, and re-layouts  7.94 us (18%)
  waiting for transfers between devices  7.03 us (16%)
  other arithmetic  4.33 us (10%)
    pallas_call x4, Pallas kernels, call(): pl.pallas_call(kernel, out_shape=outs, in_specs=specs, out_specs=jax.tree...  13.2 us
    ppermute x6, starting transfers between devices, swapped(): return lax.ppermute(value, axis, [(i, i ^ mask) for i in range(count)])  10.1 us
    unnamed x17, local copies, waits for them, and re-layouts  7.93 us
    ppermute x6, waiting for transfers between devices, swapped(): return lax.ppermute(value, axis, [(i, i ^ mask) for i in range(count)])  7.03 us
    concatenate x3, other arithmetic, shards(): jnp.concatenate([grand_pool, swapped(grand_pool, 'morton', mask)], axis=0)  2.02 us
    concatenate x1, other arithmetic, shards(): jnp.concatenate([blocks[p] for p in held], axis=0)  0.9 us
  transfers between devices with their start and end apart: 7, of which 3 were waited for; matrix products, arithmetic and copies ran while one was open for 21% of the time, Pallas kernels for 5%

profile of v2, /device:TPU:0, one launch (start us, length us, event | category | flops | bytes accessed | tf_op | source)
XLA Modules:
  0.0 43.3 jit_solution(2462360122555585307)
XLA Ops:
  0.0 1.6 %shard_map.83 = bf16[16,2432]{1,0:T(8,128)(2,1)} custom-call(bf16[16,8,294]{2,1,0:T(8,128)(2,1)} %dens_ref.1), custom_call_target="tpu_custom_call" | custom-call | tf_op jit(solution)/shard_map/pallas_call | solution.py:222
  1.6 4.1 %collective-permute-start = (bf16[16,2432]{1,0:T(8,128)(2,1)}, bf16[16,2432]{1,0:T(8,128)(2,1)S(1)}, u32[]{:S(2)}, u32[]{:S(2)}) collective-permute-start(bf16[16,2432]{1,0:T(8,128)(2,1)} %shard_map.83), channel_id=1, source_target_pairs={{0,2},{1,3},{2,0},{3,1},{4,6},{5,7},{6,4},{7,5},{8,10},{9,11},{10,... | collective-permute-start | bytes 233480 | tf_op jit(solution)/shard_map/ppermute | solution.py:17
  5.7 4.3 %collective-permute-done = bf16[16,2432]{1,0:T(8,128)(2,1)S(1)} collective-permute-done((bf16[16,2432]{1,0:T(8,128)(2,1)}, bf16[16,2432]{1,0:T(8,128)(2,1)S(1)}, u32[]{:S(2)}, u32[]{:S(2)}) %collective-permute-start) | collective-permute-done | bytes 77856 | tf_op jit(solution)/shard_map/ppermute | solution.py:17
  9.9 0.9 %pad_maximum_fusion.1 = bf16[32,2432]{1,0:T(8,128)(2,1)S(1)} fusion(bf16[16,2432]{1,0:T(8,128)(2,1)S(1)} %collective-permute-done, bf16[16,2432]{1,0:T(8,128)(2,1)} %shard_map.83), kind=kLoop, calls=%fused_computation.1 | loop fusion | flops 311296 | bytes 311296 | tf_op jit(solution)/shard_map/concatenate | solution.py:259
  10.8 0.9 %collective-permute-start.1 = (bf16[32,2432]{1,0:T(8,128)(2,1)S(1)}, bf16[32,2432]{1,0:T(8,128)(2,1)S(1)}, u32[]{:S(2)}, u32[]{:S(2)}) collective-permute-start(bf16[32,2432]{1,0:T(8,128)(2,1)S(1)} %pad_maximum_fusion.1), channel_id=1, source_target_pairs={{0,1},{1,0},{2,3},{3,2},{4,5},{5,4},{6,7},{7,6},{8,9},{9,8},{10,11... | collective-permute-start | bytes 466952 | tf_op jit(solution)/shard_map/ppermute | solution.py:17
  11.7 0.0 copy-start.3
  11.7 3.0 %copy.9.up_ref = bf16[8,294,294]{2,1,0:T(8,128)(2,1)} copy(bf16[8,294,294]{2,0,1:T(8,128)(2,1)} %param.13) | data formatting | bytes 2765952 | tf_op args[5]
  14.7 0.0 copy-start.2
  14.7 1.4 %collective-permute-done.1 = bf16[32,2432]{1,0:T(8,128)(2,1)S(1)} collective-permute-done((bf16[32,2432]{1,0:T(8,128)(2,1)S(1)}, bf16[32,2432]{1,0:T(8,128)(2,1)S(1)}, u32[]{:S(2)}, u32[]{:S(2)}) %collective-permute-start.1) | collective-permute-done | bytes 155680 | tf_op jit(solution)/shard_map/ppermute | solution.py:17
  16.1 0.0 copy-done.3
  16.2 0.8 %pad_maximum_fusion.rows_ref.range_ref = bf16[64,2432]{1,0:T(8,128)(2,1)} fusion(bf16[16,2432]{1,0:T(8,128)(2,1)S(1)} %get-tuple-element.10, bf16[16,2432]{1,0:T(8,128)(2,1)S(1)} %collective-permute-done, bf16[16,2432]{1,0:T(8,128)(2,1)S(1)} %get-tuple-element.9, bf16[16,2432]{1,0:T(8,128)(2,1)S(1)} %copy-done.3), kind=kLoop, calls=%fused_computation | loop fusion | flops 1245184 | bytes 622592 | tf_op jit(solution)/shard_map/concatenate | solution.py:263
  16.9 0.0 copy-start.1
  16.9 3.3 %shard_map.84 = bf16[8,294]{1,0:T(8,128)(2,1)} custom-call(s32[1]{0:T(128)} %bitcast.index_ref, bf16[64,2432]{1,0:T(8,128)(2,1)} %pad_maximum_fusion.rows_ref.range_ref, bf16[8,294,294]{2,1,0:T(8,128)(2,1)} %copy.9.up_ref), custom_call_target="tpu_custom_call" | custom-call | tf_op jit(solution)/shard_map/pallas_call | solution.py:222
  20.2 0.0 collective-permute-start.4
  20.2 1.4 %collective-permute-done.4 = bf16[8,294]{1,0:T(8,128)(2,1)S(1)} collective-permute-done((bf16[8,294]{1,0:T(8,128)(2,1)}, bf16[8,294]{1,0:T(8,128)(2,1)S(1)}, u32[]{:S(2)}, u32[]{:S(2)}) %collective-permute-start.4) | collective-permute-done | bytes 4736 | tf_op jit(solution)/shard_map/ppermute | solution.py:17
  21.6 0.7 %pad_maximum_fusion.4 = bf16[16,294]{1,0:T(8,128)(2,1)S(1)} fusion(bf16[8,294]{1,0:T(8,128)(2,1)S(1)} %collective-permute-done.4, bf16[8,294]{1,0:T(8,128)(2,1)} %shard_map.84), kind=kLoop, calls=%fused_computation.4 | loop fusion | flops 18816 | bytes 18816 | tf_op jit(solution)/shard_map/concatenate | solution.py:300
  22.3 1.7 %collective-permute-start.5 = (bf16[16,294]{1,0:T(8,128)(2,1)S(1)}, bf16[16,294]{1,0:T(8,128)(2,1)S(1)}, u32[]{:S(2)}, u32[]{:S(2)}) collective-permute-start(bf16[16,294]{1,0:T(8,128)(2,1)S(1)} %pad_maximum_fusion.4), channel_id=1, source_target_pairs={{0,8},{4,12},{8,0},{12,4},{16,24},{20,28},{24,16},{28,20},{1,9},{5... | collective-permute-start | bytes 28232 | tf_op jit(solution)/shard_map/ppermute | solution.py:17
  24.0 0.0 copy-done.1
  24.0 0.7 %collective-permute-start.3 = (bf16[64,2432]{1,0:T(8,128)(2,1)S(1)}, bf16[64,2432]{1,0:T(8,128)(2,1)S(1)}, u32[]{:S(2)}, u32[]{:S(2)}) collective-permute-start(bf16[64,2432]{1,0:T(8,128)(2,1)S(1)} %copy-done.1), channel_id=1, source_target_pairs={{4,8},{12,16},{20,24},{8,4},{16,12},{24,20},{5,9},{13,17},{21,25},... | collective-permute-start | bytes 933896 | tf_op jit(solution)/shard_map/ppermute | solution.py:266
  24.7 1.7 %collective-permute-start.2 = (bf16[64,2432]{1,0:T(8,128)(2,1)S(1)}, bf16[64,2432]{1,0:T(8,128)(2,1)S(1)}, u32[]{:S(2)}, u32[]{:S(2)}) collective-permute-start(bf16[64,2432]{1,0:T(8,128)(2,1)S(1)} %copy-done.1), channel_id=1, source_target_pairs={{0,4},{4,0},{8,12},{12,8},{16,20},{20,16},{24,28},{28,24},{1,5},{5... | collective-permute-start | bytes 933896 | tf_op jit(solution)/shard_map/ppermute | solution.py:17
  26.4 0.0 collective-permute-done.5
  26.4 0.7 %pad_maximum_fusion.3 = bf16[32,294]{1,0:T(8,128)(2,1)S(1)} fusion(bf16[16,294]{1,0:T(8,128)(2,1)S(1)} %collective-permute-done.5, bf16[8,294]{1,0:T(8,128)(2,1)S(1)} %collective-permute-done.4, bf16[8,294]{1,0:T(8,128)(2,1)} %shard_map.84), kind=kLoop, calls=%fused_computation.3 | loop fusion | flops 56448 | bytes 37632 | tf_op jit(solution)/shard_map/concatenate | solution.py:300
  27.1 0.0 copy-start
  27.1 1.7 %collective-permute-start.6 = (bf16[32,294]{1,0:T(8,128)(2,1)S(1)}, bf16[32,294]{1,0:T(8,128)(2,1)S(1)}, u32[]{:S(2)}, u32[]{:S(2)}) collective-permute-start(bf16[32,294]{1,0:T(8,128)(2,1)S(1)} %pad_maximum_fusion.3), channel_id=1, source_target_pairs={{0,16},{4,20},{8,24},{12,28},{16,0},{20,4},{24,8},{28,12},{1,17},{... | collective-permute-start | bytes 56456 | tf_op jit(solution)/shard_map/ppermute | solution.py:17
  28.8 0.6 %pad_add_fusion.index_ref = s32[4]{0:T(128)} fusion(s32[1]{0:T(128)} %bitcast.4, s32[1]{0:T(128)} %bitcast.3, s32[1]{0:T(128)} %bitcast.2, s32[1]{0:T(128)} %bitcast.1), kind=kLoop, calls=%fused_computation.5 | loop fusion | flops 12 | bytes 32 | tf_op jit(solution)/shard_map/stack | solution.py:269
  29.5 0.0 copy-done.2
  29.5 1.5 %copy.11.down_ref = bf16[8,294,294]{2,1,0:T(8,128)(2,1)} copy(bf16[8,294,294]{2,0,1:T(8,128)(2,1)S(1)} %copy-done.2) | data formatting | bytes 2765952 | tf_op args[7]
  31.0 0.0 copy-done
  31.0 0.0 copy-start.6
  31.0 2.6 %copy.10.far_ref = bf16[16,294,294]{2,1,0:T(8,128)(2,1)} copy(bf16[16,294,294]{2,0,1:T(8,128)(2,1)S(1)} %copy-done) | data formatting | bytes 5531904 | tf_op args[6]
  33.6 2.2 %shard_map.82 = (bf16[256,192]{1,0:T(8,128)(2,1)}, bf16[256,64]{1,0:T(8,128)(2,1)}) custom-call(s32[4]{0:T(128)} %pad_add_fusion.index_ref, s32[16,189]{1,0:T(8,128)} %sources_ref.1, s32[16,189]{1,0:T(8,128)} %classes_ref.1, s32[1,189]{1,0:T(1,128)} %grand_sources_ref.1, s32[1,189]{1,0:T(1,128)} %grand_classes_ref.1), custom_call_target="tpu_custom_call" | custom-call | tf_op jit(solution)/shard_map/pallas_call | solution.py:222
  35.8 0.0 collective-permute-done.6
  35.8 0.0 copy-done.6
  35.8 0.6 %pad_maximum_fusion.2.grand_pool_ref = bf16[64,294]{1,0:T(8,128)(2,1)} fusion(bf16[32,294]{1,0:T(8,128)(2,1)S(1)} %collective-permute-done.6, bf16[16,294]{1,0:T(8,128)(2,1)S(1)} %collective-permute-done.5, bf16[8,294]{1,0:T(8,128)(2,1)S(1)} %collective-permute-done.4, bf16[8,294]{1,0:T(8,128)(2,1)S(1)} %copy-done.6), kind=kLoop, calls=%fused_computation.2 | loop fusion | flops 150528 | bytes 75264 | tf_op jit(solution)/shard_map/concatenate | solution.py:300
  36.4 0.0 collective-permute-done.3.outer_ref
  36.4 0.0 copy-start.4
  36.4 0.0 collective-permute-done.2.inner_ref
  36.4 0.0 copy-start.5
  36.4 0.7 %copy-done.4 = bf16[64,2432]{1,0:T(8,128)(2,1)} copy-done((bf16[64,2432]{1,0:T(8,128)(2,1)}, bf16[64,2432]{1,0:T(8,128)(2,1)S(1)}, u32[]{:S(2)}) %copy-start.4) | copy-done | bytes 311320
  37.1 0.1 copy-done.5
  37.2 6.1 %shard_map.85 = bf16[16,8,294]{2,1,0:T(8,128)(2,1)} custom-call(s32[1]{0:T(128)} %bitcast.index_ref, bf16[256,192]{1,0:T(8,128)(2,1)} %get-tuple-element.7.counts_ref, bf16[256,64]{1,0:T(8,128)(2,1)} %get-tuple-element.8.grand_counts_ref, bf16[64,2432]{1,0:T(8,128)(2,1)} %copy-done.5, bf16[64,2432]{1,0:T(8,128)(2,1)} %pad_maximum_fusion.rows_ref.range_ref, ...), custom_call_target="tpu_custom_call" | custom-call | tf_op jit(solution)/shard_map/pallas_call | solution.py:222
  (1 shorter events, 0.0 us)
Async XLA Ops:
  1.6 8.3 %collective-permute-start = (bf16[16,2432]{1,0:T(8,128)(2,1)}, bf16[16,2432]{1,0:T(8,128)(2,1)S(1)}, u32[]{:S(2)}, u32[]{:S(2)}) collective-permute-start(bf16[16,2432]{1,0:T(8,128)(2,1)} %shard_map.83), channel_id=1, source_target_pairs={{0,2},{1,3},{2,0},{3,1},{4,6},{5,7},{6,4},{7,5},{8,10},{9,11},{10,... | collective-permute-start | bytes 233480 | tf_op jit(solution)/shard_map/ppermute | solution.py:17
  10.8 5.3 %collective-permute-start.1 = (bf16[32,2432]{1,0:T(8,128)(2,1)S(1)}, bf16[32,2432]{1,0:T(8,128)(2,1)S(1)}, u32[]{:S(2)}, u32[]{:S(2)}) collective-permute-start(bf16[32,2432]{1,0:T(8,128)(2,1)S(1)} %pad_maximum_fusion.1), channel_id=1, source_target_pairs={{0,1},{1,0},{2,3},{3,2},{4,5},{5,4},{6,7},{7,6},{8,9},{9,8},{10,11... | collective-permute-start | bytes 466952 | tf_op jit(solution)/shard_map/ppermute | solution.py:17
  11.7 4.4 %copy-start.3 = (bf16[16,2432]{1,0:T(8,128)(2,1)S(1)}, bf16[16,2432]{1,0:T(8,128)(2,1)}, u32[]{:S(2)}) copy-start(bf16[16,2432]{1,0:T(8,128)(2,1)} %shard_map.83) | copy-start | bytes 233476
  14.7 14.8 %copy-start.2 = (bf16[8,294,294]{2,0,1:T(8,128)(2,1)S(1)}, bf16[8,294,294]{2,0,1:T(8,128)(2,1)}, u32[]{:S(2)}) copy-start(bf16[8,294,294]{2,0,1:T(8,128)(2,1)} %param.15) | copy-start | bytes 4148932
  16.9 7.1 %copy-start.1 = (bf16[64,2432]{1,0:T(8,128)(2,1)S(1)}, bf16[64,2432]{1,0:T(8,128)(2,1)}, u32[]{:S(2)}) copy-start(bf16[64,2432]{1,0:T(8,128)(2,1)} %pad_maximum_fusion.rows_ref.range_ref) | copy-start | bytes 933892
  20.2 1.4 %collective-permute-start.4 = (bf16[8,294]{1,0:T(8,128)(2,1)}, bf16[8,294]{1,0:T(8,128)(2,1)S(1)}, u32[]{:S(2)}, u32[]{:S(2)}) collective-permute-start(bf16[8,294]{1,0:T(8,128)(2,1)} %shard_map.84), channel_id=1, source_target_pairs={{0,4},{4,0},{8,12},{12,8},{16,20},{20,16},{24,28},{28,24},{1,5},{5... | collective-permute-start | bytes 14120 | tf_op jit(solution)/shard_map/ppermute | solution.py:17
  22.3 4.1 %collective-permute-start.5 = (bf16[16,294]{1,0:T(8,128)(2,1)S(1)}, bf16[16,294]{1,0:T(8,128)(2,1)S(1)}, u32[]{:S(2)}, u32[]{:S(2)}) collective-permute-start(bf16[16,294]{1,0:T(8,128)(2,1)S(1)} %pad_maximum_fusion.4), channel_id=1, source_target_pairs={{0,8},{4,12},{8,0},{12,4},{16,24},{20,28},{24,16},{28,20},{1,9},{5... | collective-permute-start | bytes 28232 | tf_op jit(solution)/shard_map/ppermute | solution.py:17
  24.0 12.4 %collective-permute-start.3 = (bf16[64,2432]{1,0:T(8,128)(2,1)S(1)}, bf16[64,2432]{1,0:T(8,128)(2,1)S(1)}, u32[]{:S(2)}, u32[]{:S(2)}) collective-permute-start(bf16[64,2432]{1,0:T(8,128)(2,1)S(1)} %copy-done.1), channel_id=1, source_target_pairs={{4,8},{12,16},{20,24},{8,4},{16,12},{24,20},{5,9},{13,17},{21,25},... | collective-permute-start | bytes 933896 | tf_op jit(solution)/shard_map/ppermute | solution.py:266
  24.7 11.7 %collective-permute-start.2 = (bf16[64,2432]{1,0:T(8,128)(2,1)S(1)}, bf16[64,2432]{1,0:T(8,128)(2,1)S(1)}, u32[]{:S(2)}, u32[]{:S(2)}) collective-permute-start(bf16[64,2432]{1,0:T(8,128)(2,1)S(1)} %copy-done.1), channel_id=1, source_target_pairs={{0,4},{4,0},{8,12},{12,8},{16,20},{20,16},{24,28},{28,24},{1,5},{5... | collective-permute-start | bytes 933896 | tf_op jit(solution)/shard_map/ppermute | solution.py:17
  27.1 3.9 %copy-start = (bf16[16,294,294]{2,0,1:T(8,128)(2,1)S(1)}, bf16[16,294,294]{2,0,1:T(8,128)(2,1)}, u32[]{:S(2)}) copy-start(bf16[16,294,294]{2,0,1:T(8,128)(2,1)} %param.14) | copy-start | bytes 8297860
  27.1 8.7 %collective-permute-start.6 = (bf16[32,294]{1,0:T(8,128)(2,1)S(1)}, bf16[32,294]{1,0:T(8,128)(2,1)S(1)}, u32[]{:S(2)}, u32[]{:S(2)}) collective-permute-start(bf16[32,294]{1,0:T(8,128)(2,1)S(1)} %pad_maximum_fusion.3), channel_id=1, source_target_pairs={{0,16},{4,20},{8,24},{12,28},{16,0},{20,4},{24,8},{28,12},{1,17},{... | collective-permute-start | bytes 56456 | tf_op jit(solution)/shard_map/ppermute | solution.py:17
  31.0 4.8 %copy-start.6 = (bf16[8,294]{1,0:T(8,128)(2,1)S(1)}, bf16[8,294]{1,0:T(8,128)(2,1)}, u32[]{:S(2)}) copy-start(bf16[8,294]{1,0:T(8,128)(2,1)} %shard_map.84) | copy-start | bytes 14116
  36.4 0.7 %copy-start.4 = (bf16[64,2432]{1,0:T(8,128)(2,1)}, bf16[64,2432]{1,0:T(8,128)(2,1)S(1)}, u32[]{:S(2)}) copy-start(bf16[64,2432]{1,0:T(8,128)(2,1)S(1)} %collective-permute-done.3.outer_ref) | copy-start | bytes 933892
  36.4 0.8 %copy-start.5 = (bf16[64,2432]{1,0:T(8,128)(2,1)}, bf16[64,2432]{1,0:T(8,128)(2,1)S(1)}, u32[]{:S(2)}) copy-start(bf16[64,2432]{1,0:T(8,128)(2,1)S(1)} %collective-permute-done.2.inner_ref) | copy-start | bytes 933892

commit v3 on v2

--- a/solution.py
+++ b/solution.py
@@ -90,7 +90,7 @@
 
 def counts_kernel(
     rhs_count,
-    index_ref,
+    span,
     sources_ref,
     classes_ref,
     grand_sources_ref,
@@ -103,7 +103,10 @@
     pool_size = counts_ref.shape[1]
     classes_count = counts_ref.shape[0] // own
     range_size = pool_size // 3
-    sub_index, odd, row_pick, grand_index = (index_ref[i] for i in range(4))
+    sub_index, morton_index = lax.axis_index("sub"), lax.axis_index("morton")
+    odd = morton_index % 2
+    row_pick = sub_index // span
+    grand_index = morton_index * grand_sources_ref.shape[0] + row_pick
     for t in range(own):
         sources = sources_ref[t : t + 1, :]
         slot = sources // range_size
@@ -134,12 +137,12 @@
     grand_counts_ref[...] = jnp.where(row_rhs == column_rhs, all_pairs, 0.0).astype(BF16)
 
 
-def grand_kernel(lanes, span, index_ref, rows_ref, up_ref, out_ref, wide, parents):
+def grand_kernel(lanes, span, rows_ref, up_ref, out_ref, wide, parents):
     rhs_count, width = lanes.rhs_count, lanes.width
     range_size = rows_ref.shape[0]
     fan = up_ref.shape[0]
     parent_count = range_size // fan
-    position = index_ref[0]
+    position = lax.axis_index("sub") % span
     fill(wide, rows_ref[...].astype(F32))
     total = jnp.zeros((rhs_count * parent_count, width), F32)
     for k in range(fan):
@@ -159,7 +162,7 @@
 
 def far_kernel(
     lanes,
-    index_ref,
+    span,
     counts_ref,
     grand_counts_ref,
     inner_ref,
@@ -178,7 +181,7 @@
     fan = down_ref.shape[0]
     group = grand_counts_ref.shape[0] // classes_count
     parents_here = own // fan
-    position = index_ref[0]
+    position = lax.axis_index("sub") % span
     grand_aggregate[...] = jnp.dot(
         grand_counts_ref[...], grand_pool_ref[...], preferred_element_type=F32
     ).astype(BF16)
@@ -216,16 +219,18 @@
     return pltpu.VMEM((tiles_of(width), rows, LANES), F32)
 
 
-def call(kernel, outs, scratch, scalars, *operands):
+def call(name, kernel, outs, scratch, *operands):
     whole = pl.BlockSpec(memory_space=pltpu.VMEM)
-    specs = [pl.BlockSpec(memory_space=pltpu.SMEM)] * len(scalars) + [whole] * len(operands)
+    operands = [pltpu.with_memory_space_constraint(x, pltpu.VMEM) for x in operands]
     return pl.pallas_call(
         kernel,
         out_shape=outs,
-        in_specs=specs,
+        in_specs=[whole] * len(operands),
         out_specs=jax.tree.map(lambda _: whole, outs),
         scratch_shapes=scratch,
-    )(*scalars, *operands)
+        compiler_params=pltpu.CompilerParams(vmem_limit_bytes=16 << 20),
+        name=name,
+    )(*operands)
 
 
 def shards(
@@ -235,22 +240,19 @@
     classes_count = far_ops.shape[0]
     fan = up_ops.shape[0]
     sub_count, morton_count = lax.axis_size("sub"), lax.axis_size("morton")
-    sub_index, morton_index = lax.axis_index("sub"), lax.axis_index("morton")
     range_size = own * sub_count
     leaves_of_grand = fan * fan
     grand_span = leaves_of_grand // own
     grands_here = range_size // leaves_of_grand
     grand_count = morton_count * grands_here
-    position = sub_index % grand_span
-    row_pick = sub_index // grand_span
     lanes = Lanes(rhs_count, width)
-    struct = jax.ShapeDtypeStruct
+    struct = pltpu.VMEM
 
     rows = call(
+        "flatten",
         functools.partial(flat_kernel, lanes),
         struct((own, lanes.total), BF16),
         [tiled(own * rhs_count, width)],
-        [],
         leaf_dens,
     )
     blocks = {0: rows}
@@ -266,33 +268,29 @@
     outer_rows = lax.ppermute(range_rows, "morton", outer)
     inner_rows = swapped(range_rows, "morton", 1)
 
-    index = jnp.stack(
-        [sub_index, morton_index % 2, row_pick, morton_index * grands_here + row_pick]
-    ).astype(jnp.int32)
     group = -(-rhs_count // 16) * 16
     counts, grand_counts = call(
-        functools.partial(counts_kernel, rhs_count),
+        "counts",
+        functools.partial(counts_kernel, rhs_count, grand_span),
         (
             struct((classes_count * own, 3 * range_size), BF16),
             struct((classes_count * group, grand_count * rhs_count), BF16),
         ),
         [tiled(classes_count * own, 3 * range_size)],
-        [index],
         leaf_sources,
         leaf_classes,
         grand_sources,
         grand_classes,
     )
 
-    place = position.reshape(1).astype(jnp.int32)
     grand_pool = call(
+        "grands",
         functools.partial(grand_kernel, lanes, grand_span),
         struct((grands_here * rhs_count, width), BF16),
         [
             tiled(range_size, lanes.total),
             tiled(rhs_count * range_size // fan, width),
         ],
-        [place],
         range_rows,
         up_ops,
     )
@@ -300,14 +298,14 @@
         grand_pool = jnp.concatenate([grand_pool, swapped(grand_pool, "morton", mask)], axis=0)
 
     return call(
-        functools.partial(far_kernel, lanes),
-        struct(leaf_dens.shape, BF16),
+        "far",
+        functools.partial(far_kernel, lanes, grand_span),
+        jax.ShapeDtypeStruct(leaf_dens.shape, BF16),
         [
             pltpu.VMEM((classes_count * own, lanes.total), BF16),
             pltpu.VMEM((classes_count * group, width), BF16),
             tiled(own * rhs_count, width),
         ],
-        [place],
         counts,
         grand_counts,
         inner_rows,

time: 43.7 us -> 34.8 us (0.80)
  Pallas kernels: 13.2 us -> 4.96 us
  waiting for transfers between devices: 7.03 us -> 13.8 us
  other arithmetic: 4.33 us -> 0.07 us
  local copies, waits for them, and re-layouts: 7.94 us -> 4.87 us
    pallas_call x4, Pallas kernels: 13.2 us -> 4.96 us  [call(): pl.pallas_call(kernel, out_shape=outs, in_specs=[whole] * len(operands),...]
    ppermute x6, waiting for transfers between devices: 7.03 us -> 13.8 us  [swapped(): return lax.ppermute(value, axis, [(i, i ^ mask) for i in range(count)])]
    unnamed x17, local copies, waits for them, and re-layouts: 7.93 us -> 4.86 us
    concatenate x3, other arithmetic: 2.02 us -> 0.02 us  [shards(): jnp.concatenate([grand_pool, swapped(grand_pool, 'morton', mask)], axis=0)]
    concatenate x1, other arithmetic: 0.9 us -> 0.01 us  [shards(): jnp.concatenate([blocks[p] for p in held], axis=0)]
    concatenate x1, other arithmetic: 0.76 us -> 0.03 us  [shards(): range_rows = jnp.concatenate([blocks[p] for p in range(sub_count)], axis=0)]
    another operation x1 -> x0, other arithmetic: 0.65 us -> none  [shards(): jnp.stack([sub_index, morton_index % 2, row_pick, morton_index * grands_h...]
  transfers between devices with their start and end apart: 7 -> 7, of which waited for: 3 -> 4; matrix products, arithmetic and copies ran while one was open for 21% -> 8% of each run, Pallas kernels for 5% -> 2%
where the time goes in v3:
time: 34.8 us; the launch traced here: 34.6 us
  waiting for transfers between devices  13.8 us (40%)
  starting transfers between devices  10.8 us (31%)
  Pallas kernels  4.96 us (14%)
  local copies, waits for them, and re-layouts  4.87 us (14%)
    ppermute x6, waiting for transfers between devices, swapped(): return lax.ppermute(value, axis, [(i, i ^ mask) for i in range(count)])  13.8 us
    ppermute x6, starting transfers between devices, swapped(): return lax.ppermute(value, axis, [(i, i ^ mask) for i in range(count)])  10.1 us
    pallas_call x4, Pallas kernels, call(): pl.pallas_call(kernel, out_shape=outs, in_specs=[whole] * len(operands),...  4.96 us
    unnamed x17, local copies, waits for them, and re-layouts  4.86 us
  transfers between devices with their start and end apart: 7, of which 4 were waited for; matrix products, arithmetic and copies ran while one was open for 8% of the time, Pallas kernels for 2%

profile of v3, /device:TPU:0, one launch (start us, length us, event | category | flops | bytes accessed | tf_op | source)
XLA Modules:
  0.0 34.6 jit_solution(16734233459776499046)
XLA Ops:
  0.0 0.0 copy-start
  0.0 0.9 %copy-done = bf16[16,8,294]{2,1,0:T(8,128)(2,1)S(1)} copy-done((bf16[16,8,294]{2,1,0:T(8,128)(2,1)S(1)}, bf16[16,8,294]{2,1,0:T(8,128)(2,1)}, u32[]{:S(2)}) %copy-start) | copy-done | bytes 75288
  0.9 0.1 flatten.1
  1.0 4.1 %collective-permute-start = (bf16[16,2432]{1,0:T(8,128)(2,1)S(1)}, bf16[16,2432]{1,0:T(8,128)(2,1)S(1)}, u32[]{:S(2)}, u32[]{:S(2)}) collective-permute-start(bf16[16,2432]{1,0:T(8,128)(2,1)S(1)} %flatten.1), channel_id=1, source_target_pairs={{0,2},{1,3},{2,0},{3,1},{4,6},{5,7},{6,4},{7,5},{8,10},{9,11},{10,... | collective-permute-start | bytes 233480 | tf_op jit(solution)/shard_map/ppermute | solution.py:17
  5.1 4.0 %collective-permute-done = bf16[16,2432]{1,0:T(8,128)(2,1)S(1)} collective-permute-done((bf16[16,2432]{1,0:T(8,128)(2,1)S(1)}, bf16[16,2432]{1,0:T(8,128)(2,1)S(1)}, u32[]{:S(2)}, u32[]{:S(2)}) %collective-permute-start) | collective-permute-done | bytes 77856 | tf_op jit(solution)/shard_map/ppermute | solution.py:17
  9.1 0.8 %collective-permute-start.1 = (bf16[32,2432]{1,0:T(8,128)(2,1)S(1)}, bf16[32,2432]{1,0:T(8,128)(2,1)S(1)}, u32[]{:S(2)}, u32[]{:S(2)}) collective-permute-start(bf16[32,2432]{1,0:T(8,128)(2,1)S(1)} %pad_maximum_fusion.1), channel_id=1, source_target_pairs={{0,1},{1,0},{2,3},{3,2},{4,5},{5,4},{6,7},{7,6},{8,9},{9,8},{10,11... | collective-permute-start | bytes 466952 | tf_op jit(solution)/shard_map/ppermute | solution.py:17
  9.9 1.7 %copy.9.up_ref = bf16[8,294,294]{2,1,0:T(8,128)(2,1)S(1)} copy(bf16[8,294,294]{2,0,1:T(8,128)(2,1)} %param.13) | data formatting | bytes 2765952 | tf_op args[5]
  11.6 0.0 copy-start.6
  11.6 2.8 %collective-permute-done.1 = bf16[32,2432]{1,0:T(8,128)(2,1)S(1)} collective-permute-done((bf16[32,2432]{1,0:T(8,128)(2,1)S(1)}, bf16[32,2432]{1,0:T(8,128)(2,1)S(1)}, u32[]{:S(2)}, u32[]{:S(2)}) %collective-permute-start.1) | collective-permute-done | bytes 155680 | tf_op jit(solution)/shard_map/ppermute | solution.py:17
  14.5 1.1 %grands.1 = bf16[8,294]{1,0:T(8,128)(2,1)S(1)} custom-call(bf16[64,2432]{1,0:T(8,128)(2,1)S(1)} %pad_maximum_fusion.rows_ref.range_ref, bf16[8,294,294]{2,1,0:T(8,128)(2,1)S(1)} %copy.9.up_ref), custom_call_target="tpu_custom_call" | custom-call | tf_op jit(solution)/shard_map/grands/pallas_call | solution.py:225
  15.5 0.0 collective-permute-start.4
  15.5 0.7 %collective-permute-start.3 = (bf16[64,2432]{1,0:T(8,128)(2,1)S(1)}, bf16[64,2432]{1,0:T(8,128)(2,1)S(1)}, u32[]{:S(2)}, u32[]{:S(2)}) collective-permute-start(bf16[64,2432]{1,0:T(8,128)(2,1)S(1)} %pad_maximum_fusion.rows_ref.range_ref), channel_id=1, source_target_pairs={{4,8},{12,16},{20,24},{8,4},{16,12},{24,20},{5,9},{13,17},{21,25},... | collective-permute-start | bytes 933896 | tf_op jit(solution)/shard_map/ppermute | solution.py:268
  16.2 3.1 %collective-permute-start.2 = (bf16[64,2432]{1,0:T(8,128)(2,1)S(1)}, bf16[64,2432]{1,0:T(8,128)(2,1)S(1)}, u32[]{:S(2)}, u32[]{:S(2)}) collective-permute-start(bf16[64,2432]{1,0:T(8,128)(2,1)S(1)} %pad_maximum_fusion.rows_ref.range_ref), channel_id=1, source_target_pairs={{0,4},{4,0},{8,12},{12,8},{16,20},{20,16},{24,28},{28,24},{1,5},{5... | collective-permute-start | bytes 933896 | tf_op jit(solution)/shard_map/ppermute | solution.py:17
  19.3 0.0 collective-permute-done.4
  19.4 1.6 %collective-permute-start.5 = (bf16[16,294]{1,0:T(8,128)(2,1)S(1)}, bf16[16,294]{1,0:T(8,128)(2,1)S(1)}, u32[]{:S(2)}, u32[]{:S(2)}) collective-permute-start(bf16[16,294]{1,0:T(8,128)(2,1)S(1)} %pad_maximum_fusion.4), channel_id=1, source_target_pairs={{0,8},{4,12},{8,0},{12,4},{16,24},{20,28},{24,16},{28,20},{1,9},{5... | collective-permute-start | bytes 28232 | tf_op jit(solution)/shard_map/ppermute | solution.py:17
  20.9 6.7 %collective-permute-done.5 = bf16[16,294]{1,0:T(8,128)(2,1)S(1)} collective-permute-done((bf16[16,294]{1,0:T(8,128)(2,1)S(1)}, bf16[16,294]{1,0:T(8,128)(2,1)S(1)}, u32[]{:S(2)}, u32[]{:S(2)}) %collective-permute-start.5) | collective-permute-done | bytes 9440 | tf_op jit(solution)/shard_map/ppermute | solution.py:17
  27.6 0.0 copy-start.5
  27.6 0.6 %collective-permute-start.6 = (bf16[32,294]{1,0:T(8,128)(2,1)S(1)}, bf16[32,294]{1,0:T(8,128)(2,1)S(1)}, u32[]{:S(2)}, u32[]{:S(2)}) collective-permute-start(bf16[32,294]{1,0:T(8,128)(2,1)S(1)} %pad_maximum_fusion.3), channel_id=1, source_target_pairs={{0,16},{4,20},{8,24},{12,28},{16,0},{20,4},{24,8},{28,12},{1,17},{... | collective-permute-start | bytes 56456 | tf_op jit(solution)/shard_map/ppermute | solution.py:17
  28.2 0.0 copy-done.6
  28.2 0.2 copy.11.down_ref
  28.4 1.2 %copy-done.5 = bf16[16,294,294]{2,0,1:T(8,128)(2,1)S(1)} copy-done((bf16[16,294,294]{2,0,1:T(8,128)(2,1)S(1)}, bf16[16,294,294]{2,0,1:T(8,128)(2,1)}, u32[]{:S(2)}) %copy-start.5) | copy-done | bytes 2765976
  29.6 0.0 copy-start.1
  29.6 0.0 copy-start.2
  29.6 0.0 copy-start.3
  29.6 0.0 copy-start.4
  29.6 0.8 %copy.10.far_ref = bf16[16,294,294]{2,1,0:T(8,128)(2,1)S(1)} copy(bf16[16,294,294]{2,0,1:T(8,128)(2,1)S(1)} %copy-done.5) | data formatting | bytes 5531904 | tf_op args[6]
  30.4 0.0 copy-done.1
  30.4 0.0 copy-done.2
  30.4 0.0 copy-done.3
  30.5 0.0 copy-done.4
  30.5 0.7 %counts.1 = (bf16[256,192]{1,0:T(8,128)(2,1)S(1)}, bf16[256,64]{1,0:T(8,128)(2,1)S(1)}) custom-call(s32[16,189]{1,0:T(8,128)S(1)} %copy-done.1, s32[16,189]{1,0:T(8,128)S(1)} %copy-done.2, s32[1,189]{1,0:T(1,128)S(1)} %copy-done.3, s32[1,189]{1,0:T(1,128)S(1)} %copy-done.4), custom_call_target="tpu_custom_call" | custom-call | tf_op jit(solution)/shard_map/counts/pallas_call | solution.py:225
  31.2 0.3 collective-permute-done.6
  31.5 0.0 collective-permute-done.3.outer_ref
  31.5 0.0 collective-permute-done.2.inner_ref
  31.5 3.1 %far.1 = bf16[16,8,294]{2,1,0:T(8,128)(2,1)} custom-call(bf16[256,192]{1,0:T(8,128)(2,1)S(1)} %get-tuple-element.7.counts_ref, bf16[256,64]{1,0:T(8,128)(2,1)S(1)} %get-tuple-element.8.grand_counts_ref, bf16[64,2432]{1,0:T(8,128)(2,1)S(1)} %collective-permute-done.2.inner_ref, bf16[64,2432]{1,0:T(8,128)(2,1)S(1)} %pad_maximum_fusion.rows_ref.range_ref, ...), custom_call_target="tpu_custom_call" | custom-call | tf_op jit(solution)/shard_map/far/pallas_call | solution.py:225
  (6 shorter events, 0.1 us)
Async XLA Ops:
  0.0 0.9 %copy-start = (bf16[16,8,294]{2,1,0:T(8,128)(2,1)S(1)}, bf16[16,8,294]{2,1,0:T(8,128)(2,1)}, u32[]{:S(2)}) copy-start(bf16[16,8,294]{2,1,0:T(8,128)(2,1)} %dens_ref.1) | copy-start | bytes 225796
  1.0 8.1 %collective-permute-start = (bf16[16,2432]{1,0:T(8,128)(2,1)S(1)}, bf16[16,2432]{1,0:T(8,128)(2,1)S(1)}, u32[]{:S(2)}, u32[]{:S(2)}) collective-permute-start(bf16[16,2432]{1,0:T(8,128)(2,1)S(1)} %flatten.1), channel_id=1, source_target_pairs={{0,2},{1,3},{2,0},{3,1},{4,6},{5,7},{6,4},{7,5},{8,10},{9,11},{10,... | collective-permute-start | bytes 233480 | tf_op jit(solution)/shard_map/ppermute | solution.py:17
  9.1 5.3 %collective-permute-start.1 = (bf16[32,2432]{1,0:T(8,128)(2,1)S(1)}, bf16[32,2432]{1,0:T(8,128)(2,1)S(1)}, u32[]{:S(2)}, u32[]{:S(2)}) collective-permute-start(bf16[32,2432]{1,0:T(8,128)(2,1)S(1)} %pad_maximum_fusion.1), channel_id=1, source_target_pairs={{0,1},{1,0},{2,3},{3,2},{4,5},{5,4},{6,7},{7,6},{8,9},{9,8},{10,11... | collective-permute-start | bytes 466952 | tf_op jit(solution)/shard_map/ppermute | solution.py:17
  11.6 16.5 %copy-start.6 = (bf16[8,294,294]{2,0,1:T(8,128)(2,1)S(1)}, bf16[8,294,294]{2,0,1:T(8,128)(2,1)}, u32[]{:S(2)}) copy-start(bf16[8,294,294]{2,0,1:T(8,128)(2,1)} %param.15) | copy-start | bytes 4148932
  15.5 3.8 %collective-permute-start.4 = (bf16[8,294]{1,0:T(8,128)(2,1)S(1)}, bf16[8,294]{1,0:T(8,128)(2,1)S(1)}, u32[]{:S(2)}, u32[]{:S(2)}) collective-permute-start(bf16[8,294]{1,0:T(8,128)(2,1)S(1)} %grands.1), channel_id=1, source_target_pairs={{0,4},{4,0},{8,12},{12,8},{16,20},{20,16},{24,28},{28,24},{1,5},{5... | collective-permute-start | bytes 14120 | tf_op jit(solution)/shard_map/ppermute | solution.py:17
  15.5 15.9 %collective-permute-start.3 = (bf16[64,2432]{1,0:T(8,128)(2,1)S(1)}, bf16[64,2432]{1,0:T(8,128)(2,1)S(1)}, u32[]{:S(2)}, u32[]{:S(2)}) collective-permute-start(bf16[64,2432]{1,0:T(8,128)(2,1)S(1)} %pad_maximum_fusion.rows_ref.range_ref), channel_id=1, source_target_pairs={{4,8},{12,16},{20,24},{8,4},{16,12},{24,20},{5,9},{13,17},{21,25},... | collective-permute-start | bytes 933896 | tf_op jit(solution)/shard_map/ppermute | solution.py:268
  16.2 15.3 %collective-permute-start.2 = (bf16[64,2432]{1,0:T(8,128)(2,1)S(1)}, bf16[64,2432]{1,0:T(8,128)(2,1)S(1)}, u32[]{:S(2)}, u32[]{:S(2)}) collective-permute-start(bf16[64,2432]{1,0:T(8,128)(2,1)S(1)} %pad_maximum_fusion.rows_ref.range_ref), channel_id=1, source_target_pairs={{0,4},{4,0},{8,12},{12,8},{16,20},{20,16},{24,28},{28,24},{1,5},{5... | collective-permute-start | bytes 933896 | tf_op jit(solution)/shard_map/ppermute | solution.py:17
  19.4 8.2 %collective-permute-start.5 = (bf16[16,294]{1,0:T(8,128)(2,1)S(1)}, bf16[16,294]{1,0:T(8,128)(2,1)S(1)}, u32[]{:S(2)}, u32[]{:S(2)}) collective-permute-start(bf16[16,294]{1,0:T(8,128)(2,1)S(1)} %pad_maximum_fusion.4), channel_id=1, source_target_pairs={{0,8},{4,12},{8,0},{12,4},{16,24},{20,28},{24,16},{28,20},{1,9},{5... | collective-permute-start | bytes 28232 | tf_op jit(solution)/shard_map/ppermute | solution.py:17
  27.6 2.0 %copy-start.5 = (bf16[16,294,294]{2,0,1:T(8,128)(2,1)S(1)}, bf16[16,294,294]{2,0,1:T(8,128)(2,1)}, u32[]{:S(2)}) copy-start(bf16[16,294,294]{2,0,1:T(8,128)(2,1)} %param.14) | copy-start | bytes 8297860
  27.6 3.9 %collective-permute-start.6 = (bf16[32,294]{1,0:T(8,128)(2,1)S(1)}, bf16[32,294]{1,0:T(8,128)(2,1)S(1)}, u32[]{:S(2)}, u32[]{:S(2)}) collective-permute-start(bf16[32,294]{1,0:T(8,128)(2,1)S(1)} %pad_maximum_fusion.3), channel_id=1, source_target_pairs={{0,16},{4,20},{8,24},{12,28},{16,0},{20,4},{24,8},{28,12},{1,17},{... | collective-permute-start | bytes 56456 | tf_op jit(solution)/shard_map/ppermute | solution.py:17
  29.6 0.8 %copy-start.1 = (s32[16,189]{1,0:T(8,128)S(1)}, s32[16,189]{1,0:T(8,128)}, u32[]{:S(2)}) copy-start(s32[16,189]{1,0:T(8,128)} %sources_ref.1) | copy-start | bytes 36292
  29.6 0.8 %copy-start.2 = (s32[16,189]{1,0:T(8,128)S(1)}, s32[16,189]{1,0:T(8,128)}, u32[]{:S(2)}) copy-start(s32[16,189]{1,0:T(8,128)} %classes_ref.1) | copy-start | bytes 36292
  29.6 0.8 %copy-start.3 = (s32[1,189]{1,0:T(1,128)S(1)}, s32[1,189]{1,0:T(1,128)}, u32[]{:S(2)}) copy-start(s32[1,189]{1,0:T(1,128)} %grand_sources_ref.1) | copy-start | bytes 2272
  29.6 0.8 %copy-start.4 = (s32[1,189]{1,0:T(1,128)S(1)}, s32[1,189]{1,0:T(1,128)}, u32[]{:S(2)}) copy-start(s32[1,189]{1,0:T(1,128)} %grand_classes_ref.1) | copy-start | bytes 2272

commit v4 on v3

--- a/solution.py
+++ b/solution.py
@@ -95,6 +95,9 @@
     classes_ref,
     grand_sources_ref,
     grand_classes_ref,
+    _up_ref,
+    _far_ref,
+    _down_ref,
     counts_ref,
     grand_counts_ref,
     wide,
@@ -103,6 +106,7 @@
     pool_size = counts_ref.shape[1]
     classes_count = counts_ref.shape[0] // own
     range_size = pool_size // 3
+    half = range_size // own // 2
     sub_index, morton_index = lax.axis_index("sub"), lax.axis_index("morton")
     odd = morton_index % 2
     row_pick = sub_index // span
@@ -112,7 +116,10 @@
         slot = sources // range_size
         inside = sources - slot * range_size
         slot = jnp.where(odd == 1, slot, 2 - slot)
-        places = slot * range_size + (inside ^ (sub_index * own))
+        inside = inside ^ (sub_index * own)
+        block = inside // own
+        inside += (block % 2 * half + block // 2 - block) * own
+        places = slot * range_size + inside
         counts = class_counts(
             classes_ref[t : t + 1, :], places, classes_count, wide.shape[0] * LANES
         )
@@ -151,10 +158,13 @@
         total += jnp.dot(left.astype(BF16), up_ref[k], preferred_element_type=F32)
     fill(parents, total.astype(BF16).astype(F32))
     per_block = fan // span
+    half = parent_count // per_block // 2
     for grand in range(parent_count // fan):
         total = jnp.zeros((rhs_count, width), F32)
         for child in range(fan):
-            rows = every(parents, grand * fan + child, rhs_count, parent_count, width)
+            block = grand * span + child // per_block
+            held = (block % 2 * half + block // 2) * per_block + child % per_block
+            rows = every(parents, held, rhs_count, parent_count, width)
             operator = ((child // per_block) ^ position) * per_block + child % per_block
             total += jnp.dot(rows.astype(BF16), up_ref[operator], preferred_element_type=F32)
         out_ref[grand * rhs_count : (grand + 1) * rhs_count, :] = total.astype(BF16)
@@ -167,7 +177,8 @@
     grand_counts_ref,
     inner_ref,
     range_ref,
-    outer_ref,
+    outer_even_ref,
+    outer_odd_ref,
     grand_pool_ref,
     far_ref,
     down_ref,
@@ -185,7 +196,8 @@
     grand_aggregate[...] = jnp.dot(
         grand_counts_ref[...], grand_pool_ref[...], preferred_element_type=F32
     ).astype(BF16)
-    pool = jnp.concatenate([inner_ref[...], range_ref[...], outer_ref[...]], axis=0)
+    refs = (inner_ref, range_ref, outer_even_ref, outer_odd_ref)
+    pool = jnp.concatenate([ref[...] for ref in refs], axis=0)
     aggregate[...] = jnp.dot(counts_ref[...], pool, preferred_element_type=F32).astype(BF16)
     total = jnp.zeros((rhs_count * own + group, width), F32)
     for c in range(classes_count):
@@ -219,7 +231,7 @@
     return pltpu.VMEM((tiles_of(width), rows, LANES), F32)
 
 
-def call(name, kernel, outs, scratch, *operands):
+def call(kernel, outs, scratch, *operands):
     whole = pl.BlockSpec(memory_space=pltpu.VMEM)
     operands = [pltpu.with_memory_space_constraint(x, pltpu.VMEM) for x in operands]
     return pl.pallas_call(
@@ -229,7 +241,6 @@
         out_specs=jax.tree.map(lambda _: whole, outs),
         scratch_shapes=scratch,
         compiler_params=pltpu.CompilerParams(vmem_limit_bytes=16 << 20),
-        name=name,
     )(*operands)
 
 
@@ -249,28 +260,28 @@
     struct = pltpu.VMEM
 
     rows = call(
-        "flatten",
         functools.partial(flat_kernel, lanes),
         struct((own, lanes.total), BF16),
         [tiled(own * rhs_count, width)],
         leaf_dens,
     )
-    blocks = {0: rows}
-    for mask in reversed(masks_of(sub_count)):
-        held = sorted(blocks)
-        joined = jnp.concatenate([blocks[p] for p in held], axis=0) if len(held) > 1 else rows
+    held = {0: rows}
+    for mask in reversed(masks_of(sub_count)[1:]):
+        order = sorted(held)
+        joined = jnp.concatenate([held[p] for p in order], axis=0)
         other = swapped(joined, "sub", mask)
-        for at, p in enumerate(held):
-            blocks[p ^ mask] = other[at * own : (at + 1) * own]
-    range_rows = jnp.concatenate([blocks[p] for p in range(sub_count)], axis=0)
-    outer = [(i, i + 1) for i in range(1, morton_count - 1, 2)]
-    outer = outer + [(j, i) for i, j in outer]
-    outer_rows = lax.ppermute(range_rows, "morton", outer)
+        for at, p in enumerate(order):
+            held[p ^ mask] = other[at * own : (at + 1) * own]
+    even_rows = jnp.concatenate([held[p] for p in sorted(held)], axis=0)
+    odd_rows = swapped(even_rows, "sub", 1)
+    pairs = [(i, i + 1) for i in range(1, morton_count - 1, 2)]
+    outer_even = lax.ppermute(even_rows, "morton", pairs + [(j, i) for i, j in pairs])
+    outer_odd = swapped(outer_even, "sub", 1)
+    range_rows = jnp.concatenate([even_rows, odd_rows], axis=0)
     inner_rows = swapped(range_rows, "morton", 1)
 
     group = -(-rhs_count // 16) * 16
     counts, grand_counts = call(
-        "counts",
         functools.partial(counts_kernel, rhs_count, grand_span),
         (
             struct((classes_count * own, 3 * range_size), BF16),
@@ -281,10 +292,12 @@
         leaf_classes,
         grand_sources,
         grand_classes,
+        up_ops,
+        far_ops,
+        down_ops,
     )
 
     grand_pool = call(
-        "grands",
         functools.partial(grand_kernel, lanes, grand_span),
         struct((grands_here * rhs_count, width), BF16),
         [
@@ -295,10 +308,10 @@
         up_ops,
     )
     for mask in masks_of(morton_count):
-        grand_pool = jnp.concatenate([grand_pool, swapped(grand_pool, "morton", mask)], axis=0)
+        other = swapped(grand_pool, "morton", mask)
+        grand_pool = jnp.concatenate([grand_pool, other], axis=0)
 
     return call(
-        "far",
         functools.partial(far_kernel, lanes, grand_span),
         jax.ShapeDtypeStruct(leaf_dens.shape, BF16),
         [
@@ -310,7 +323,8 @@
         grand_counts,
         inner_rows,
         range_rows,
-        outer_rows,
+        outer_even,
+        outer_odd,
         grand_pool,
         far_ops,
         down_ops,

time: 34.8 us -> 28.8 us (0.83)
  waiting for transfers between devices: 13.8 us -> 7.47 us
  starting transfers between devices: 10.8 us -> 11.7 us
  local copies, waits for them, and re-layouts: 4.87 us -> 4.28 us
    ppermute x6 -> x7, waiting for transfers between devices: 13.8 us -> 7.47 us  [swapped(): return lax.ppermute(value, axis, [(i, i ^ mask) for i in range(count)])]
    ppermute x6 -> x7, starting transfers between devices: 10.1 us -> 11 us  [swapped(): return lax.ppermute(value, axis, [(i, i ^ mask) for i in range(count)])]
    unnamed x17, local copies, waits for them, and re-layouts: 4.86 us -> 4.28 us
  transfers between devices with their start and end apart: 7 -> 8, of which waited for: 4 -> 4; matrix products, arithmetic and copies ran while one was open for 8% -> 10% of each run, Pallas kernels for 2% -> 6%
where the time goes in v4:
time: 28.8 us; the launch traced here: 28.6 us
  starting transfers between devices  11.7 us (41%)
  waiting for transfers between devices  7.47 us (26%)
  Pallas kernels  4.98 us (17%)
  local copies, waits for them, and re-layouts  4.28 us (15%)
    ppermute x7, starting transfers between devices, swapped(): return lax.ppermute(value, axis, [(i, i ^ mask) for i in range(count)])  11 us
    ppermute x7, waiting for transfers between devices, swapped(): return lax.ppermute(value, axis, [(i, i ^ mask) for i in range(count)])  7.47 us
    pallas_call x4, Pallas kernels, call(): pl.pallas_call(kernel, out_shape=outs, in_specs=[whole] * len(operands),...  4.98 us
    unnamed x17, local copies, waits for them, and re-layouts  4.28 us
    ppermute x1, starting transfers between devices, shards(): lax.ppermute(even_rows, 'morton', pairs + [(j, i) for i, j in pairs])  0.67 us
  transfers between devices with their start and end apart: 8, of which 4 were waited for; matrix products, arithmetic and copies ran while one was open for 10% of the time, Pallas kernels for 6%

profile of v4, /device:TPU:0, one launch (start us, length us, event | category | flops | bytes accessed | tf_op | source)
XLA Modules:
  0.0 28.6 jit_solution(6545447958320893294)
XLA Ops:
  0.0 0.0 copy-start
  0.0 0.9 %copy-done = bf16[16,8,294]{2,1,0:T(8,128)(2,1)S(1)} copy-done((bf16[16,8,294]{2,1,0:T(8,128)(2,1)S(1)}, bf16[16,8,294]{2,1,0:T(8,128)(2,1)}, u32[]{:S(2)}) %copy-start) | copy-done | bytes 75288
  0.9 0.1 shard_map.83
  1.0 4.1 %collective-permute-start = (bf16[16,2432]{1,0:T(8,128)(2,1)S(1)}, bf16[16,2432]{1,0:T(8,128)(2,1)S(1)}, u32[]{:S(2)}, u32[]{:S(2)}) collective-permute-start(bf16[16,2432]{1,0:T(8,128)(2,1)S(1)} %shard_map.83), channel_id=1, source_target_pairs={{0,2},{1,3},{2,0},{3,1},{4,6},{5,7},{6,4},{7,5},{8,10},{9,11},{10,... | collective-permute-start | bytes 233480 | tf_op jit(solution)/shard_map/ppermute | solution.py:17
  5.1 4.0 %collective-permute-done = bf16[16,2432]{1,0:T(8,128)(2,1)S(1)} collective-permute-done((bf16[16,2432]{1,0:T(8,128)(2,1)S(1)}, bf16[16,2432]{1,0:T(8,128)(2,1)S(1)}, u32[]{:S(2)}, u32[]{:S(2)}) %collective-permute-start) | collective-permute-done | bytes 77856 | tf_op jit(solution)/shard_map/ppermute | solution.py:17
  9.1 0.8 %collective-permute-start.1 = (bf16[32,2432]{1,0:T(8,128)(2,1)S(1)}, bf16[32,2432]{1,0:T(8,128)(2,1)S(1)}, u32[]{:S(2)}, u32[]{:S(2)}) collective-permute-start(bf16[32,2432]{1,0:T(8,128)(2,1)S(1)} %pad_maximum_fusion.1), channel_id=1, source_target_pairs={{0,1},{1,0},{2,3},{3,2},{4,5},{5,4},{6,7},{7,6},{8,9},{9,8},{10,11... | collective-permute-start | bytes 466952 | tf_op jit(solution)/shard_map/ppermute | solution.py:17
  9.9 0.0 copy-start.5
  9.9 1.9 %copy.9._up_ref.up_ref = bf16[8,294,294]{2,1,0:T(8,128)(2,1)S(1)} copy(bf16[8,294,294]{2,0,1:T(8,128)(2,1)} %param.13) | data formatting | bytes 2765952 | tf_op args[5]
  11.8 0.7 %collective-permute-start.3 = (bf16[32,2432]{1,0:T(8,128)(2,1)S(1)}, bf16[32,2432]{1,0:T(8,128)(2,1)S(1)}, u32[]{:S(2)}, u32[]{:S(2)}) collective-permute-start(bf16[32,2432]{1,0:T(8,128)(2,1)S(1)} %pad_maximum_fusion.1), channel_id=1, source_target_pairs={{4,8},{12,16},{20,24},{8,4},{16,12},{24,20},{5,9},{13,17},{21,25},... | collective-permute-start | bytes 466952 | tf_op jit(solution)/shard_map/ppermute | solution.py:278
  12.5 2.0 %collective-permute-done.1 = bf16[32,2432]{1,0:T(8,128)(2,1)S(1)} collective-permute-done((bf16[32,2432]{1,0:T(8,128)(2,1)S(1)}, bf16[32,2432]{1,0:T(8,128)(2,1)S(1)}, u32[]{:S(2)}, u32[]{:S(2)}) %collective-permute-start.1) | collective-permute-done | bytes 155680 | tf_op jit(solution)/shard_map/ppermute | solution.py:17
  14.5 1.1 %shard_map.84 = bf16[8,294]{1,0:T(8,128)(2,1)S(1)} custom-call(bf16[64,2432]{1,0:T(8,128)(2,1)S(1)} %pad_maximum_fusion.rows_ref.range_ref, bf16[8,294,294]{2,1,0:T(8,128)(2,1)S(1)} %copy.9._up_ref.up_ref), custom_call_target="tpu_custom_call" | custom-call | tf_op jit(solution)/shard_map/pallas_call | solution.py:237
  15.5 0.9 %collective-permute-start.5 = (bf16[8,294]{1,0:T(8,128)(2,1)S(1)}, bf16[8,294]{1,0:T(8,128)(2,1)S(1)}, u32[]{:S(2)}, u32[]{:S(2)}) collective-permute-start(bf16[8,294]{1,0:T(8,128)(2,1)S(1)} %shard_map.84), channel_id=1, source_target_pairs={{0,4},{4,0},{8,12},{12,8},{16,20},{20,16},{24,28},{28,24},{1,5},{5... | collective-permute-start | bytes 14120 | tf_op jit(solution)/shard_map/ppermute | solution.py:17
  16.4 0.0 collective-permute-start.2
  16.5 0.8 %collective-permute-done.5 = bf16[8,294]{1,0:T(8,128)(2,1)S(1)} collective-permute-done((bf16[8,294]{1,0:T(8,128)(2,1)S(1)}, bf16[8,294]{1,0:T(8,128)(2,1)S(1)}, u32[]{:S(2)}, u32[]{:S(2)}) %collective-permute-start.5) | collective-permute-done | bytes 4736 | tf_op jit(solution)/shard_map/ppermute | solution.py:17
  17.3 1.5 %collective-permute-start.6 = (bf16[16,294]{1,0:T(8,128)(2,1)S(1)}, bf16[16,294]{1,0:T(8,128)(2,1)S(1)}, u32[]{:S(2)}, u32[]{:S(2)}) collective-permute-start(bf16[16,294]{1,0:T(8,128)(2,1)S(1)} %pad_maximum_fusion.4), channel_id=1, source_target_pairs={{0,8},{4,12},{8,0},{12,4},{16,24},{20,28},{24,16},{28,20},{1,9},{5... | collective-permute-start | bytes 28232 | tf_op jit(solution)/shard_map/ppermute | solution.py:17
  18.8 0.0 collective-permute-done.3.outer_even_ref
  18.8 1.5 %collective-permute-start.4 = (bf16[32,2432]{1,0:T(8,128)(2,1)S(1)}, bf16[32,2432]{1,0:T(8,128)(2,1)S(1)}, u32[]{:S(2)}, u32[]{:S(2)}) collective-permute-start(bf16[32,2432]{1,0:T(8,128)(2,1)S(1)} %collective-permute-done.3.outer_even_ref), channel_id=1, source_target_pairs={{0,1},{1,0},{2,3},{3,2},{4,5},{5,4},{6,7},{7,6},{8,9},{9,8},{10,11... | collective-permute-start | bytes 466952 | tf_op jit(solution)/shard_map/ppermute | solution.py:17
  20.3 0.7 %collective-permute-done.6 = bf16[16,294]{1,0:T(8,128)(2,1)S(1)} collective-permute-done((bf16[16,294]{1,0:T(8,128)(2,1)S(1)}, bf16[16,294]{1,0:T(8,128)(2,1)S(1)}, u32[]{:S(2)}, u32[]{:S(2)}) %collective-permute-start.6) | collective-permute-done | bytes 9440 | tf_op jit(solution)/shard_map/ppermute | solution.py:17
  21.0 0.0 copy-start.6
  21.0 2.2 %collective-permute-start.7 = (bf16[32,294]{1,0:T(8,128)(2,1)S(1)}, bf16[32,294]{1,0:T(8,128)(2,1)S(1)}, u32[]{:S(2)}, u32[]{:S(2)}) collective-permute-start(bf16[32,294]{1,0:T(8,128)(2,1)S(1)} %pad_maximum_fusion.3), channel_id=1, source_target_pairs={{0,16},{4,20},{8,24},{12,28},{16,0},{20,4},{24,8},{28,12},{1,17},{... | collective-permute-start | bytes 56456 | tf_op jit(solution)/shard_map/ppermute | solution.py:17
  23.1 0.0 copy-done.5
  23.1 0.8 %copy.10._far_ref.far_ref = bf16[16,294,294]{2,1,0:T(8,128)(2,1)S(1)} copy(bf16[16,294,294]{2,0,1:T(8,128)(2,1)S(1)} %copy-done.5) | data formatting | bytes 5531904 | tf_op args[6]
  24.0 0.0 copy-done.6
  24.0 0.0 copy-start.1
  24.0 0.0 copy-start.2
  24.0 0.0 copy-start.3
  24.0 0.0 copy-start.4
  24.0 0.2 copy.11._down_ref.down_ref
  24.3 0.4 %copy-done.1 = s32[16,189]{1,0:T(8,128)S(1)} copy-done((s32[16,189]{1,0:T(8,128)S(1)}, s32[16,189]{1,0:T(8,128)}, u32[]{:S(2)}) %copy-start.1) | copy-done | bytes 12120
  24.7 0.0 copy-done.2
  24.7 0.0 copy-done.3
  24.7 0.0 copy-done.4
  24.7 0.8 %shard_map.82 = (bf16[256,192]{1,0:T(8,128)(2,1)S(1)}, bf16[256,64]{1,0:T(8,128)(2,1)S(1)}) custom-call(s32[16,189]{1,0:T(8,128)S(1)} %copy-done.1, s32[16,189]{1,0:T(8,128)S(1)} %copy-done.2, s32[1,189]{1,0:T(1,128)S(1)} %copy-done.3, s32[1,189]{1,0:T(1,128)S(1)} %copy-done.4, bf16[8,294,294]{2,1,0:T(8,128)(2,1)S(1)} %copy.9._up_ref.up_ref, ...), custom_call_target="tpu_custom_call" | custom-call | tf_op jit(solution)/shard_map/pallas_call | solution.py:237
  25.5 0.0 collective-permute-done.7
  25.5 0.0 collective-permute-done.4.outer_odd_ref
  25.5 0.0 collective-permute-done.2.inner_ref
  25.5 3.1 %shard_map.85 = bf16[16,8,294]{2,1,0:T(8,128)(2,1)} custom-call(bf16[256,192]{1,0:T(8,128)(2,1)S(1)} %get-tuple-element.7.counts_ref, bf16[256,64]{1,0:T(8,128)(2,1)S(1)} %get-tuple-element.8.grand_counts_ref, bf16[64,2432]{1,0:T(8,128)(2,1)S(1)} %collective-permute-done.2.inner_ref, bf16[64,2432]{1,0:T(8,128)(2,1)S(1)} %pad_maximum_fusion.rows_ref.range_ref, ...), custom_call_target="tpu_custom_call" | custom-call | tf_op jit(solution)/shard_map/pallas_call | solution.py:237
  (5 shorter events, 0.1 us)
Async XLA Ops:
  0.0 0.9 %copy-start = (bf16[16,8,294]{2,1,0:T(8,128)(2,1)S(1)}, bf16[16,8,294]{2,1,0:T(8,128)(2,1)}, u32[]{:S(2)}) copy-start(bf16[16,8,294]{2,1,0:T(8,128)(2,1)} %dens_ref.1) | copy-start | bytes 225796
  1.0 8.1 %collective-permute-start = (bf16[16,2432]{1,0:T(8,128)(2,1)S(1)}, bf16[16,2432]{1,0:T(8,128)(2,1)S(1)}, u32[]{:S(2)}, u32[]{:S(2)}) collective-permute-start(bf16[16,2432]{1,0:T(8,128)(2,1)S(1)} %shard_map.83), channel_id=1, source_target_pairs={{0,2},{1,3},{2,0},{3,1},{4,6},{5,7},{6,4},{7,5},{8,10},{9,11},{10,... | collective-permute-start | bytes 233480 | tf_op jit(solution)/shard_map/ppermute | solution.py:17
  9.1 5.3 %collective-permute-start.1 = (bf16[32,2432]{1,0:T(8,128)(2,1)S(1)}, bf16[32,2432]{1,0:T(8,128)(2,1)S(1)}, u32[]{:S(2)}, u32[]{:S(2)}) collective-permute-start(bf16[32,2432]{1,0:T(8,128)(2,1)S(1)} %pad_maximum_fusion.1), channel_id=1, source_target_pairs={{0,1},{1,0},{2,3},{3,2},{4,5},{5,4},{6,7},{7,6},{8,9},{9,8},{10,11... | collective-permute-start | bytes 466952 | tf_op jit(solution)/shard_map/ppermute | solution.py:17
  9.9 13.2 %copy-start.5 = (bf16[16,294,294]{2,0,1:T(8,128)(2,1)S(1)}, bf16[16,294,294]{2,0,1:T(8,128)(2,1)}, u32[]{:S(2)}) copy-start(bf16[16,294,294]{2,0,1:T(8,128)(2,1)} %param.14) | copy-start | bytes 8297860
  11.8 7.0 %collective-permute-start.3 = (bf16[32,2432]{1,0:T(8,128)(2,1)S(1)}, bf16[32,2432]{1,0:T(8,128)(2,1)S(1)}, u32[]{:S(2)}, u32[]{:S(2)}) collective-permute-start(bf16[32,2432]{1,0:T(8,128)(2,1)S(1)} %pad_maximum_fusion.1), channel_id=1, source_target_pairs={{4,8},{12,16},{20,24},{8,4},{16,12},{24,20},{5,9},{13,17},{21,25},... | collective-permute-start | bytes 466952 | tf_op jit(solution)/shard_map/ppermute | solution.py:278
  15.5 1.7 %collective-permute-start.5 = (bf16[8,294]{1,0:T(8,128)(2,1)S(1)}, bf16[8,294]{1,0:T(8,128)(2,1)S(1)}, u32[]{:S(2)}, u32[]{:S(2)}) collective-permute-start(bf16[8,294]{1,0:T(8,128)(2,1)S(1)} %shard_map.84), channel_id=1, source_target_pairs={{0,4},{4,0},{8,12},{12,8},{16,20},{20,16},{24,28},{28,24},{1,5},{5... | collective-permute-start | bytes 14120 | tf_op jit(solution)/shard_map/ppermute | solution.py:17
  16.4 9.1 %collective-permute-start.2 = (bf16[64,2432]{1,0:T(8,128)(2,1)S(1)}, bf16[64,2432]{1,0:T(8,128)(2,1)S(1)}, u32[]{:S(2)}, u32[]{:S(2)}) collective-permute-start(bf16[64,2432]{1,0:T(8,128)(2,1)S(1)} %pad_maximum_fusion.rows_ref.range_ref), channel_id=1, source_target_pairs={{0,4},{4,0},{8,12},{12,8},{16,20},{20,16},{24,28},{28,24},{1,5},{5... | collective-permute-start | bytes 933896 | tf_op jit(solution)/shard_map/ppermute | solution.py:17
  17.3 3.7 %collective-permute-start.6 = (bf16[16,294]{1,0:T(8,128)(2,1)S(1)}, bf16[16,294]{1,0:T(8,128)(2,1)S(1)}, u32[]{:S(2)}, u32[]{:S(2)}) collective-permute-start(bf16[16,294]{1,0:T(8,128)(2,1)S(1)} %pad_maximum_fusion.4), channel_id=1, source_target_pairs={{0,8},{4,12},{8,0},{12,4},{16,24},{20,28},{24,16},{28,20},{1,9},{5... | collective-permute-start | bytes 28232 | tf_op jit(solution)/shard_map/ppermute | solution.py:17
  18.8 6.8 %collective-permute-start.4 = (bf16[32,2432]{1,0:T(8,128)(2,1)S(1)}, bf16[32,2432]{1,0:T(8,128)(2,1)S(1)}, u32[]{:S(2)}, u32[]{:S(2)}) collective-permute-start(bf16[32,2432]{1,0:T(8,128)(2,1)S(1)} %collective-permute-done.3.outer_even_ref), channel_id=1, source_target_pairs={{0,1},{1,0},{2,3},{3,2},{4,5},{5,4},{6,7},{7,6},{8,9},{9,8},{10,11... | collective-permute-start | bytes 466952 | tf_op jit(solution)/shard_map/ppermute | solution.py:17
  21.0 3.0 %copy-start.6 = (bf16[8,294,294]{2,0,1:T(8,128)(2,1)S(1)}, bf16[8,294,294]{2,0,1:T(8,128)(2,1)}, u32[]{:S(2)}) copy-start(bf16[8,294,294]{2,0,1:T(8,128)(2,1)} %param.15) | copy-start | bytes 4148932
  21.0 4.5 %collective-permute-start.7 = (bf16[32,294]{1,0:T(8,128)(2,1)S(1)}, bf16[32,294]{1,0:T(8,128)(2,1)S(1)}, u32[]{:S(2)}, u32[]{:S(2)}) collective-permute-start(bf16[32,294]{1,0:T(8,128)(2,1)S(1)} %pad_maximum_fusion.3), channel_id=1, source_target_pairs={{0,16},{4,20},{8,24},{12,28},{16,0},{20,4},{24,8},{28,12},{1,17},{... | collective-permute-start | bytes 56456 | tf_op jit(solution)/shard_map/ppermute | solution.py:17
  24.0 0.7 %copy-start.1 = (s32[16,189]{1,0:T(8,128)S(1)}, s32[16,189]{1,0:T(8,128)}, u32[]{:S(2)}) copy-start(s32[16,189]{1,0:T(8,128)} %sources_ref.1) | copy-start | bytes 36292
  24.0 0.7 %copy-start.2 = (s32[16,189]{1,0:T(8,128)S(1)}, s32[16,189]{1,0:T(8,128)}, u32[]{:S(2)}) copy-start(s32[16,189]{1,0:T(8,128)} %classes_ref.1) | copy-start | bytes 36292
  24.0 0.7 %copy-start.3 = (s32[1,189]{1,0:T(1,128)S(1)}, s32[1,189]{1,0:T(1,128)}, u32[]{:S(2)}) copy-start(s32[1,189]{1,0:T(1,128)} %grand_sources_ref.1) | copy-start | bytes 2272
  24.0 0.7 %copy-start.4 = (s32[1,189]{1,0:T(1,128)S(1)}, s32[1,189]{1,0:T(1,128)}, u32[]{:S(2)}) copy-start(s32[1,189]{1,0:T(1,128)} %grand_classes_ref.1) | copy-start | bytes 2272

commit v5 on v4

--- a/solution.py
+++ b/solution.py
@@ -96,8 +96,6 @@
     grand_sources_ref,
     grand_classes_ref,
     _up_ref,
-    _far_ref,
-    _down_ref,
     counts_ref,
     grand_counts_ref,
     wide,
@@ -182,6 +180,7 @@
     grand_pool_ref,
     far_ref,
     down_ref,
+    _ready_ref,
     out_ref,
     aggregate,
     grand_aggregate,
@@ -227,6 +226,10 @@
             out_ref[leaf] = local.astype(BF16)
 
 
+def ready_kernel(_far_ref, _down_ref, out_ref):
+    out_ref[...] = jnp.zeros(out_ref.shape, F32)
+
+
 def tiled(rows, width):
     return pltpu.VMEM((tiles_of(width), rows, LANES), F32)
 
@@ -293,9 +296,8 @@
         grand_sources,
         grand_classes,
         up_ops,
-        far_ops,
-        down_ops,
-    )
+    )
+    ready = call(ready_kernel, struct((8, LANES), F32), [], far_ops, down_ops)
 
     grand_pool = call(
         functools.partial(grand_kernel, lanes, grand_span),
@@ -328,6 +330,7 @@
         grand_pool,
         far_ops,
         down_ops,
+        ready,
     )
 
 

time: 28.8 us -> 29.1 us (1.010)
    pallas_call x4 -> x5, Pallas kernels: 4.98 us -> 4.98 us  [call(): pl.pallas_call(kernel, out_shape=outs, in_specs=[whole] * len(operands),...]
where the time goes in v5:
time: 29.1 us; the launch traced here: 28.8 us
  starting transfers between devices  11.8 us (41%)
  waiting for transfers between devices  7.48 us (26%)
  Pallas kernels  4.98 us (17%)
  local copies, waits for them, and re-layouts  4.36 us (15%)
    ppermute x7, starting transfers between devices, swapped(): return lax.ppermute(value, axis, [(i, i ^ mask) for i in range(count)])  11 us
    ppermute x7, waiting for transfers between devices, swapped(): return lax.ppermute(value, axis, [(i, i ^ mask) for i in range(count)])  7.48 us
    pallas_call x5, Pallas kernels, call(): pl.pallas_call(kernel, out_shape=outs, in_specs=[whole] * len(operands),...  4.98 us
    unnamed x17, local copies, waits for them, and re-layouts  4.36 us
    ppermute x1, starting transfers between devices, shards(): lax.ppermute(even_rows, 'morton', pairs + [(j, i) for i, j in pairs])  0.8 us
  transfers between devices with their start and end apart: 8, of which 4 were waited for; matrix products, arithmetic and copies ran while one was open for 10% of the time, Pallas kernels for 6%

profile of v5, /device:TPU:0, one launch (start us, length us, event | category | flops | bytes accessed | tf_op | source)
XLA Modules:
  0.0 28.8 jit_solution(1116932551921193312)
XLA Ops:
  0.0 0.0 copy-start
  0.0 0.9 %copy-done = bf16[16,8,294]{2,1,0:T(8,128)(2,1)S(1)} copy-done((bf16[16,8,294]{2,1,0:T(8,128)(2,1)S(1)}, bf16[16,8,294]{2,1,0:T(8,128)(2,1)}, u32[]{:S(2)}) %copy-start) | copy-done | bytes 75288
  0.9 0.1 shard_map.83
  1.0 4.1 %collective-permute-start = (bf16[16,2432]{1,0:T(8,128)(2,1)S(1)}, bf16[16,2432]{1,0:T(8,128)(2,1)S(1)}, u32[]{:S(2)}, u32[]{:S(2)}) collective-permute-start(bf16[16,2432]{1,0:T(8,128)(2,1)S(1)} %shard_map.83), channel_id=1, source_target_pairs={{0,2},{1,3},{2,0},{3,1},{4,6},{5,7},{6,4},{7,5},{8,10},{9,11},{10,... | collective-permute-start | bytes 233480 | tf_op jit(solution)/shard_map/ppermute | solution.py:17
  5.1 4.0 %collective-permute-done = bf16[16,2432]{1,0:T(8,128)(2,1)S(1)} collective-permute-done((bf16[16,2432]{1,0:T(8,128)(2,1)S(1)}, bf16[16,2432]{1,0:T(8,128)(2,1)S(1)}, u32[]{:S(2)}, u32[]{:S(2)}) %collective-permute-start) | collective-permute-done | bytes 77856 | tf_op jit(solution)/shard_map/ppermute | solution.py:17
  9.1 0.8 %collective-permute-start.1 = (bf16[32,2432]{1,0:T(8,128)(2,1)S(1)}, bf16[32,2432]{1,0:T(8,128)(2,1)S(1)}, u32[]{:S(2)}, u32[]{:S(2)}) collective-permute-start(bf16[32,2432]{1,0:T(8,128)(2,1)S(1)} %pad_maximum_fusion.1), channel_id=1, source_target_pairs={{0,1},{1,0},{2,3},{3,2},{4,5},{5,4},{6,7},{7,6},{8,9},{9,8},{10,11... | collective-permute-start | bytes 466952 | tf_op jit(solution)/shard_map/ppermute | solution.py:17
  9.9 1.7 %copy.9._up_ref.up_ref = bf16[8,294,294]{2,1,0:T(8,128)(2,1)S(1)} copy(bf16[8,294,294]{2,0,1:T(8,128)(2,1)} %param.13) | data formatting | bytes 2765952 | tf_op args[5]
  11.6 0.0 copy-start.6
  11.6 0.8 %collective-permute-start.3 = (bf16[32,2432]{1,0:T(8,128)(2,1)S(1)}, bf16[32,2432]{1,0:T(8,128)(2,1)S(1)}, u32[]{:S(2)}, u32[]{:S(2)}) collective-permute-start(bf16[32,2432]{1,0:T(8,128)(2,1)S(1)} %pad_maximum_fusion.1), channel_id=1, source_target_pairs={{4,8},{12,16},{20,24},{8,4},{16,12},{24,20},{5,9},{13,17},{21,25},... | collective-permute-start | bytes 466952 | tf_op jit(solution)/shard_map/ppermute | solution.py:281
  12.5 2.0 %collective-permute-done.1 = bf16[32,2432]{1,0:T(8,128)(2,1)S(1)} collective-permute-done((bf16[32,2432]{1,0:T(8,128)(2,1)S(1)}, bf16[32,2432]{1,0:T(8,128)(2,1)S(1)}, u32[]{:S(2)}, u32[]{:S(2)}) %collective-permute-start.1) | collective-permute-done | bytes 155680 | tf_op jit(solution)/shard_map/ppermute | solution.py:17
  14.5 1.1 %shard_map.84 = bf16[8,294]{1,0:T(8,128)(2,1)S(1)} custom-call(bf16[64,2432]{1,0:T(8,128)(2,1)S(1)} %pad_maximum_fusion.rows_ref.range_ref, bf16[8,294,294]{2,1,0:T(8,128)(2,1)S(1)} %copy.9._up_ref.up_ref), custom_call_target="tpu_custom_call" | custom-call | tf_op jit(solution)/shard_map/pallas_call | solution.py:240
  15.5 0.9 %collective-permute-start.5 = (bf16[8,294]{1,0:T(8,128)(2,1)S(1)}, bf16[8,294]{1,0:T(8,128)(2,1)S(1)}, u32[]{:S(2)}, u32[]{:S(2)}) collective-permute-start(bf16[8,294]{1,0:T(8,128)(2,1)S(1)} %shard_map.84), channel_id=1, source_target_pairs={{0,4},{4,0},{8,12},{12,8},{16,20},{20,16},{24,28},{28,24},{1,5},{5... | collective-permute-start | bytes 14120 | tf_op jit(solution)/shard_map/ppermute | solution.py:17
  16.4 0.0 collective-permute-start.2
  16.5 0.8 %collective-permute-done.5 = bf16[8,294]{1,0:T(8,128)(2,1)S(1)} collective-permute-done((bf16[8,294]{1,0:T(8,128)(2,1)S(1)}, bf16[8,294]{1,0:T(8,128)(2,1)S(1)}, u32[]{:S(2)}, u32[]{:S(2)}) %collective-permute-start.5) | collective-permute-done | bytes 4736 | tf_op jit(solution)/shard_map/ppermute | solution.py:17
  17.2 1.5 %collective-permute-start.6 = (bf16[16,294]{1,0:T(8,128)(2,1)S(1)}, bf16[16,294]{1,0:T(8,128)(2,1)S(1)}, u32[]{:S(2)}, u32[]{:S(2)}) collective-permute-start(bf16[16,294]{1,0:T(8,128)(2,1)S(1)} %pad_maximum_fusion.4), channel_id=1, source_target_pairs={{0,8},{4,12},{8,0},{12,4},{16,24},{20,28},{24,16},{28,20},{1,9},{5... | collective-permute-start | bytes 28232 | tf_op jit(solution)/shard_map/ppermute | solution.py:17
  18.7 0.0 collective-permute-done.3.outer_even_ref
  18.7 1.5 %collective-permute-start.4 = (bf16[32,2432]{1,0:T(8,128)(2,1)S(1)}, bf16[32,2432]{1,0:T(8,128)(2,1)S(1)}, u32[]{:S(2)}, u32[]{:S(2)}) collective-permute-start(bf16[32,2432]{1,0:T(8,128)(2,1)S(1)} %collective-permute-done.3.outer_even_ref), channel_id=1, source_target_pairs={{0,1},{1,0},{2,3},{3,2},{4,5},{5,4},{6,7},{7,6},{8,9},{9,8},{10,11... | collective-permute-start | bytes 466952 | tf_op jit(solution)/shard_map/ppermute | solution.py:17
  20.3 0.7 %collective-permute-done.6 = bf16[16,294]{1,0:T(8,128)(2,1)S(1)} collective-permute-done((bf16[16,294]{1,0:T(8,128)(2,1)S(1)}, bf16[16,294]{1,0:T(8,128)(2,1)S(1)}, u32[]{:S(2)}, u32[]{:S(2)}) %collective-permute-start.6) | collective-permute-done | bytes 9440 | tf_op jit(solution)/shard_map/ppermute | solution.py:17
  20.9 0.0 copy-start.5
  21.0 2.2 %collective-permute-start.7 = (bf16[32,294]{1,0:T(8,128)(2,1)S(1)}, bf16[32,294]{1,0:T(8,128)(2,1)S(1)}, u32[]{:S(2)}, u32[]{:S(2)}) collective-permute-start(bf16[32,294]{1,0:T(8,128)(2,1)S(1)} %pad_maximum_fusion.3), channel_id=1, source_target_pairs={{0,16},{4,20},{8,24},{12,28},{16,0},{20,4},{24,8},{28,12},{1,17},{... | collective-permute-start | bytes 56456 | tf_op jit(solution)/shard_map/ppermute | solution.py:17
  23.1 0.0 copy-done.6
  23.1 0.2 copy.14._down_ref.down_ref
  23.4 0.0 copy-done.5
  23.4 0.8 %copy.13._far_ref.far_ref = bf16[16,294,294]{2,1,0:T(8,128)(2,1)S(1)} copy(bf16[16,294,294]{2,0,1:T(8,128)(2,1)S(1)} %copy-done.5) | data formatting | bytes 5531904 | tf_op args[6]
  24.2 0.0 copy-start.1
  24.2 0.0 copy-start.2
  24.2 0.0 copy-start.3
  24.2 0.0 copy-start.4
  24.3 0.7 %copy-done.1 = s32[16,189]{1,0:T(8,128)S(1)} copy-done((s32[16,189]{1,0:T(8,128)S(1)}, s32[16,189]{1,0:T(8,128)}, u32[]{:S(2)}) %copy-start.1) | copy-done | bytes 12120
  24.9 0.0 copy-done.2
  24.9 0.0 copy-done.3
  24.9 0.0 copy-done.4
  24.9 0.8 %shard_map.82 = (bf16[256,192]{1,0:T(8,128)(2,1)S(1)}, bf16[256,64]{1,0:T(8,128)(2,1)S(1)}) custom-call(s32[16,189]{1,0:T(8,128)S(1)} %copy-done.1, s32[16,189]{1,0:T(8,128)S(1)} %copy-done.2, s32[1,189]{1,0:T(1,128)S(1)} %copy-done.3, s32[1,189]{1,0:T(1,128)S(1)} %copy-done.4, bf16[8,294,294]{2,1,0:T(8,128)(2,1)S(1)} %copy.9._up_ref.up_ref), custom_call_target="tpu_custom_call" | custom-call | tf_op jit(solution)/shard_map/pallas_call | solution.py:240
  25.7 0.0 collective-permute-done.7
  25.7 0.0 collective-permute-done.4.outer_odd_ref
  25.7 0.0 collective-permute-done.2.inner_ref
  25.8 3.1 %shard_map.86 = bf16[16,8,294]{2,1,0:T(8,128)(2,1)} custom-call(bf16[256,192]{1,0:T(8,128)(2,1)S(1)} %get-tuple-element.7.counts_ref, bf16[256,64]{1,0:T(8,128)(2,1)S(1)} %get-tuple-element.8.grand_counts_ref, bf16[64,2432]{1,0:T(8,128)(2,1)S(1)} %collective-permute-done.2.inner_ref, bf16[64,2432]{1,0:T(8,128)(2,1)S(1)} %pad_maximum_fusion.rows_ref.range_ref, ...), custom_call_target="tpu_custom_call" | custom-call | tf_op jit(solution)/shard_map/pallas_call | solution.py:240
  (6 shorter events, 0.1 us)
Async XLA Ops:
  0.0 0.9 %copy-start = (bf16[16,8,294]{2,1,0:T(8,128)(2,1)S(1)}, bf16[16,8,294]{2,1,0:T(8,128)(2,1)}, u32[]{:S(2)}) copy-start(bf16[16,8,294]{2,1,0:T(8,128)(2,1)} %dens_ref.1) | copy-start | bytes 225796
  1.0 8.1 %collective-permute-start = (bf16[16,2432]{1,0:T(8,128)(2,1)S(1)}, bf16[16,2432]{1,0:T(8,128)(2,1)S(1)}, u32[]{:S(2)}, u32[]{:S(2)}) collective-permute-start(bf16[16,2432]{1,0:T(8,128)(2,1)S(1)} %shard_map.83), channel_id=1, source_target_pairs={{0,2},{1,3},{2,0},{3,1},{4,6},{5,7},{6,4},{7,5},{8,10},{9,11},{10,... | collective-permute-start | bytes 233480 | tf_op jit(solution)/shard_map/ppermute | solution.py:17
  9.1 5.3 %collective-permute-start.1 = (bf16[32,2432]{1,0:T(8,128)(2,1)S(1)}, bf16[32,2432]{1,0:T(8,128)(2,1)S(1)}, u32[]{:S(2)}, u32[]{:S(2)}) collective-permute-start(bf16[32,2432]{1,0:T(8,128)(2,1)S(1)} %pad_maximum_fusion.1), channel_id=1, source_target_pairs={{0,1},{1,0},{2,3},{3,2},{4,5},{5,4},{6,7},{7,6},{8,9},{9,8},{10,11... | collective-permute-start | bytes 466952 | tf_op jit(solution)/shard_map/ppermute | solution.py:17
  11.6 11.5 %copy-start.6 = (bf16[8,294,294]{2,0,1:T(8,128)(2,1)S(1)}, bf16[8,294,294]{2,0,1:T(8,128)(2,1)}, u32[]{:S(2)}) copy-start(bf16[8,294,294]{2,0,1:T(8,128)(2,1)} %param.15) | copy-start | bytes 4148932
  11.6 7.1 %collective-permute-start.3 = (bf16[32,2432]{1,0:T(8,128)(2,1)S(1)}, bf16[32,2432]{1,0:T(8,128)(2,1)S(1)}, u32[]{:S(2)}, u32[]{:S(2)}) collective-permute-start(bf16[32,2432]{1,0:T(8,128)(2,1)S(1)} %pad_maximum_fusion.1), channel_id=1, source_target_pairs={{4,8},{12,16},{20,24},{8,4},{16,12},{24,20},{5,9},{13,17},{21,25},... | collective-permute-start | bytes 466952 | tf_op jit(solution)/shard_map/ppermute | solution.py:281
  15.5 1.7 %collective-permute-start.5 = (bf16[8,294]{1,0:T(8,128)(2,1)S(1)}, bf16[8,294]{1,0:T(8,128)(2,1)S(1)}, u32[]{:S(2)}, u32[]{:S(2)}) collective-permute-start(bf16[8,294]{1,0:T(8,128)(2,1)S(1)} %shard_map.84), channel_id=1, source_target_pairs={{0,4},{4,0},{8,12},{12,8},{16,20},{20,16},{24,28},{28,24},{1,5},{5... | collective-permute-start | bytes 14120 | tf_op jit(solution)/shard_map/ppermute | solution.py:17
  16.4 9.3 %collective-permute-start.2 = (bf16[64,2432]{1,0:T(8,128)(2,1)S(1)}, bf16[64,2432]{1,0:T(8,128)(2,1)S(1)}, u32[]{:S(2)}, u32[]{:S(2)}) collective-permute-start(bf16[64,2432]{1,0:T(8,128)(2,1)S(1)} %pad_maximum_fusion.rows_ref.range_ref), channel_id=1, source_target_pairs={{0,4},{4,0},{8,12},{12,8},{16,20},{20,16},{24,28},{28,24},{1,5},{5... | collective-permute-start | bytes 933896 | tf_op jit(solution)/shard_map/ppermute | solution.py:17
  17.2 3.7 %collective-permute-start.6 = (bf16[16,294]{1,0:T(8,128)(2,1)S(1)}, bf16[16,294]{1,0:T(8,128)(2,1)S(1)}, u32[]{:S(2)}, u32[]{:S(2)}) collective-permute-start(bf16[16,294]{1,0:T(8,128)(2,1)S(1)} %pad_maximum_fusion.4), channel_id=1, source_target_pairs={{0,8},{4,12},{8,0},{12,4},{16,24},{20,28},{24,16},{28,20},{1,9},{5... | collective-permute-start | bytes 28232 | tf_op jit(solution)/shard_map/ppermute | solution.py:17
  18.7 7.0 %collective-permute-start.4 = (bf16[32,2432]{1,0:T(8,128)(2,1)S(1)}, bf16[32,2432]{1,0:T(8,128)(2,1)S(1)}, u32[]{:S(2)}, u32[]{:S(2)}) collective-permute-start(bf16[32,2432]{1,0:T(8,128)(2,1)S(1)} %collective-permute-done.3.outer_even_ref), channel_id=1, source_target_pairs={{0,1},{1,0},{2,3},{3,2},{4,5},{5,4},{6,7},{7,6},{8,9},{9,8},{10,11... | collective-permute-start | bytes 466952 | tf_op jit(solution)/shard_map/ppermute | solution.py:17
  20.9 2.4 %copy-start.5 = (bf16[16,294,294]{2,0,1:T(8,128)(2,1)S(1)}, bf16[16,294,294]{2,0,1:T(8,128)(2,1)}, u32[]{:S(2)}) copy-start(bf16[16,294,294]{2,0,1:T(8,128)(2,1)} %param.14) | copy-start | bytes 8297860
  21.0 4.8 %collective-permute-start.7 = (bf16[32,294]{1,0:T(8,128)(2,1)S(1)}, bf16[32,294]{1,0:T(8,128)(2,1)S(1)}, u32[]{:S(2)}, u32[]{:S(2)}) collective-permute-start(bf16[32,294]{1,0:T(8,128)(2,1)S(1)} %pad_maximum_fusion.3), channel_id=1, source_target_pairs={{0,16},{4,20},{8,24},{12,28},{16,0},{20,4},{24,8},{28,12},{1,17},{... | collective-permute-start | bytes 56456 | tf_op jit(solution)/shard_map/ppermute | solution.py:17
  24.2 0.7 %copy-start.1 = (s32[16,189]{1,0:T(8,128)S(1)}, s32[16,189]{1,0:T(8,128)}, u32[]{:S(2)}) copy-start(s32[16,189]{1,0:T(8,128)} %sources_ref.1) | copy-start | bytes 36292
  24.2 0.7 %copy-start.2 = (s32[16,189]{1,0:T(8,128)S(1)}, s32[16,189]{1,0:T(8,128)}, u32[]{:S(2)}) copy-start(s32[16,189]{1,0:T(8,128)} %classes_ref.1) | copy-start | bytes 36292
  24.2 0.7 %copy-start.3 = (s32[1,189]{1,0:T(1,128)S(1)}, s32[1,189]{1,0:T(1,128)}, u32[]{:S(2)}) copy-start(s32[1,189]{1,0:T(1,128)} %grand_sources_ref.1) | copy-start | bytes 2272
  24.2 0.7 %copy-start.4 = (s32[1,189]{1,0:T(1,128)S(1)}, s32[1,189]{1,0:T(1,128)}, u32[]{:S(2)}) copy-start(s32[1,189]{1,0:T(1,128)} %grand_classes_ref.1) | copy-start | bytes 2272

commit v6 on v5

--- a/solution.py
+++ b/solution.py
@@ -275,10 +275,14 @@
         other = swapped(joined, "sub", mask)
         for at, p in enumerate(order):
             held[p ^ mask] = other[at * own : (at + 1) * own]
-    even_rows = jnp.concatenate([held[p] for p in sorted(held)], axis=0)
-    odd_rows = swapped(even_rows, "sub", 1)
+    near_own = swapped(rows, "sub", 1)
+    rest_rows = jnp.concatenate([held[p] for p in sorted(held) if p], axis=0)
+    even_rows = jnp.concatenate([rows, rest_rows], axis=0)
+    odd_rows = jnp.concatenate([near_own, swapped(rest_rows, "sub", 1)], axis=0)
     pairs = [(i, i + 1) for i in range(1, morton_count - 1, 2)]
-    outer_even = lax.ppermute(even_rows, "morton", pairs + [(j, i) for i, j in pairs])
+    ends = [(0, morton_count - 1), (morton_count - 1, 0)]
+    swaps = pairs + [(j, i) for i, j in pairs] + ends
+    outer_even = lax.ppermute(even_rows, "morton", swaps)
     outer_odd = swapped(outer_even, "sub", 1)
     range_rows = jnp.concatenate([even_rows, odd_rows], axis=0)
     inner_rows = swapped(range_rows, "morton", 1)

time: 29.1 us -> 26.9 us (0.924)
  waiting for transfers between devices: 7.48 us -> 3.47 us
  starting transfers between devices: 11.8 us -> 13.7 us
    ppermute x7 -> x8, waiting for transfers between devices: 7.48 us -> 3.47 us  [swapped(): return lax.ppermute(value, axis, [(i, i ^ mask) for i in range(count)])]
    ppermute x7 -> x8, starting transfers between devices: 11 us -> 12.3 us  [swapped(): return lax.ppermute(value, axis, [(i, i ^ mask) for i in range(count)])]
    ppermute x1, starting transfers between devices: 0.8 us -> 1.44 us  [shards(): outer_even = lax.ppermute(even_rows, 'morton', swaps)]
  transfers between devices with their start and end apart: 8 -> 9, of which waited for: 4 -> 4; matrix products, arithmetic and copies ran while one was open for 10% -> 11% of each run, Pallas kernels for 6% -> 7%
where the time goes in v6:
time: 26.9 us; the launch traced here: 26.7 us
  starting transfers between devices  13.7 us (51%)
  Pallas kernels  4.98 us (19%)
  local copies, waits for them, and re-layouts  4.36 us (16%)
  waiting for transfers between devices  3.47 us (13%)
    ppermute x8, starting transfers between devices, swapped(): return lax.ppermute(value, axis, [(i, i ^ mask) for i in range(count)])  12.3 us
    pallas_call x5, Pallas kernels, call(): pl.pallas_call(kernel, out_shape=outs, in_specs=[whole] * len(operands),...  4.98 us
    unnamed x17, local copies, waits for them, and re-layouts  4.36 us
    ppermute x8, waiting for transfers between devices, swapped(): return lax.ppermute(value, axis, [(i, i ^ mask) for i in range(count)])  3.47 us
    ppermute x1, starting transfers between devices, shards(): outer_even = lax.ppermute(even_rows, 'morton', swaps)  1.44 us
  transfers between devices with their start and end apart: 9, of which 4 were waited for; matrix products, arithmetic and copies ran while one was open for 11% of the time, Pallas kernels for 7%

profile of v6, /device:TPU:0, one launch (start us, length us, event | category | flops | bytes accessed | tf_op | source)
XLA Modules:
  0.0 26.7 jit_solution(3263397252317225160)
XLA Ops:
  0.0 0.0 copy-start
  0.0 0.9 %copy-done = bf16[16,8,294]{2,1,0:T(8,128)(2,1)S(1)} copy-done((bf16[16,8,294]{2,1,0:T(8,128)(2,1)S(1)}, bf16[16,8,294]{2,1,0:T(8,128)(2,1)}, u32[]{:S(2)}) %copy-start) | copy-done | bytes 75288
  0.9 0.1 shard_map.83
  1.0 4.1 %collective-permute-start = (bf16[16,2432]{1,0:T(8,128)(2,1)S(1)}, bf16[16,2432]{1,0:T(8,128)(2,1)S(1)}, u32[]{:S(2)}, u32[]{:S(2)}) collective-permute-start(bf16[16,2432]{1,0:T(8,128)(2,1)S(1)} %shard_map.83), channel_id=1, source_target_pairs={{0,2},{1,3},{2,0},{3,1},{4,6},{5,7},{6,4},{7,5},{8,10},{9,11},{10,... | collective-permute-start | bytes 233480 | tf_op jit(solution)/shard_map/ppermute | solution.py:17
  5.1 1.6 %collective-permute-start.1 = (bf16[16,2432]{1,0:T(8,128)(2,1)S(1)}, bf16[16,2432]{1,0:T(8,128)(2,1)S(1)}, u32[]{:S(2)}, u32[]{:S(2)}) collective-permute-start(bf16[16,2432]{1,0:T(8,128)(2,1)S(1)} %shard_map.83), channel_id=1, source_target_pairs={{0,1},{1,0},{2,3},{3,2},{4,5},{5,4},{6,7},{7,6},{8,9},{9,8},{10,11... | collective-permute-start | bytes 233480 | tf_op jit(solution)/shard_map/ppermute | solution.py:17
  6.7 1.7 %copy.9._up_ref.up_ref = bf16[8,294,294]{2,1,0:T(8,128)(2,1)S(1)} copy(bf16[8,294,294]{2,0,1:T(8,128)(2,1)} %param.13) | data formatting | bytes 2765952 | tf_op args[5]
  8.4 0.0 copy-start.6
  8.4 0.2 collective-permute-done
  8.6 1.3 %collective-permute-start.2 = (bf16[16,2432]{1,0:T(8,128)(2,1)S(1)}, bf16[16,2432]{1,0:T(8,128)(2,1)S(1)}, u32[]{:S(2)}, u32[]{:S(2)}) collective-permute-start(bf16[16,2432]{1,0:T(8,128)(2,1)S(1)} %collective-permute-done), channel_id=1, source_target_pairs={{0,1},{1,0},{2,3},{3,2},{4,5},{5,4},{6,7},{7,6},{8,9},{9,8},{10,11... | collective-permute-start | bytes 233480 | tf_op jit(solution)/shard_map/ppermute | solution.py:17
  9.9 1.4 %collective-permute-start.4 = (bf16[32,2432]{1,0:T(8,128)(2,1)S(1)}, bf16[32,2432]{1,0:T(8,128)(2,1)S(1)}, u32[]{:S(2)}, u32[]{:S(2)}) collective-permute-start(bf16[32,2432]{1,0:T(8,128)(2,1)S(1)} %pad_maximum_fusion.1), channel_id=1, source_target_pairs={{4,8},{12,16},{20,24},{8,4},{16,12},{24,20},{0,28},{28,0},{5,9},{1... | collective-permute-start | bytes 466952 | tf_op jit(solution)/shard_map/ppermute | solution.py:285
  11.4 0.0 collective-permute-done.1
  11.4 1.7 %collective-permute-done.2 = bf16[16,2432]{1,0:T(8,128)(2,1)S(1)} collective-permute-done((bf16[16,2432]{1,0:T(8,128)(2,1)S(1)}, bf16[16,2432]{1,0:T(8,128)(2,1)S(1)}, u32[]{:S(2)}, u32[]{:S(2)}) %collective-permute-start.2) | collective-permute-done | bytes 77856 | tf_op jit(solution)/shard_map/ppermute | solution.py:17
  13.0 1.1 %shard_map.84 = bf16[8,294]{1,0:T(8,128)(2,1)S(1)} custom-call(bf16[64,2432]{1,0:T(8,128)(2,1)S(1)} %pad_maximum_fusion.rows_ref.range_ref, bf16[8,294,294]{2,1,0:T(8,128)(2,1)S(1)} %copy.9._up_ref.up_ref), custom_call_target="tpu_custom_call" | custom-call | tf_op jit(solution)/shard_map/pallas_call | solution.py:240
  14.1 0.0 collective-permute-start.6
  14.1 0.5 %collective-permute-start.3 = (bf16[64,2432]{1,0:T(8,128)(2,1)S(1)}, bf16[64,2432]{1,0:T(8,128)(2,1)S(1)}, u32[]{:S(2)}, u32[]{:S(2)}) collective-permute-start(bf16[64,2432]{1,0:T(8,128)(2,1)S(1)} %pad_maximum_fusion.rows_ref.range_ref), channel_id=1, source_target_pairs={{0,4},{4,0},{8,12},{12,8},{16,20},{20,16},{24,28},{28,24},{1,5},{5... | collective-permute-start | bytes 933896 | tf_op jit(solution)/shard_map/ppermute | solution.py:17
  14.6 0.7 %collective-permute-done.6 = bf16[8,294]{1,0:T(8,128)(2,1)S(1)} collective-permute-done((bf16[8,294]{1,0:T(8,128)(2,1)S(1)}, bf16[8,294]{1,0:T(8,128)(2,1)S(1)}, u32[]{:S(2)}, u32[]{:S(2)}) %collective-permute-start.6) | collective-permute-done | bytes 4736 | tf_op jit(solution)/shard_map/ppermute | solution.py:17
  15.3 1.9 %collective-permute-start.7 = (bf16[16,294]{1,0:T(8,128)(2,1)S(1)}, bf16[16,294]{1,0:T(8,128)(2,1)S(1)}, u32[]{:S(2)}, u32[]{:S(2)}) collective-permute-start(bf16[16,294]{1,0:T(8,128)(2,1)S(1)} %pad_maximum_fusion.4), channel_id=1, source_target_pairs={{0,8},{4,12},{8,0},{12,4},{16,24},{20,28},{24,16},{28,20},{1,9},{5... | collective-permute-start | bytes 28232 | tf_op jit(solution)/shard_map/ppermute | solution.py:17
  17.2 0.0 collective-permute-done.4.outer_even_ref
  17.2 0.9 %collective-permute-start.5 = (bf16[32,2432]{1,0:T(8,128)(2,1)S(1)}, bf16[32,2432]{1,0:T(8,128)(2,1)S(1)}, u32[]{:S(2)}, u32[]{:S(2)}) collective-permute-start(bf16[32,2432]{1,0:T(8,128)(2,1)S(1)} %collective-permute-done.4.outer_even_ref), channel_id=1, source_target_pairs={{0,1},{1,0},{2,3},{3,2},{4,5},{5,4},{6,7},{7,6},{8,9},{9,8},{10,11... | collective-permute-start | bytes 466952 | tf_op jit(solution)/shard_map/ppermute | solution.py:17
  18.1 0.9 %collective-permute-done.7 = bf16[16,294]{1,0:T(8,128)(2,1)S(1)} collective-permute-done((bf16[16,294]{1,0:T(8,128)(2,1)S(1)}, bf16[16,294]{1,0:T(8,128)(2,1)S(1)}, u32[]{:S(2)}, u32[]{:S(2)}) %collective-permute-start.7) | collective-permute-done | bytes 9440 | tf_op jit(solution)/shard_map/ppermute | solution.py:17
  19.0 0.0 copy-start.5
  19.0 2.0 %collective-permute-start.8 = (bf16[32,294]{1,0:T(8,128)(2,1)S(1)}, bf16[32,294]{1,0:T(8,128)(2,1)S(1)}, u32[]{:S(2)}, u32[]{:S(2)}) collective-permute-start(bf16[32,294]{1,0:T(8,128)(2,1)S(1)} %pad_maximum_fusion.3), channel_id=1, source_target_pairs={{0,16},{4,20},{8,24},{12,28},{16,0},{20,4},{24,8},{28,12},{1,17},{... | collective-permute-start | bytes 56456 | tf_op jit(solution)/shard_map/ppermute | solution.py:17
  21.0 0.0 copy-done.6
  21.0 0.2 copy.14._down_ref.down_ref
  21.2 0.0 copy-done.5
  21.3 0.8 %copy.13._far_ref.far_ref = bf16[16,294,294]{2,1,0:T(8,128)(2,1)S(1)} copy(bf16[16,294,294]{2,0,1:T(8,128)(2,1)S(1)} %copy-done.5) | data formatting | bytes 5531904 | tf_op args[6]
  22.1 0.0 copy-start.1
  22.1 0.0 copy-start.2
  22.1 0.0 copy-start.3
  22.1 0.0 copy-start.4
  22.1 0.7 %copy-done.1 = s32[16,189]{1,0:T(8,128)S(1)} copy-done((s32[16,189]{1,0:T(8,128)S(1)}, s32[16,189]{1,0:T(8,128)}, u32[]{:S(2)}) %copy-start.1) | copy-done | bytes 12120
  22.8 0.0 copy-done.2
  22.8 0.0 copy-done.3
  22.8 0.0 copy-done.4
  22.8 0.8 %shard_map.82 = (bf16[256,192]{1,0:T(8,128)(2,1)S(1)}, bf16[256,64]{1,0:T(8,128)(2,1)S(1)}) custom-call(s32[16,189]{1,0:T(8,128)S(1)} %copy-done.1, s32[16,189]{1,0:T(8,128)S(1)} %copy-done.2, s32[1,189]{1,0:T(1,128)S(1)} %copy-done.3, s32[1,189]{1,0:T(1,128)S(1)} %copy-done.4, bf16[8,294,294]{2,1,0:T(8,128)(2,1)S(1)} %copy.9._up_ref.up_ref), custom_call_target="tpu_custom_call" | custom-call | tf_op jit(solution)/shard_map/pallas_call | solution.py:240
  23.6 0.0 collective-permute-done.8
  23.6 0.0 collective-permute-done.5.outer_odd_ref
  23.6 0.0 collective-permute-done.3.inner_ref
  23.6 3.1 %shard_map.86 = bf16[16,8,294]{2,1,0:T(8,128)(2,1)} custom-call(bf16[256,192]{1,0:T(8,128)(2,1)S(1)} %get-tuple-element.7.counts_ref, bf16[256,64]{1,0:T(8,128)(2,1)S(1)} %get-tuple-element.8.grand_counts_ref, bf16[64,2432]{1,0:T(8,128)(2,1)S(1)} %collective-permute-done.3.inner_ref, bf16[64,2432]{1,0:T(8,128)(2,1)S(1)} %pad_maximum_fusion.rows_ref.range_ref, ...), custom_call_target="tpu_custom_call" | custom-call | tf_op jit(solution)/shard_map/pallas_call | solution.py:240
  (6 shorter events, 0.1 us)
Async XLA Ops:
  0.0 0.9 %copy-start = (bf16[16,8,294]{2,1,0:T(8,128)(2,1)S(1)}, bf16[16,8,294]{2,1,0:T(8,128)(2,1)}, u32[]{:S(2)}) copy-start(bf16[16,8,294]{2,1,0:T(8,128)(2,1)} %dens_ref.1) | copy-start | bytes 225796
  1.0 7.6 %collective-permute-start = (bf16[16,2432]{1,0:T(8,128)(2,1)S(1)}, bf16[16,2432]{1,0:T(8,128)(2,1)S(1)}, u32[]{:S(2)}, u32[]{:S(2)}) collective-permute-start(bf16[16,2432]{1,0:T(8,128)(2,1)S(1)} %shard_map.83), channel_id=1, source_target_pairs={{0,2},{1,3},{2,0},{3,1},{4,6},{5,7},{6,4},{7,5},{8,10},{9,11},{10,... | collective-permute-start | bytes 233480 | tf_op jit(solution)/shard_map/ppermute | solution.py:17
  5.1 6.3 %collective-permute-start.1 = (bf16[16,2432]{1,0:T(8,128)(2,1)S(1)}, bf16[16,2432]{1,0:T(8,128)(2,1)S(1)}, u32[]{:S(2)}, u32[]{:S(2)}) collective-permute-start(bf16[16,2432]{1,0:T(8,128)(2,1)S(1)} %shard_map.83), channel_id=1, source_target_pairs={{0,1},{1,0},{2,3},{3,2},{4,5},{5,4},{6,7},{7,6},{8,9},{9,8},{10,11... | collective-permute-start | bytes 233480 | tf_op jit(solution)/shard_map/ppermute | solution.py:17
  8.4 12.6 %copy-start.6 = (bf16[8,294,294]{2,0,1:T(8,128)(2,1)S(1)}, bf16[8,294,294]{2,0,1:T(8,128)(2,1)}, u32[]{:S(2)}) copy-start(bf16[8,294,294]{2,0,1:T(8,128)(2,1)} %param.15) | copy-start | bytes 4148932
  8.6 4.4 %collective-permute-start.2 = (bf16[16,2432]{1,0:T(8,128)(2,1)S(1)}, bf16[16,2432]{1,0:T(8,128)(2,1)S(1)}, u32[]{:S(2)}, u32[]{:S(2)}) collective-permute-start(bf16[16,2432]{1,0:T(8,128)(2,1)S(1)} %collective-permute-done), channel_id=1, source_target_pairs={{0,1},{1,0},{2,3},{3,2},{4,5},{5,4},{6,7},{7,6},{8,9},{9,8},{10,11... | collective-permute-start | bytes 233480 | tf_op jit(solution)/shard_map/ppermute | solution.py:17
  9.9 7.3 %collective-permute-start.4 = (bf16[32,2432]{1,0:T(8,128)(2,1)S(1)}, bf16[32,2432]{1,0:T(8,128)(2,1)S(1)}, u32[]{:S(2)}, u32[]{:S(2)}) collective-permute-start(bf16[32,2432]{1,0:T(8,128)(2,1)S(1)} %pad_maximum_fusion.1), channel_id=1, source_target_pairs={{4,8},{12,16},{20,24},{8,4},{16,12},{24,20},{0,28},{28,0},{5,9},{1... | collective-permute-start | bytes 466952 | tf_op jit(solution)/shard_map/ppermute | solution.py:285
  14.1 1.2 %collective-permute-start.6 = (bf16[8,294]{1,0:T(8,128)(2,1)S(1)}, bf16[8,294]{1,0:T(8,128)(2,1)S(1)}, u32[]{:S(2)}, u32[]{:S(2)}) collective-permute-start(bf16[8,294]{1,0:T(8,128)(2,1)S(1)} %shard_map.84), channel_id=1, source_target_pairs={{0,4},{4,0},{8,12},{12,8},{16,20},{20,16},{24,28},{28,24},{1,5},{5... | collective-permute-start | bytes 14120 | tf_op jit(solution)/shard_map/ppermute | solution.py:17
  14.1 9.5 %collective-permute-start.3 = (bf16[64,2432]{1,0:T(8,128)(2,1)S(1)}, bf16[64,2432]{1,0:T(8,128)(2,1)S(1)}, u32[]{:S(2)}, u32[]{:S(2)}) collective-permute-start(bf16[64,2432]{1,0:T(8,128)(2,1)S(1)} %pad_maximum_fusion.rows_ref.range_ref), channel_id=1, source_target_pairs={{0,4},{4,0},{8,12},{12,8},{16,20},{20,16},{24,28},{28,24},{1,5},{5... | collective-permute-start | bytes 933896 | tf_op jit(solution)/shard_map/ppermute | solution.py:17
  15.3 3.7 %collective-permute-start.7 = (bf16[16,294]{1,0:T(8,128)(2,1)S(1)}, bf16[16,294]{1,0:T(8,128)(2,1)S(1)}, u32[]{:S(2)}, u32[]{:S(2)}) collective-permute-start(bf16[16,294]{1,0:T(8,128)(2,1)S(1)} %pad_maximum_fusion.4), channel_id=1, source_target_pairs={{0,8},{4,12},{8,0},{12,4},{16,24},{20,28},{24,16},{28,20},{1,9},{5... | collective-permute-start | bytes 28232 | tf_op jit(solution)/shard_map/ppermute | solution.py:17
  17.2 6.4 %collective-permute-start.5 = (bf16[32,2432]{1,0:T(8,128)(2,1)S(1)}, bf16[32,2432]{1,0:T(8,128)(2,1)S(1)}, u32[]{:S(2)}, u32[]{:S(2)}) collective-permute-start(bf16[32,2432]{1,0:T(8,128)(2,1)S(1)} %collective-permute-done.4.outer_even_ref), channel_id=1, source_target_pairs={{0,1},{1,0},{2,3},{3,2},{4,5},{5,4},{6,7},{7,6},{8,9},{9,8},{10,11... | collective-permute-start | bytes 466952 | tf_op jit(solution)/shard_map/ppermute | solution.py:17
  19.0 2.3 %copy-start.5 = (bf16[16,294,294]{2,0,1:T(8,128)(2,1)S(1)}, bf16[16,294,294]{2,0,1:T(8,128)(2,1)}, u32[]{:S(2)}) copy-start(bf16[16,294,294]{2,0,1:T(8,128)(2,1)} %param.14) | copy-start | bytes 8297860
  19.0 4.6 %collective-permute-start.8 = (bf16[32,294]{1,0:T(8,128)(2,1)S(1)}, bf16[32,294]{1,0:T(8,128)(2,1)S(1)}, u32[]{:S(2)}, u32[]{:S(2)}) collective-permute-start(bf16[32,294]{1,0:T(8,128)(2,1)S(1)} %pad_maximum_fusion.3), channel_id=1, source_target_pairs={{0,16},{4,20},{8,24},{12,28},{16,0},{20,4},{24,8},{28,12},{1,17},{... | collective-permute-start | bytes 56456 | tf_op jit(solution)/shard_map/ppermute | solution.py:17
  22.1 0.7 %copy-start.1 = (s32[16,189]{1,0:T(8,128)S(1)}, s32[16,189]{1,0:T(8,128)}, u32[]{:S(2)}) copy-start(s32[16,189]{1,0:T(8,128)} %sources_ref.1) | copy-start | bytes 36292
  22.1 0.7 %copy-start.2 = (s32[16,189]{1,0:T(8,128)S(1)}, s32[16,189]{1,0:T(8,128)}, u32[]{:S(2)}) copy-start(s32[16,189]{1,0:T(8,128)} %classes_ref.1) | copy-start | bytes 36292
  22.1 0.7 %copy-start.3 = (s32[1,189]{1,0:T(1,128)S(1)}, s32[1,189]{1,0:T(1,128)}, u32[]{:S(2)}) copy-start(s32[1,189]{1,0:T(1,128)} %grand_sources_ref.1) | copy-start | bytes 2272
  22.1 0.7 %copy-start.4 = (s32[1,189]{1,0:T(1,128)S(1)}, s32[1,189]{1,0:T(1,128)}, u32[]{:S(2)}) copy-start(s32[1,189]{1,0:T(1,128)} %grand_classes_ref.1) | copy-start | bytes 2272

commit v7 on v6

--- a/solution.py
+++ b/solution.py
@@ -180,7 +180,7 @@
     grand_pool_ref,
     far_ref,
     down_ref,
-    _ready_ref,
+    tails_ref,
     out_ref,
     aggregate,
     grand_aggregate,
@@ -198,12 +198,29 @@
     refs = (inner_ref, range_ref, outer_even_ref, outer_odd_ref)
     pool = jnp.concatenate([ref[...] for ref in refs], axis=0)
     aggregate[...] = jnp.dot(counts_ref[...], pool, preferred_element_type=F32).astype(BF16)
-    total = jnp.zeros((rhs_count * own + group, width), F32)
+    main, step = lanes.main, tails_ref.shape[0] // classes_count
+    spare = jnp.zeros((own, step - lanes.tail), BF16)
+    spare_grand = jnp.zeros((group, step - lanes.tail), BF16)
+    lefts = []
+    for n in range(rhs_count):
+        parts = []
+        for c in range(classes_count):
+            parts += [aggregate[c * own : (c + 1) * own, lanes.tail_of(n)], spare]
+        lefts.append(jnp.concatenate(parts, axis=1))
+    parts = []
     for c in range(classes_count):
-        rows = aggregate[c * own : (c + 1) * own, :]
-        parts = [lanes.take(rows, n) for n in range(rhs_count)]
-        parts.append(grand_aggregate[c * group : (c + 1) * group, :])
-        total += jnp.dot(jnp.concatenate(parts, axis=0), far_ref[c], preferred_element_type=F32)
+        parts += [grand_aggregate[c * group : (c + 1) * group, main:], spare_grand]
+    lefts.append(jnp.concatenate(parts, axis=1))
+    total = jnp.dot(jnp.concatenate(lefts, axis=0), tails_ref[...], preferred_element_type=F32)
+    for first in range(0, classes_count, 4):
+        lefts = []
+        for c in range(first, first + 4):
+            rows = aggregate[c * own : (c + 1) * own, :]
+            parts = [rows[:, lanes.main_of(n)] for n in range(rhs_count)]
+            parts.append(grand_aggregate[c * group : (c + 1) * group, :main])
+            lefts.append(jnp.concatenate(parts, axis=0))
+        right = far_ref[first : first + 4, :main, :].reshape(4 * main, width)
+        total += jnp.dot(jnp.concatenate(lefts, axis=1), right, preferred_element_type=F32)
     pad = jnp.zeros((own, far_rows.shape[0] * LANES - width), F32)
     for n in range(rhs_count):
         rows = jnp.concatenate([total[n * own : (n + 1) * own, :], pad], axis=1)
@@ -226,8 +243,14 @@
             out_ref[leaf] = local.astype(BF16)
 
 
-def ready_kernel(_far_ref, _down_ref, out_ref):
-    out_ref[...] = jnp.zeros(out_ref.shape, F32)
+def tails_kernel(main, far_ref, _down_ref, out_ref, wide):
+    classes_count, width = far_ref.shape[0], far_ref.shape[2]
+    tail = far_ref.shape[1] - main
+    step = out_ref.shape[0] // classes_count
+    for c in range(classes_count):
+        wide[c * step : c * step + tail, :] = far_ref[c, main:, :].astype(F32)
+        wide[c * step + tail : (c + 1) * step, :] = jnp.zeros((step - tail, width), F32)
+    out_ref[...] = wide[...].astype(BF16)
 
 
 def tiled(rows, width):
@@ -301,7 +324,14 @@
         grand_classes,
         up_ops,
     )
-    ready = call(ready_kernel, struct((8, LANES), F32), [], far_ops, down_ops)
+    tail_step = -(-lanes.tail // 8) * 8
+    tails = call(
+        functools.partial(tails_kernel, lanes.main),
+        struct((classes_count * tail_step, width), BF16),
+        [pltpu.VMEM((classes_count * tail_step, width), F32)],
+        far_ops,
+        down_ops,
+    )
 
     grand_pool = call(
         functools.partial(grand_kernel, lanes, grand_span),
@@ -334,7 +364,7 @@
         grand_pool,
         far_ops,
         down_ops,
-        ready,
+        tails,
     )
 
 

time: 26.9 us -> 26.4 us (0.981)
  Pallas kernels: 4.98 us -> 4.51 us
    pallas_call x5, Pallas kernels: 4.98 us -> 4.51 us  [call(): pl.pallas_call(kernel, out_shape=outs, in_specs=[whole] * len(operands),...]
where the time goes in v7:
time: 26.4 us; the launch traced here: 26.1 us
  starting transfers between devices  13.7 us (52%)
  Pallas kernels  4.51 us (17%)
  local copies, waits for them, and re-layouts  4.25 us (16%)
  waiting for transfers between devices  3.47 us (13%)
    ppermute x8, starting transfers between devices, swapped(): return lax.ppermute(value, axis, [(i, i ^ mask) for i in range(count)])  12.3 us
    pallas_call x5, Pallas kernels, call(): pl.pallas_call(kernel, out_shape=outs, in_specs=[whole] * len(operands),...  4.51 us
    unnamed x17, local copies, waits for them, and re-layouts  4.25 us
    ppermute x8, waiting for transfers between devices, swapped(): return lax.ppermute(value, axis, [(i, i ^ mask) for i in range(count)])  3.47 us
    ppermute x1, starting transfers between devices, shards(): outer_even = lax.ppermute(even_rows, 'morton', swaps)  1.43 us
  transfers between devices with their start and end apart: 9, of which 4 were waited for; matrix products, arithmetic and copies ran while one was open for 11% of the time, Pallas kernels for 7%

profile of v7, /device:TPU:0, one launch (start us, length us, event | category | flops | bytes accessed | tf_op | source)
XLA Modules:
  0.0 26.1 jit_solution(16272584052893578991)
XLA Ops:
  0.0 0.0 copy-start
  0.0 0.9 %copy-done = bf16[16,8,294]{2,1,0:T(8,128)(2,1)S(1)} copy-done((bf16[16,8,294]{2,1,0:T(8,128)(2,1)S(1)}, bf16[16,8,294]{2,1,0:T(8,128)(2,1)}, u32[]{:S(2)}) %copy-start) | copy-done | bytes 75288
  0.9 0.1 shard_map.83
  1.0 4.1 %collective-permute-start = (bf16[16,2432]{1,0:T(8,128)(2,1)S(1)}, bf16[16,2432]{1,0:T(8,128)(2,1)S(1)}, u32[]{:S(2)}, u32[]{:S(2)}) collective-permute-start(bf16[16,2432]{1,0:T(8,128)(2,1)S(1)} %shard_map.83), channel_id=1, source_target_pairs={{0,2},{1,3},{2,0},{3,1},{4,6},{5,7},{6,4},{7,5},{8,10},{9,11},{10,... | collective-permute-start | bytes 233480 | tf_op jit(solution)/shard_map/ppermute | solution.py:17
  5.1 1.6 %collective-permute-start.1 = (bf16[16,2432]{1,0:T(8,128)(2,1)S(1)}, bf16[16,2432]{1,0:T(8,128)(2,1)S(1)}, u32[]{:S(2)}, u32[]{:S(2)}) collective-permute-start(bf16[16,2432]{1,0:T(8,128)(2,1)S(1)} %shard_map.83), channel_id=1, source_target_pairs={{0,1},{1,0},{2,3},{3,2},{4,5},{5,4},{6,7},{7,6},{8,9},{9,8},{10,11... | collective-permute-start | bytes 233480 | tf_op jit(solution)/shard_map/ppermute | solution.py:17
  6.7 1.7 %copy.9._up_ref.up_ref = bf16[8,294,294]{2,1,0:T(8,128)(2,1)S(1)} copy(bf16[8,294,294]{2,0,1:T(8,128)(2,1)} %param.13) | data formatting | bytes 2765952 | tf_op args[5]
  8.4 0.0 copy-start.6
  8.4 0.2 collective-permute-done
  8.6 1.3 %collective-permute-start.2 = (bf16[16,2432]{1,0:T(8,128)(2,1)S(1)}, bf16[16,2432]{1,0:T(8,128)(2,1)S(1)}, u32[]{:S(2)}, u32[]{:S(2)}) collective-permute-start(bf16[16,2432]{1,0:T(8,128)(2,1)S(1)} %collective-permute-done), channel_id=1, source_target_pairs={{0,1},{1,0},{2,3},{3,2},{4,5},{5,4},{6,7},{7,6},{8,9},{9,8},{10,11... | collective-permute-start | bytes 233480 | tf_op jit(solution)/shard_map/ppermute | solution.py:17
  9.9 1.4 %collective-permute-start.4 = (bf16[32,2432]{1,0:T(8,128)(2,1)S(1)}, bf16[32,2432]{1,0:T(8,128)(2,1)S(1)}, u32[]{:S(2)}, u32[]{:S(2)}) collective-permute-start(bf16[32,2432]{1,0:T(8,128)(2,1)S(1)} %pad_maximum_fusion.1), channel_id=1, source_target_pairs={{4,8},{12,16},{20,24},{8,4},{16,12},{24,20},{0,28},{28,0},{5,9},{1... | collective-permute-start | bytes 466952 | tf_op jit(solution)/shard_map/ppermute | solution.py:308
  11.4 0.0 collective-permute-done.1
  11.4 1.7 %collective-permute-done.2 = bf16[16,2432]{1,0:T(8,128)(2,1)S(1)} collective-permute-done((bf16[16,2432]{1,0:T(8,128)(2,1)S(1)}, bf16[16,2432]{1,0:T(8,128)(2,1)S(1)}, u32[]{:S(2)}, u32[]{:S(2)}) %collective-permute-start.2) | collective-permute-done | bytes 77856 | tf_op jit(solution)/shard_map/ppermute | solution.py:17
  13.0 1.1 %shard_map.84 = bf16[8,294]{1,0:T(8,128)(2,1)S(1)} custom-call(bf16[64,2432]{1,0:T(8,128)(2,1)S(1)} %pad_maximum_fusion.rows_ref.range_ref, bf16[8,294,294]{2,1,0:T(8,128)(2,1)S(1)} %copy.9._up_ref.up_ref), custom_call_target="tpu_custom_call" | custom-call | tf_op jit(solution)/shard_map/pallas_call | solution.py:263
  14.1 0.0 collective-permute-start.6
  14.1 0.5 %collective-permute-start.3 = (bf16[64,2432]{1,0:T(8,128)(2,1)S(1)}, bf16[64,2432]{1,0:T(8,128)(2,1)S(1)}, u32[]{:S(2)}, u32[]{:S(2)}) collective-permute-start(bf16[64,2432]{1,0:T(8,128)(2,1)S(1)} %pad_maximum_fusion.rows_ref.range_ref), channel_id=1, source_target_pairs={{0,4},{4,0},{8,12},{12,8},{16,20},{20,16},{24,28},{28,24},{1,5},{5... | collective-permute-start | bytes 933896 | tf_op jit(solution)/shard_map/ppermute | solution.py:17
  14.6 0.7 %collective-permute-done.6 = bf16[8,294]{1,0:T(8,128)(2,1)S(1)} collective-permute-done((bf16[8,294]{1,0:T(8,128)(2,1)S(1)}, bf16[8,294]{1,0:T(8,128)(2,1)S(1)}, u32[]{:S(2)}, u32[]{:S(2)}) %collective-permute-start.6) | collective-permute-done | bytes 4736 | tf_op jit(solution)/shard_map/ppermute | solution.py:17
  15.3 1.9 %collective-permute-start.7 = (bf16[16,294]{1,0:T(8,128)(2,1)S(1)}, bf16[16,294]{1,0:T(8,128)(2,1)S(1)}, u32[]{:S(2)}, u32[]{:S(2)}) collective-permute-start(bf16[16,294]{1,0:T(8,128)(2,1)S(1)} %pad_maximum_fusion.4), channel_id=1, source_target_pairs={{0,8},{4,12},{8,0},{12,4},{16,24},{20,28},{24,16},{28,20},{1,9},{5... | collective-permute-start | bytes 28232 | tf_op jit(solution)/shard_map/ppermute | solution.py:17
  17.2 0.0 collective-permute-done.4.outer_even_ref
  17.2 0.9 %collective-permute-start.5 = (bf16[32,2432]{1,0:T(8,128)(2,1)S(1)}, bf16[32,2432]{1,0:T(8,128)(2,1)S(1)}, u32[]{:S(2)}, u32[]{:S(2)}) collective-permute-start(bf16[32,2432]{1,0:T(8,128)(2,1)S(1)} %collective-permute-done.4.outer_even_ref), channel_id=1, source_target_pairs={{0,1},{1,0},{2,3},{3,2},{4,5},{5,4},{6,7},{7,6},{8,9},{9,8},{10,11... | collective-permute-start | bytes 466952 | tf_op jit(solution)/shard_map/ppermute | solution.py:17
  18.1 0.9 %collective-permute-done.7 = bf16[16,294]{1,0:T(8,128)(2,1)S(1)} collective-permute-done((bf16[16,294]{1,0:T(8,128)(2,1)S(1)}, bf16[16,294]{1,0:T(8,128)(2,1)S(1)}, u32[]{:S(2)}, u32[]{:S(2)}) %collective-permute-start.7) | collective-permute-done | bytes 9440 | tf_op jit(solution)/shard_map/ppermute | solution.py:17
  19.0 0.0 copy-start.5
  19.0 2.0 %collective-permute-start.8 = (bf16[32,294]{1,0:T(8,128)(2,1)S(1)}, bf16[32,294]{1,0:T(8,128)(2,1)S(1)}, u32[]{:S(2)}, u32[]{:S(2)}) collective-permute-start(bf16[32,294]{1,0:T(8,128)(2,1)S(1)} %pad_maximum_fusion.3), channel_id=1, source_target_pairs={{0,16},{4,20},{8,24},{12,28},{16,0},{20,4},{24,8},{28,12},{1,17},{... | collective-permute-start | bytes 56456 | tf_op jit(solution)/shard_map/ppermute | solution.py:17
  21.0 0.0 copy-done.6
  21.0 0.2 copy.14._down_ref.down_ref
  21.2 0.0 copy-done.5
  21.3 0.8 %copy.13.far_ref = bf16[16,294,294]{2,1,0:T(8,128)(2,1)S(1)} copy(bf16[16,294,294]{2,0,1:T(8,128)(2,1)S(1)} %copy-done.5) | data formatting | bytes 5531904 | tf_op args[6]
  22.1 0.0 copy-start.1
  22.1 0.0 copy-start.2
  22.1 0.0 copy-start.3
  22.1 0.0 copy-start.4
  22.1 0.1 shard_map.85.tails_ref
  22.2 0.5 %copy-done.1 = s32[16,189]{1,0:T(8,128)S(1)} copy-done((s32[16,189]{1,0:T(8,128)S(1)}, s32[16,189]{1,0:T(8,128)}, u32[]{:S(2)}) %copy-start.1) | copy-done | bytes 12120
  22.8 0.0 copy-done.2
  22.8 0.0 copy-done.3
  22.8 0.0 copy-done.4
  22.8 0.8 %shard_map.82 = (bf16[256,192]{1,0:T(8,128)(2,1)S(1)}, bf16[256,64]{1,0:T(8,128)(2,1)S(1)}) custom-call(s32[16,189]{1,0:T(8,128)S(1)} %copy-done.1, s32[16,189]{1,0:T(8,128)S(1)} %copy-done.2, s32[1,189]{1,0:T(1,128)S(1)} %copy-done.3, s32[1,189]{1,0:T(1,128)S(1)} %copy-done.4, bf16[8,294,294]{2,1,0:T(8,128)(2,1)S(1)} %copy.9._up_ref.up_ref), custom_call_target="tpu_custom_call" | custom-call | tf_op jit(solution)/shard_map/pallas_call | solution.py:263
  23.6 0.0 collective-permute-done.8
  23.6 0.0 collective-permute-done.5.outer_odd_ref
  23.6 0.0 collective-permute-done.3.inner_ref
  23.6 2.5 %shard_map.86 = bf16[16,8,294]{2,1,0:T(8,128)(2,1)} custom-call(bf16[256,192]{1,0:T(8,128)(2,1)S(1)} %get-tuple-element.7.counts_ref, bf16[256,64]{1,0:T(8,128)(2,1)S(1)} %get-tuple-element.8.grand_counts_ref, bf16[64,2432]{1,0:T(8,128)(2,1)S(1)} %collective-permute-done.3.inner_ref, bf16[64,2432]{1,0:T(8,128)(2,1)S(1)} %pad_maximum_fusion.rows_ref.range_ref, ...), custom_call_target="tpu_custom_call" | custom-call | tf_op jit(solution)/shard_map/pallas_call | solution.py:263
  (5 shorter events, 0.1 us)
Async XLA Ops:
  0.0 0.9 %copy-start = (bf16[16,8,294]{2,1,0:T(8,128)(2,1)S(1)}, bf16[16,8,294]{2,1,0:T(8,128)(2,1)}, u32[]{:S(2)}) copy-start(bf16[16,8,294]{2,1,0:T(8,128)(2,1)} %dens_ref.1) | copy-start | bytes 225796
  1.0 7.6 %collective-permute-start = (bf16[16,2432]{1,0:T(8,128)(2,1)S(1)}, bf16[16,2432]{1,0:T(8,128)(2,1)S(1)}, u32[]{:S(2)}, u32[]{:S(2)}) collective-permute-start(bf16[16,2432]{1,0:T(8,128)(2,1)S(1)} %shard_map.83), channel_id=1, source_target_pairs={{0,2},{1,3},{2,0},{3,1},{4,6},{5,7},{6,4},{7,5},{8,10},{9,11},{10,... | collective-permute-start | bytes 233480 | tf_op jit(solution)/shard_map/ppermute | solution.py:17
  5.1 6.3 %collective-permute-start.1 = (bf16[16,2432]{1,0:T(8,128)(2,1)S(1)}, bf16[16,2432]{1,0:T(8,128)(2,1)S(1)}, u32[]{:S(2)}, u32[]{:S(2)}) collective-permute-start(bf16[16,2432]{1,0:T(8,128)(2,1)S(1)} %shard_map.83), channel_id=1, source_target_pairs={{0,1},{1,0},{2,3},{3,2},{4,5},{5,4},{6,7},{7,6},{8,9},{9,8},{10,11... | collective-permute-start | bytes 233480 | tf_op jit(solution)/shard_map/ppermute | solution.py:17
  8.4 12.6 %copy-start.6 = (bf16[8,294,294]{2,0,1:T(8,128)(2,1)S(1)}, bf16[8,294,294]{2,0,1:T(8,128)(2,1)}, u32[]{:S(2)}) copy-start(bf16[8,294,294]{2,0,1:T(8,128)(2,1)} %param.15) | copy-start | bytes 4148932
  8.6 4.4 %collective-permute-start.2 = (bf16[16,2432]{1,0:T(8,128)(2,1)S(1)}, bf16[16,2432]{1,0:T(8,128)(2,1)S(1)}, u32[]{:S(2)}, u32[]{:S(2)}) collective-permute-start(bf16[16,2432]{1,0:T(8,128)(2,1)S(1)} %collective-permute-done), channel_id=1, source_target_pairs={{0,1},{1,0},{2,3},{3,2},{4,5},{5,4},{6,7},{7,6},{8,9},{9,8},{10,11... | collective-permute-start | bytes 233480 | tf_op jit(solution)/shard_map/ppermute | solution.py:17
  9.9 7.3 %collective-permute-start.4 = (bf16[32,2432]{1,0:T(8,128)(2,1)S(1)}, bf16[32,2432]{1,0:T(8,128)(2,1)S(1)}, u32[]{:S(2)}, u32[]{:S(2)}) collective-permute-start(bf16[32,2432]{1,0:T(8,128)(2,1)S(1)} %pad_maximum_fusion.1), channel_id=1, source_target_pairs={{4,8},{12,16},{20,24},{8,4},{16,12},{24,20},{0,28},{28,0},{5,9},{1... | collective-permute-start | bytes 466952 | tf_op jit(solution)/shard_map/ppermute | solution.py:308
  14.1 1.2 %collective-permute-start.6 = (bf16[8,294]{1,0:T(8,128)(2,1)S(1)}, bf16[8,294]{1,0:T(8,128)(2,1)S(1)}, u32[]{:S(2)}, u32[]{:S(2)}) collective-permute-start(bf16[8,294]{1,0:T(8,128)(2,1)S(1)} %shard_map.84), channel_id=1, source_target_pairs={{0,4},{4,0},{8,12},{12,8},{16,20},{20,16},{24,28},{28,24},{1,5},{5... | collective-permute-start | bytes 14120 | tf_op jit(solution)/shard_map/ppermute | solution.py:17
  14.1 9.5 %collective-permute-start.3 = (bf16[64,2432]{1,0:T(8,128)(2,1)S(1)}, bf16[64,2432]{1,0:T(8,128)(2,1)S(1)}, u32[]{:S(2)}, u32[]{:S(2)}) collective-permute-start(bf16[64,2432]{1,0:T(8,128)(2,1)S(1)} %pad_maximum_fusion.rows_ref.range_ref), channel_id=1, source_target_pairs={{0,4},{4,0},{8,12},{12,8},{16,20},{20,16},{24,28},{28,24},{1,5},{5... | collective-permute-start | bytes 933896 | tf_op jit(solution)/shard_map/ppermute | solution.py:17
  15.3 3.7 %collective-permute-start.7 = (bf16[16,294]{1,0:T(8,128)(2,1)S(1)}, bf16[16,294]{1,0:T(8,128)(2,1)S(1)}, u32[]{:S(2)}, u32[]{:S(2)}) collective-permute-start(bf16[16,294]{1,0:T(8,128)(2,1)S(1)} %pad_maximum_fusion.4), channel_id=1, source_target_pairs={{0,8},{4,12},{8,0},{12,4},{16,24},{20,28},{24,16},{28,20},{1,9},{5... | collective-permute-start | bytes 28232 | tf_op jit(solution)/shard_map/ppermute | solution.py:17
  17.2 6.4 %collective-permute-start.5 = (bf16[32,2432]{1,0:T(8,128)(2,1)S(1)}, bf16[32,2432]{1,0:T(8,128)(2,1)S(1)}, u32[]{:S(2)}, u32[]{:S(2)}) collective-permute-start(bf16[32,2432]{1,0:T(8,128)(2,1)S(1)} %collective-permute-done.4.outer_even_ref), channel_id=1, source_target_pairs={{0,1},{1,0},{2,3},{3,2},{4,5},{5,4},{6,7},{7,6},{8,9},{9,8},{10,11... | collective-permute-start | bytes 466952 | tf_op jit(solution)/shard_map/ppermute | solution.py:17
  19.0 2.2 %copy-start.5 = (bf16[16,294,294]{2,0,1:T(8,128)(2,1)S(1)}, bf16[16,294,294]{2,0,1:T(8,128)(2,1)}, u32[]{:S(2)}) copy-start(bf16[16,294,294]{2,0,1:T(8,128)(2,1)} %param.14) | copy-start | bytes 8297860
  19.0 4.6 %collective-permute-start.8 = (bf16[32,294]{1,0:T(8,128)(2,1)S(1)}, bf16[32,294]{1,0:T(8,128)(2,1)S(1)}, u32[]{:S(2)}, u32[]{:S(2)}) collective-permute-start(bf16[32,294]{1,0:T(8,128)(2,1)S(1)} %pad_maximum_fusion.3), channel_id=1, source_target_pairs={{0,16},{4,20},{8,24},{12,28},{16,0},{20,4},{24,8},{28,12},{1,17},{... | collective-permute-start | bytes 56456 | tf_op jit(solution)/shard_map/ppermute | solution.py:17
  22.1 0.7 %copy-start.1 = (s32[16,189]{1,0:T(8,128)S(1)}, s32[16,189]{1,0:T(8,128)}, u32[]{:S(2)}) copy-start(s32[16,189]{1,0:T(8,128)} %sources_ref.1) | copy-start | bytes 36292
  22.1 0.7 %copy-start.2 = (s32[16,189]{1,0:T(8,128)S(1)}, s32[16,189]{1,0:T(8,128)}, u32[]{:S(2)}) copy-start(s32[16,189]{1,0:T(8,128)} %classes_ref.1) | copy-start | bytes 36292
  22.1 0.7 %copy-start.3 = (s32[1,189]{1,0:T(1,128)S(1)}, s32[1,189]{1,0:T(1,128)}, u32[]{:S(2)}) copy-start(s32[1,189]{1,0:T(1,128)} %grand_sources_ref.1) | copy-start | bytes 2272
  22.1 0.7 %copy-start.4 = (s32[1,189]{1,0:T(1,128)S(1)}, s32[1,189]{1,0:T(1,128)}, u32[]{:S(2)}) copy-start(s32[1,189]{1,0:T(1,128)} %grand_classes_ref.1) | copy-start | bytes 2272
